TPU v7x, 512 devices: a whole 4x4x16 slice. The times are simulated.
512 devices in a mesh: dp: 64 (over x, z_lo, core), seq: 8 (over y, z_hi).
Axes of the slice: x: 4, y: 4, z: 16 (z_hi: 2, z_lo: 8; z = z_hi * 8 + z_lo), core: 2. Of those that a mesh axis runs over, the one named last changes fastest.
Arguments:
- queries: bfloat16 [65536, 6144], P(('dp', 'seq')), may hold values from -8 to 8
- latent: bfloat16 [65536, 512], P(('dp', 'seq')), may hold values from -24 to 24
- key_rope: bfloat16 [65536, 64], P(('dp', 'seq')), may hold values from -8 to 8
- up_weight: bfloat16 [512, 8192], P(None, 'seq'), may hold values from -0.25 to 0.25
- out_grad: bfloat16 [65536, 4096], P(('dp', 'seq')), may hold values from -6 to 6
Outputs:
- latent_grad: float32 [65536, 512], P(('dp', 'seq'))
- weight_grad: float32 [512, 8192], P('dp', 'seq')
All inputs are finite; a program needn't handle non-finite values.
Results may differ from a plain program's by a relative error of at most 0.0065.
Values may be sent and summed in bfloat16 or wider, within the bound.
No kernel may reach another device: no remote copies, remote signals or barrier semaphores. Data moves between devices by JAX's collectives and lax.ppermute only.
A program may use at most 64 MiB of HBM per device.

v0:
```python
import math

import jax
import jax.numpy as jnp
from jax import lax
from jax.sharding import Mesh
from jax.sharding import PartitionSpec as P

NOPE = 128
ROPE = 64
VDIM = 128
SEQ = ("seq_0", "seq_1")
DP_SEQ = ("dp", "seq_0", "seq_1")


def in_one_piece(arrays, axis, dim, along):
    widths = [a.shape[along] for a in arrays]
    both = jnp.concatenate(arrays, axis=along)
    result = lax.all_gather(both, axis, axis=dim, tiled=True)
    return tuple(jnp.split(result, [sum(widths[:k]) for k in range(1, len(widths))], axis=along))


def scatter_axes(array, axes, dim):
    if not axes:
        return array
    nearer = lax.psum_scatter(array, axes[0], scatter_dimension=dim, tiled=True)
    return scatter_axes(nearer, axes[1:], dim)


def cut_along(array, dim, length):
    before, after = (array.shape[:dim], array.shape[dim + 1 :])
    return jnp.moveaxis(array.reshape(*before, length, -1, *after), dim, 0)


def sum_at_owner(array, axis, dim):
    pieces = cut_along(array, dim, lax.axis_size(axis))
    arrived = lax.all_to_all(pieces, axis, split_axis=0, concat_axis=0, tiled=True)
    return arrived.sum(axis=0)


def per_device(queries, latent, key_rope, up_weight, out_grad):
    query_width = NOPE + ROPE
    kv_width = NOPE + VDIM
    score_scale = query_width ** (-0.5)
    latent_full, rope_full = in_one_piece((latent, key_rope), SEQ, 0, 1)
    length = latent_full.shape[0]
    local_heads = up_weight.shape[1] // kv_width
    kv_cols = jnp.dot(latent_full, up_weight, preferred_element_type=jnp.float32).astype(
        jnp.bfloat16
    )
    block_rows = math.gcd(length, 512)

    def head_block(head_index, query_all, grad_out):
        kv_all = lax.dynamic_slice_in_dim(kv_cols, head_index * kv_width, kv_width, 1)
        query_nope = query_all[:, :NOPE]
        query_rope = query_all[:, NOPE:]
        keys_nope = kv_all[:, :NOPE]
        values = kv_all[:, NOPE:]
        key_grad = jnp.zeros((length, NOPE), jnp.float32)
        value_grad = jnp.zeros((length, VDIM), jnp.float32)
        for segment in range(length // block_rows):
            row_start = segment * block_rows
            row_end = row_start + block_rows
            scores = jnp.dot(
                query_nope[row_start:row_end],
                keys_nope[:row_end].T,
                preferred_element_type=jnp.float32,
            )
            scores = scores + jnp.dot(
                query_rope[row_start:row_end],
                rope_full[:row_end].T,
                preferred_element_type=jnp.float32,
            )
            scores = scores * score_scale
            query_pos = row_start + lax.broadcasted_iota(jnp.int32, (block_rows, row_end), 0)
            key_pos = lax.broadcasted_iota(jnp.int32, (block_rows, row_end), 1)
            scores = jnp.where(key_pos <= query_pos, scores, jnp.float32(-1e30))
            row_max = jnp.max(scores, axis=1, keepdims=True)
            expo = jnp.exp(scores - row_max)
            attend = expo / jnp.sum(expo, axis=1, keepdims=True)
            attend_rounded = attend.astype(jnp.bfloat16)
            grad_rows = grad_out[row_start:row_end]
            value_grad = value_grad.at[:row_end].add(
                jnp.dot(attend_rounded.T, grad_rows, preferred_element_type=jnp.float32)
            )
            prob_grad = jnp.dot(grad_rows, values[:row_end].T, preferred_element_type=jnp.float32)
            row_dot = jnp.sum(attend * prob_grad, axis=1, keepdims=True)
            score_grad = (attend * (prob_grad - row_dot) * score_scale).astype(jnp.bfloat16)
            key_grad = key_grad.at[:row_end].add(
                jnp.dot(
                    score_grad.T, query_nope[row_start:row_end], preferred_element_type=jnp.float32
                )
            )
        return jnp.concatenate([key_grad, value_grad], axis=1).astype(jnp.bfloat16)

    start_cols = jnp.zeros((length, local_heads * kv_width), jnp.bfloat16)
    query_heads, grad_heads = (
        lax.all_to_all(queries, SEQ, split_axis=1, concat_axis=0, tiled=True),
        lax.all_to_all(out_grad, SEQ, split_axis=1, concat_axis=0, tiled=True),
    )

    def one_head(head_index, grad_cols):
        query_all = lax.dynamic_slice_in_dim(query_heads, head_index * query_width, query_width, 1)
        grad_out = lax.dynamic_slice_in_dim(grad_heads, head_index * VDIM, VDIM, 1)
        joined = head_block(head_index, query_all, grad_out)
        return lax.dynamic_update_slice_in_dim(grad_cols, joined, head_index * kv_width, 1)

    grad_cols = lax.fori_loop(0, local_heads, one_head, start_cols)
    latent_part = jnp.dot(grad_cols, up_weight.T, preferred_element_type=jnp.float32)
    latent_grad = scatter_axes(latent_part, SEQ, 0)
    replicas = lax.axis_size("dp")
    weight_full = jnp.dot(latent_full.T, grad_cols, preferred_element_type=jnp.float32)
    summed = sum_at_owner(weight_full, "dp", 0)
    return (latent_grad, summed / replicas)


def solution(mesh):
    torus = Mesh(mesh.devices.reshape(mesh.shape["dp"], 4, 2), ("dp", "seq_0", "seq_1"))
    in_specs = (P(DP_SEQ, None), P(DP_SEQ, None), P(DP_SEQ, None), P(None, SEQ), P(DP_SEQ, None))
    out_specs = (P(DP_SEQ, None), P("dp", SEQ))
    return jax.shard_map(
        per_device, mesh=torus, in_specs=in_specs, out_specs=out_specs, check_vma=False
    )
```

profile of v0, /device:TPU:1, one launch (start us, length us, event | category | flops | bytes accessed | tf_op | source)
XLA Modules:
  0.0 438.4 jit_solution(139880134441688414)
XLA Ops:
  7.2 2.5 copy.15
  9.6 18.3 %all-to-all-start.1 = ((bf16[128,8,512]{2,0,1:T(8,128)(2,1)}), bf16[128,8,512]{2,0,1:T(8,128)(2,1)}, u32[]{:S(2)}, u32[]{:S(2)}) async-start(bf16[128,8,512]{2,0,1:T(8,128)(2,1)} %bitcast.20), calls=%async_computation.1 | async-start | bytes 2097152 | tf_op jit(solution)/shard_map/all_to_all | solution.py:99
  27.9 1.3 copy.14
  29.2 27.5 %all-to-all-done.1 = bf16[128,8,512]{2,0,1:T(8,128)(2,1)} async-done(((bf16[128,8,512]{2,0,1:T(8,128)(2,1)}), bf16[128,8,512]{2,0,1:T(8,128)(2,1)}, u32[]{:S(2)}, u32[]{:S(2)}) %all-to-all-start.1) | async-done | bytes 1048608 | tf_op jit(solution)/shard_map/all_to_all | solution.py:99
  56.7 3.6 all-to-all-start
  60.5 0.7 pad_maximum_fusion
  61.2 166.4 %all-gather.2.cloned.1.call-done = bf16[1024,576]{1,0:T(8,128)(2,1)} async-done(((bf16[128,576]{1,0:T(8,128)(2,1)}), bf16[1024,576]{1,0:T(8,128)(2,1)}) %all-gather.2.cloned.1.call-update) | async-done | bytes 1179664 | tf_op jit(solution)/shard_map/all_gather | solution.py:19
  227.6 3.8 convolution_convert_fusion
  231.4 1.6 broadcast_in_dim.43
  233.3 66.3 %while.35 = (s32[]{:T(128)}, bf16[1024,1024]{0,1:T(8,128)(2,1)}, bf16[1024,768]{1,0:T(8,128)(2,1)}, bf16[1024,1024]{1,0:T(8,128)(2,1)}, bf16[1024,64]{1,0:T(8,12...) while((s32[]{:T(128)}, bf16[1024,1024]{0,1:T(8,128)(2,1)}, ...), condition=%wide.region_7.8_spmd, body=%wide.region_0.7_spmd.sunk | while | flops 923268608 | bytes 33341852 | solution.py:108
  233.3 1.5 fusion.90
  234.8 1.3 fusion.91
  236.3 1.3 fusion.93
  237.5 1.3 multiply_reduce_fusion.5
  238.8 1.4 fusion.98
  240.3 1.5 fusion.94
  241.8 1.7 fusion.95
  243.5 0.5 fusion.96
  244.0 1.5 fusion.97
  245.5 1.7 multiply_reduce_fusion.4
  247.2 1.9 fusion.99
  249.1 0.9 maximum_dynamic-update-slice_fusion.2
  250.0 1.4 fusion.90
  251.3 1.3 fusion.91
  252.8 1.3 fusion.93
  254.1 1.3 multiply_reduce_fusion.5
  255.4 1.4 fusion.98
  256.8 1.5 fusion.94
  258.4 1.7 fusion.95
  260.0 0.5 fusion.96
  260.5 1.5 fusion.97
  262.1 1.7 multiply_reduce_fusion.4
  263.8 1.9 fusion.99
  265.7 0.9 maximum_dynamic-update-slice_fusion.2
  266.5 1.4 fusion.90
  267.9 1.3 fusion.91
  269.4 1.3 fusion.93
  270.7 1.3 multiply_reduce_fusion.5
  272.0 1.4 fusion.98
  273.4 1.5 fusion.94
  274.9 1.7 fusion.95
  276.6 0.5 fusion.96
  277.1 1.5 fusion.97
  278.6 1.7 multiply_reduce_fusion.4
  280.3 1.9 fusion.99
  282.2 0.9 maximum_dynamic-update-slice_fusion.2
  283.1 1.4 fusion.90
  284.4 1.3 fusion.91
  285.9 1.3 fusion.93
  287.2 1.3 multiply_reduce_fusion.5
  288.5 1.4 fusion.98
  289.9 1.5 fusion.94
  291.5 1.7 fusion.95
  293.1 0.5 fusion.96
  293.6 1.5 fusion.97
  295.2 1.7 multiply_reduce_fusion.4
  296.9 1.9 fusion.99
  298.8 0.8 maximum_dynamic-update-slice_fusion.2
  299.6 4.2 convolution_bitcast_fusion
  303.9 8.8 %all-to-all-start.2 = ((f32[64,8,1024]{2,1,0:T(8,128)}), f32[64,8,1024]{2,1,0:T(8,128)S(1)}, u32[]{:S(2)}, u32[]{:S(2)}) async-start(f32[64,8,1024]{2,1,0:T(8,128)} %convolution_bitcast_fusion), calls=%async_computation.4 | async-start | bytes 4194304 | tf_op jit(solution)/shard_map/all_to_all | solution.py:37
  312.7 4.3 fusion.52
  317.0 35.5 %reduce-scatter.3.cloned.1.call-done = f32[256,512]{1,0:T(8,128)} async-done(((f32[1024,512]{1,0:T(8,128)}), f32[256,512]{1,0:T(8,128)}) %reduce-scatter.3.cloned.1.call-update) | async-done | bytes 524304 | tf_op jit(solution)/shard_map/reduce_scatter | solution.py:26
  352.5 78.5 %all-to-all-done.2 = f32[64,8,1024]{2,1,0:T(8,128)S(1)} async-done(((f32[64,8,1024]{2,1,0:T(8,128)}), f32[64,8,1024]{2,1,0:T(8,128)S(1)}, u32[]{:S(2)}, u32[]{:S(2)}) %all-to-all-start.2) | async-done | bytes 2097184 | tf_op jit(solution)/shard_map/all_to_all | solution.py:37
  431.2 0.6 broadcast_multiply_fusion
  (32 shorter events, 1.5 us)
Async XLA Ops:
  7.2 220.4 %copy-start = (bf16[512,1024]{1,0:T(8,128)(2,1)S(1)}, bf16[512,1024]{1,0:T(8,128)(2,1)}, u32[]{:S(2)}) copy-start(bf16[512,1024]{1,0:T(8,128)(2,1)} %param.22) | copy-start | bytes 3145732
  7.2 20.7 %copy-start.3 = (bf16[128,6144]{1,0:T(8,128)(2,1)S(1)}, bf16[128,6144]{1,0:T(8,128)(2,1)}, u32[]{:S(2)}) copy-start(bf16[128,6144]{1,0:T(8,128)(2,1)} %param.19) | copy-start | bytes 4718596
  9.6 47.1 %all-to-all-start.1 = ((bf16[128,8,512]{2,0,1:T(8,128)(2,1)}), bf16[128,8,512]{2,0,1:T(8,128)(2,1)}, u32[]{:S(2)}, u32[]{:S(2)}) async-start(bf16[128,8,512]{2,0,1:T(8,128)(2,1)} %bitcast.20), calls=%async_computation.1 | async-start | bytes 2097152 | tf_op jit(solution)/shard_map/all_to_all | solution.py:99
  29.2 31.2 %copy-start.5 = (bf16[128,64]{0,1:T(8,128)(2,1)S(1)}, bf16[128,64]{0,1:T(8,128)(2,1)}, u32[]{:S(2)}) copy-start(bf16[128,64]{0,1:T(8,128)(2,1)} %param.21) | copy-start | bytes 49156
  29.2 31.3 %copy-start.4 = (bf16[128,512]{1,0:T(8,128)(2,1)S(1)}, bf16[128,512]{1,0:T(8,128)(2,1)}, u32[]{:S(2)}) copy-start(bf16[128,512]{1,0:T(8,128)(2,1)} %param.20) | copy-start | bytes 393220
  56.7 174.7 %all-to-all-start = ((bf16[128,8,768]{2,0,1:T(8,128)(2,1)}), bf16[128,8,768]{2,0,1:T(8,128)(2,1)S(1)}, u32[]{:S(2)}, u32[]{:S(2)}) async-start(bf16[128,8,768]{2,0,1:T(8,128)(2,1)} %bitcast.24), calls=%async_computation | async-start | bytes 3145728 | tf_op jit(solution)/shard_map/all_to_all | solution.py:98
  60.3 167.3 %all-gather.2.cloned.1.call-start = ((), (), s32[]{:S(2)}) async-start(), calls=%async_computation.5 | async-start | bytes 1474560 | tf_op jit(solution)/shard_map/all_gather | solution.py:19
  231.4 1.8 slice-start
  231.4 1.8 copy-start.2
  233.3 66.3 %copy-start.1 = (bf16[1024,576]{1,0:T(8,128)(2,1)S(1)}, bf16[1024,576]{1,0:T(8,128)(2,1)}, u32[]{:S(2)}) copy-start(bf16[1024,576]{1,0:T(8,128)(2,1)} %all-gather.2.cloned.1.call-done) | copy-start | bytes 3538948
  303.9 127.2 %all-to-all-start.2 = ((f32[64,8,1024]{2,1,0:T(8,128)}), f32[64,8,1024]{2,1,0:T(8,128)S(1)}, u32[]{:S(2)}, u32[]{:S(2)}) async-start(f32[64,8,1024]{2,1,0:T(8,128)} %convolution_bitcast_fusion), calls=%async_computation.4 | async-start | bytes 4194304 | tf_op jit(solution)/shard_map/all_to_all | solution.py:37
  312.6 39.9 %reduce-scatter.3.cloned.1.call-start = ((), (), s32[]{:S(2)}) async-start(), calls=%async_computation.6 | async-start | bytes 2621440 | tf_op jit(solution)/shard_map/reduce_scatter | solution.py:26
  317.0 114.9 %reduce-scatter.5.cloned.1.call-start = ((), (), s32[]{:S(2)}) async-start(), calls=%async_computation.7 | async-start | bytes 786432 | tf_op jit(solution)/shard_map/reduce_scatter | solution.py:26
Sparse Core Ops, SparseCore 0:
  64.9 162.6 all-gather.1
  317.1 35.3 reduce-scatter.2
  356.1 39.9 reduce-scatter.4
where the time goes:
time: 440 us; the launch traced here: 438 us
  waiting for transfers between devices  308 us (70%)
  matrix products  72.2 us (16%)
  starting transfers between devices  30.7 us (7%)
  between operations  13.8 us (3%)
  other arithmetic  7.73 us (2%)
  local copies, waits for them, and re-layouts  5.69 us (1%)
    all_gather x1, waiting for transfers between devices, in_one_piece(): result = lax.all_gather(both, axis, axis=dim, tiled=True)  166 us
    all_to_all x1, waiting for transfers between devices, sum_at_owner(): lax.all_to_all(pieces, axis, split_axis=0, concat_axis=0, tiled=True)  78.5 us
    reduce_scatter x2, waiting for transfers between devices, scatter_axes(): nearer = lax.psum_scatter(array, axes[0], scatter_dimension=dim, tiled=True)  35.5 us
    all_to_all x1, waiting for transfers between devices, per_device(): lax.all_to_all(out_grad, SEQ, split_axis=1, concat_axis=0, tiled=True)  27.5 us
    all_to_all x1, starting transfers between devices, per_device(): lax.all_to_all(out_grad, SEQ, split_axis=1, concat_axis=0, tiled=True)  18.3 us
    dot_general x8, matrix products, head_block(): jnp.dot(score_grad.T, query_nope[row_start:row_end], preferred_element_ty...  13.3 us
    dot_general x8, matrix products, head_block(): jnp.dot(grad_rows, values[:row_end].T, preferred_element_type=jnp.float32)  11.9 us
    dot_general x8, matrix products, head_block(): jnp.dot(query_rope[row_start:row_end], rope_full[:row_end].T, preferred_e...  11.9 us
  transfers between devices with their start and end apart: 6, of which 4 were waited for; matrix products, arithmetic and copies ran while one was open for 2% of the time, Pallas kernels for 0%

commit v1 on v0

v1 whole, which is shorter than its diff:
```python
import functools
import math

import jax
import jax.numpy as jnp
from jax import lax
from jax.experimental import pallas as pl
from jax.experimental.pallas import tpu as pltpu
from jax.sharding import Mesh
from jax.sharding import PartitionSpec as P

NOPE = 128
ROPE = 64
VDIM = 128
QW = NOPE + ROPE
KVW = NOPE + VDIM
RANK = 512
SCALE = QW ** (-0.5)
BF16 = jnp.bfloat16
F32 = jnp.float32
NT = (((1,), (1,)), ((), ()))


def head_pair(kv, rope, q2, g2, w, bias, lat_t):
    length = kv.shape[0]
    half = length // 2
    weight_parts = []
    latent_sum = None
    for h in range(2):
        keys = kv[:, h * KVW : h * KVW + NOPE]
        values = kv[:, h * KVW + NOPE : (h + 1) * KVW]
        keys_full = jnp.concatenate([keys, rope], axis=1)
        query = q2[:, h * QW : (h + 1) * QW]
        query_nope = query[:, :NOPE]
        grad = g2[:, h * VDIM : (h + 1) * VDIM]
        key_grad = [None, None]
        value_grad = [None, None]
        rows_each = half // 2
        for part in range(2):
            rows = slice(part * rows_each, (part + 1) * rows_each)
            n_keys = half * (part + 1)
            scores = lax.dot_general(
                keys_full[:n_keys], query[rows], NT, preferred_element_type=F32
            )
            masked = scores[n_keys - half :] + bias
            scores = masked if part == 0 else jnp.concatenate([scores[:half], masked], axis=0)
            row_max = jnp.max(scores, axis=0, keepdims=True)
            expo = jnp.exp2((scores - row_max) * (SCALE * math.log2(math.e)))
            probs = expo * (1.0 / jnp.sum(expo, axis=0, keepdims=True))
            probs_rounded = probs.astype(BF16)
            prob_grad = lax.dot_general(
                values[:n_keys], grad[rows], NT, preferred_element_type=F32
            )
            row_dot = jnp.sum(probs * prob_grad, axis=0, keepdims=True)
            score_grad = (probs * (prob_grad - row_dot)).astype(BF16)
            for block in range(part + 1):
                cut = slice(block * half, (block + 1) * half)
                value_part = jnp.dot(probs_rounded[cut], grad[rows], preferred_element_type=F32)
                key_part = jnp.dot(score_grad[cut], query_nope[rows], preferred_element_type=F32)
                if value_grad[block] is None:
                    value_grad[block], key_grad[block] = value_part, key_part
                else:
                    value_grad[block] = value_grad[block] + value_part
                    key_grad[block] = key_grad[block] + key_part
        grad_cols = jnp.concatenate(
            [
                jnp.concatenate([key_grad[b] * SCALE, value_grad[b]], axis=1).astype(BF16)
                for b in range(2)
            ],
            axis=0,
        )
        weight_parts.append(jnp.dot(lat_t, grad_cols, preferred_element_type=F32).astype(BF16))
        latent_part = lax.dot_general(
            grad_cols, w[:, h * KVW : (h + 1) * KVW], NT, preferred_element_type=F32
        )
        latent_sum = latent_part if latent_sum is None else latent_sum + latent_part
    return weight_parts, latent_sum


def attention_kernel(first, last, n_core, n_x, n_zl, rows_each, *refs):
    place_ref, lat_ref, w_ref = refs[:3]
    q_refs, g_refs = refs[3:7], refs[7:11]
    refs = refs[11:]
    if not first:
        acc_ref, before, refs = refs[0], refs[1:3], refs[3:]
    grad_refs = refs[:2]
    lg_refs = refs[2:-5]
    bias, lat_t, total, queries, grads = refs[-5:]
    step = pl.program_id(0)
    zh, y, core = place_ref[0], place_ref[1], place_ref[2]

    @pl.when(step == 0)
    def _():
        key_pos = lax.broadcasted_iota(jnp.int32, bias.shape, 0)
        lane = lax.broadcasted_iota(jnp.int32, bias.shape, 1)
        block = jnp.where(lane >= 128, 2, 0) + zh
        query_pos = block * 128 + (lane & 127)
        bias[...] = jnp.where(key_pos <= query_pos, F32(0.0), F32(-1e30))
        row = lax.broadcasted_iota(jnp.int32, (RANK, RANK), 0)
        col = lax.broadcasted_iota(jnp.int32, (RANK, RANK), 1)
        inner = row % rows_each
        zl = (row // rows_each) % n_zl
        x = (row // (rows_each * n_zl)) % n_x
        away = row // (rows_each * n_zl * n_x)
        owner = core + away * (1 - 2 * core)
        source = ((x * n_zl + zl) * n_core + owner) * rows_each + inner
        pick = jnp.where(source == col, F32(1.0), F32(0.0)).astype(BF16)
        lat_t[...] = lax.dot_general(
            pick, lat_ref[:, :RANK], NT, preferred_element_type=F32
        ).astype(BF16)
        total[...] = jnp.zeros_like(total) if first else acc_ref[...]

    n_y = len(q_refs)
    tokens = q_refs[0].shape[0]
    for k in range(n_y):
        start = pl.multiple_of(((y + n_y - k) % n_y) * tokens, tokens)
        queries[pl.ds(start, tokens), :] = q_refs[k][...]
        grads[pl.ds(start, tokens), :] = g_refs[k][...]
    w = w_ref[...]
    kv = jnp.dot(lat_ref[:, :RANK], w, preferred_element_type=F32).astype(BF16)
    weight_parts, latent_sum = head_pair(
        kv, lat_ref[:, RANK : RANK + ROPE], queries[...], grads[...], w, bias[...], lat_t[...]
    )
    half = RANK // n_core
    for away, ref in enumerate(grad_refs):
        if not first:
            ref[:, pl.ds(zh, 1)] = before[away][...][:, None]
        for h in range(2):
            part = weight_parts[h][away * half : (away + 1) * half].reshape(n_x, -1, KVW)
            if first:
                ref[:, :, h * KVW : (h + 1) * KVW] = part
            else:
                ref[:, pl.ds(1 - zh, 1), :, h * KVW : (h + 1) * KVW] = part[:, None]
    total[...] += latent_sum

    @pl.when(step == pl.num_programs(0) - 1)
    def _():
        if not last:
            lg_refs[0][...] = total[...]
            return
        rows = total.shape[0] // n_y
        for k in range(n_y):
            start = pl.multiple_of(((y + k) % n_y) * rows, rows)
            lg_refs[k][...] = total[pl.ds(start, rows), :].astype(BF16)


def attention(place, lat, weight, queries, out_grad, arrived, before, sizes):
    length = lat.shape[0]
    heads = weight.shape[1] // KVW
    first = own = before is None
    last = not first
    n_core, n_x, n_zl = sizes
    n_y = len(arrived) + 1
    steps = heads // 2
    rows_each = RANK // (n_core * n_x * n_zl)
    tokens = queries.shape[0]
    q_blocks = heads * QW // (2 * VDIM)

    def column(i, place_ref):
        which = place_ref[0] if own else 1 - place_ref[0]
        return (place_ref[1] * 2 + which) * steps + i

    specs = [
        pl.BlockSpec((length, lat.shape[1]), lambda i, p: (0, 0)),
        pl.BlockSpec((RANK, 2 * KVW), lambda i, p: (0, i)),
        pl.BlockSpec((tokens, 2 * QW), lambda i, p: (0, column(i, p))),
        *[pl.BlockSpec((tokens, 2 * QW), lambda i, p: (0, i)) for _ in arrived],
        pl.BlockSpec((tokens, 2 * VDIM), lambda i, p: (0, column(i, p))),
        *[pl.BlockSpec((tokens, 2 * VDIM), lambda i, p: (0, q_blocks + i)) for _ in arrived],
    ]
    args = [lat, weight, queries, *arrived, out_grad, *arrived]
    rows = RANK // (n_core * n_x)
    grad_spec = pl.BlockSpec((n_x, rows, 2 * KVW), lambda i, p: (0, 0, i))
    grad_shape = jax.ShapeDtypeStruct((n_x, rows, heads * KVW), BF16)
    if not first:
        specs.append(pl.BlockSpec((length, RANK), lambda i, p: (0, 0)))
        specs.extend([grad_spec] * 2)
        args.extend(before)
        grad_spec = pl.BlockSpec((n_x, 2, rows, 2 * KVW), lambda i, p: (0, 0, 0, i))
        grad_shape = jax.ShapeDtypeStruct((n_x, 2, rows, heads * KVW), BF16)
    flops = heads * (3 * 2 * length * RANK * KVW + 4 * 2 * length * tokens * n_y * 192)
    if last:
        rows = length // n_y
        latent_specs = [pl.BlockSpec((rows, RANK), lambda i, p: (0, 0))] * n_y
        latent_shapes = [jax.ShapeDtypeStruct((rows, RANK), BF16)] * n_y
    else:
        latent_specs = [pl.BlockSpec((length, RANK), lambda i, p: (0, 0))]
        latent_shapes = [jax.ShapeDtypeStruct((length, RANK), F32)]
    keep, send, *latent_parts = pl.pallas_call(
        functools.partial(attention_kernel, first, last, n_core, n_x, n_zl, rows_each),
        grid_spec=pltpu.PrefetchScalarGridSpec(
            num_scalar_prefetch=1,
            grid=(steps,),
            in_specs=specs,
            out_specs=[grad_spec, grad_spec, *latent_specs],
            scratch_shapes=[
                pltpu.VMEM((length // 2, length // 4), F32),
                pltpu.VMEM((RANK, length), BF16),
                pltpu.VMEM((length, RANK), F32),
                pltpu.VMEM((tokens * n_y, 2 * QW), BF16),
                pltpu.VMEM((tokens * n_y, 2 * VDIM), BF16),
            ],
        ),
        out_shape=[grad_shape, grad_shape, *latent_shapes],
        compiler_params=pltpu.CompilerParams(
            dimension_semantics=("arbitrary",), vmem_limit_bytes=56 * 2**20
        ),
        cost_estimate=pl.CostEstimate(
            flops=flops, bytes_accessed=12 * 2**20, transcendentals=heads * length * tokens * n_y
        ),
    )(place, *args)
    return keep, send, latent_parts


def split_kernel(count, place_ref, *refs):
    outs = refs[2 * count :]
    for k in range(count):
        width = refs[k].shape[1]
        outs[k][:, :width] = refs[k][...]
        outs[k][:, width:] = refs[count + k][...]


def split_heads(place, queries, out_grad, own, n_y, n_zh):
    tokens = queries.shape[0]
    parts = n_y * n_zh
    count = n_y - 1
    widths = (queries.shape[1] // parts, out_grad.shape[1] // parts)

    def block(width, k):
        def index(i, place_ref):
            which = place_ref[0] if own else 1 - place_ref[0]
            return (0, ((place_ref[1] + k + 1) % n_y) * n_zh + which)

        return pl.BlockSpec((tokens, width), index)

    return pl.pallas_call(
        functools.partial(split_kernel, count),
        grid_spec=pltpu.PrefetchScalarGridSpec(
            num_scalar_prefetch=1,
            grid=(1,),
            in_specs=[block(width, k) for width in widths for k in range(count)],
            out_specs=[pl.BlockSpec((tokens, sum(widths)), lambda i, p: (0, 0))] * count,
        ),
        out_shape=[jax.ShapeDtypeStruct((tokens, sum(widths)), BF16)] * count,
        cost_estimate=pl.CostEstimate(
            flops=0, bytes_accessed=4 * count * tokens * sum(widths), transcendentals=0
        ),
    )(place, *[queries] * count, *[out_grad] * count)


def latent_kernel(latent_ref, rope_ref, out_ref):
    rope = rope_ref[...].astype(F32).T.astype(BF16)
    rest = out_ref.shape[2] - RANK - ROPE
    joined = jnp.concatenate([rope, jnp.zeros((rope.shape[0], rest), BF16)], axis=1)
    for k in range(out_ref.shape[0]):
        out_ref[k, :, :RANK] = latent_ref[...]
        out_ref[k, :, RANK:] = joined


def latent_copies(latent, rope, count):
    shape = (count, latent.shape[0], RANK + 2 * ROPE)
    return pl.pallas_call(
        latent_kernel,
        out_shape=jax.ShapeDtypeStruct(shape, BF16),
        cost_estimate=pl.CostEstimate(
            flops=0, bytes_accessed=2 * math.prod(shape), transcendentals=0
        ),
    )(latent, rope.T)


def rotate(array, axis, shift):
    n = lax.axis_size(axis)
    return lax.ppermute(array, axis, [(i, (i + shift) % n) for i in range(n)])


def exchange(pieces, axes):
    return lax.all_to_all(pieces, axes, split_axis=0, concat_axis=0, tiled=True)


def add_up(pieces, dtype=BF16):
    return jnp.sum(pieces.astype(F32), axis=0).astype(dtype)


def to_all(array, axes, count):
    return exchange(jnp.broadcast_to(array[None], (count,) + array.shape), axes)


def per_device(queries, latent, key_rope, up_weight, out_grad):
    n_x, n_zl, n_core = lax.axis_size("x"), lax.axis_size("zl"), lax.axis_size("core")
    n_y, n_zh = lax.axis_size("y"), lax.axis_size("zh")
    zh, y, core = lax.axis_index("zh"), lax.axis_index("y"), lax.axis_index("core")
    place = jnp.stack([zh, y, core]).astype(jnp.int32)
    tokens = latent.shape[0]

    copies = latent_copies(latent, key_rope, n_y * n_zh)
    lat = exchange(copies, ("y", "zh")).reshape(n_y * n_zh * tokens, copies.shape[2])

    piece_rows = RANK // (n_x * n_core)
    mine = lax.axis_index("x") * n_core + core
    piece = lax.dynamic_slice_in_dim(up_weight, mine * piece_rows, piece_rows, 0)
    other_weight = to_all(rotate(piece, "zh", 1), ("x", "core"), n_x * n_core)
    other_weight = other_weight.reshape(up_weight.shape)

    own = split_heads(place, queries, out_grad, True, n_y, n_zh)
    other = split_heads(place, queries, out_grad, False, n_y, n_zh)
    own = [rotate(a, "y", k + 1) for k, a in enumerate(own)]
    other = [rotate(a, "y", k + 1) for k, a in enumerate(other)]
    sizes = (n_core, n_x, n_zl)
    keep, send, parts = attention(place, lat, up_weight, queries, out_grad, own, None, sizes)
    keep, send, parts = attention(
        place, lat, other_weight, queries, out_grad, other, [parts[0], keep, send], sizes
    )
    on_chip = (keep.astype(F32) + rotate(send, "core", 1).astype(F32)).astype(BF16)
    arrived = [parts[0]] + [rotate(a, "y", k + 1) for k, a in enumerate(parts[1:])]

    latent_sum = sum(a.astype(F32) for a in arrived).reshape(n_zh, tokens, RANK)
    sent = lax.dynamic_index_in_dim(latent_sum, 1 - zh, 0, keepdims=False).astype(BF16)
    kept = lax.dynamic_index_in_dim(latent_sum, zh, 0, keepdims=False)
    latent_grad = kept + rotate(sent, "zh", 1).astype(F32)

    over_x, _ = lax.optimization_barrier((add_up(exchange(on_chip, "x")), sent))
    pieces = over_x.reshape(n_zh * n_zl, -1, over_x.shape[2])
    weight_grad = add_up(exchange(pieces, ("zh", "zl")), F32)
    return latent_grad, weight_grad * (1.0 / (n_x * n_zl * n_core))


def solution(mesh):
    replicas, parts = mesh.shape["dp"], mesh.shape["seq"]
    shape = (replicas // 16, 8, 2, parts // 2, 2)
    names = ("x", "zl", "core", "y", "zh")
    torus = Mesh(mesh.devices.reshape(shape), names)
    rows = P(names, None)
    in_specs = (rows, rows, rows, P(None, ("y", "zh")), rows)
    out_specs = (rows, P(("x", "zl", "core"), ("y", "zh")))
    return jax.shard_map(
        per_device, mesh=torus, in_specs=in_specs, out_specs=out_specs, check_vma=False
    )
```

time: 440 us -> 227 us (0.52)
  the two profiles are of different devices: /device:TPU:1 before, /device:TPU:26 now
where the time goes in v1:
time: 227 us; the launch traced here: 226 us
  starting transfers between devices  127 us (56%)
  waiting for transfers between devices  47.4 us (21%)
  Pallas kernels  39.9 us (18%)
  other arithmetic  5.76 us (3%)
  local copies, waits for them, and re-layouts  4.35 us (2%)
    all_to_all x4, starting transfers between devices, exchange(): return lax.all_to_all(pieces, axes, split_axis=0, concat_axis=0, tiled=True)  73.2 us
    ppermute x12, starting transfers between devices, rotate(): return lax.ppermute(array, axis, [(i, (i + shift) % n) for i in range(n)])  54.2 us
    ppermute x12, waiting for transfers between devices, rotate(): return lax.ppermute(array, axis, [(i, (i + shift) % n) for i in range(n)])  47.4 us
    pallas_call x2, Pallas kernels, attention(): pl.pallas_call(functools.partial(attention_kernel, first, last, n_core, n...  31.9 us
    pallas_call x2, Pallas kernels, split_heads(): pl.pallas_call(functools.partial(split_kernel, count), grid_spec=pltpu.Pr...  5.87 us
  transfers between devices with their start and end apart: 16, of which 6 were waited for; matrix products, arithmetic and copies ran while one was open for 2% of the time, Pallas kernels for 10%

profile of v1, /device:TPU:26, one launch (start us, length us, event | category | flops | bytes accessed | tf_op | source)
XLA Modules:
  0.0 225.7 jit_solution(17552757630946083680)
XLA Ops:
  0.6 2.1 shard_map.68
  2.7 17.9 %all-to-all-start = ((bf16[8,128,640]{2,1,0:T(8,128)(2,1)}), bf16[8,128,640]{2,1,0:T(8,128)(2,1)S(1)}, u32[]{:S(2)}, u32[]{:S(2)}) async-start(bf16[8,128,640]{2,1,0:T(8,128)(2,1)} %shard_map.68), calls=%async_computation | async-start | bytes 2621440 | tf_op jit(solution)/shard_map/all_to_all | solution.py:277
  20.7 0.9 constant_dynamic-slice_fusion
  21.6 12.1 %collective-permute-start = (bf16[64,1024]{1,0:T(8,128)(2,1)S(1)}, bf16[64,1024]{1,0:T(8,128)(2,1)S(1)}, u32[]{:S(2)}, u32[]{:S(2)}) collective-permute-start(bf16[64,1024]{1,0:T(8,128)(2,1)S(1)} %constant_dynamic-slice_fusion), channel_id=1, source_target_pairs={{0,1},{1,0},{2,3},{3,2},{4,5},{5,4},{6,7},{7,6},{8,9},{9,8},{10,11... | collective-permute-start | bytes 393224 | tf_op jit(solution)/shard_map/ppermute | solution.py:273
  33.7 0.6 pad_add_fusion.place_ref.refs_0_
  34.3 2.9 %shard_map.70 = (bf16[128,1280]{1,0:T(8,128)(2,1)}, bf16[128,1280]{1,0:T(8,128)(2,1)}, bf16[128,1280]{1,0:T(8,128)(2,1)}) custom-call(s32[3]{0:T(128)} %pad_add_fusion.place_ref.refs_0_, bf16[128,6144]{1,0:T(8,128)(2,1)} %refs_3_.7, bf16[128,6144]{1,0:T(8,128)(2,1)} %refs_3_.7, bf16[128,6144]{1,0:T(8,128)(2,1)} %refs_3_.7, bf16[128,4096]{1,0:T(8,128)(2,1)} %refs_7_.3, ...), custom_call_target="tpu_custom_call" | custom-call | bytes 1966080 | tf_op jit(solution)/shard_map/pallas_call | solution.py:236
  37.2 2.5 %collective-permute-start.4 = (bf16[128,1280]{1,0:T(8,128)(2,1)}, bf16[128,1280]{1,0:T(8,128)(2,1)S(1)}, u32[]{:S(2)}, u32[]{:S(2)}) collective-permute-start(bf16[128,1280]{1,0:T(8,128)(2,1)} %get-tuple-element.21), channel_id=1, source_target_pairs={{0,2},{2,4},{4,6},{6,0},{1,3},{3,5},{5,7},{7,1},{8,10},{10,12},{12... | collective-permute-start | bytes 983048 | tf_op jit(solution)/shard_map/ppermute | solution.py:273
  39.7 4.3 %collective-permute-start.5 = (bf16[128,1280]{1,0:T(8,128)(2,1)}, bf16[128,1280]{1,0:T(8,128)(2,1)S(1)}, u32[]{:S(2)}, u32[]{:S(2)}) collective-permute-start(bf16[128,1280]{1,0:T(8,128)(2,1)} %get-tuple-element.22), channel_id=1, source_target_pairs={{0,4},{2,6},{4,0},{6,2},{1,5},{3,7},{5,1},{7,3},{8,12},{10,14},{12... | collective-permute-start | bytes 983048 | tf_op jit(solution)/shard_map/ppermute | solution.py:273
  43.9 1.9 collective-permute-start.6
  45.9 12.2 %collective-permute-done = bf16[64,1024]{1,0:T(8,128)(2,1)S(1)} collective-permute-done((bf16[64,1024]{1,0:T(8,128)(2,1)S(1)}, bf16[64,1024]{1,0:T(8,128)(2,1)S(1)}, u32[]{:S(2)}, u32[]{:S(2)}) %collective-permute-start) | collective-permute-done | bytes 131104 | tf_op jit(solution)/shard_map/ppermute | solution.py:273
  58.1 0.0 all-to-all-done
  58.1 1.2 broadcast_in_dim.2
  59.3 4.8 %all-to-all-start.1 = ((bf16[8,64,1024]{2,1,0:T(8,128)(2,1)}), bf16[8,64,1024]{2,1,0:T(8,128)(2,1)S(1)}, u32[]{:S(2)}, u32[]{:S(2)}) async-start(bf16[8,64,1024]{2,1,0:T(8,128)(2,1)} %broadcast_in_dim.2), calls=%async_computation.1 | async-start | bytes 2097152 | tf_op jit(solution)/shard_map/all_to_all | solution.py:277
  64.1 3.0 %shard_map.69 = (bf16[128,1280]{1,0:T(8,128)(2,1)}, bf16[128,1280]{1,0:T(8,128)(2,1)}, bf16[128,1280]{1,0:T(8,128)(2,1)}) custom-call(s32[3]{0:T(128)} %pad_add_fusion.place_ref.refs_0_, bf16[128,6144]{1,0:T(8,128)(2,1)} %refs_3_.7, bf16[128,6144]{1,0:T(8,128)(2,1)} %refs_3_.7, bf16[128,6144]{1,0:T(8,128)(2,1)} %refs_3_.7, bf16[128,4096]{1,0:T(8,128)(2,1)} %refs_7_.3, ...), custom_call_target="tpu_custom_call" | custom-call | bytes 1966080 | tf_op jit(solution)/shard_map/pallas_call | solution.py:236
  67.1 0.0 copy-done
  67.1 2.8 %collective-permute-start.1 = (bf16[128,1280]{1,0:T(8,128)(2,1)}, bf16[128,1280]{1,0:T(8,128)(2,1)S(1)}, u32[]{:S(2)}, u32[]{:S(2)}) collective-permute-start(bf16[128,1280]{1,0:T(8,128)(2,1)} %get-tuple-element.18), channel_id=1, source_target_pairs={{0,2},{2,4},{4,6},{6,0},{1,3},{3,5},{5,7},{7,1},{8,10},{10,12},{12... | collective-permute-start | bytes 983048 | tf_op jit(solution)/shard_map/ppermute | solution.py:273
  70.0 3.9 %collective-permute-start.2 = (bf16[128,1280]{1,0:T(8,128)(2,1)}, bf16[128,1280]{1,0:T(8,128)(2,1)S(1)}, u32[]{:S(2)}, u32[]{:S(2)}) collective-permute-start(bf16[128,1280]{1,0:T(8,128)(2,1)} %get-tuple-element.19), channel_id=1, source_target_pairs={{0,4},{2,6},{4,0},{6,2},{1,5},{3,7},{5,1},{7,3},{8,12},{10,14},{12... | collective-permute-start | bytes 983048 | tf_op jit(solution)/shard_map/ppermute | solution.py:273
  73.9 0.0 collective-permute-done.4.refs_4_.refs_8_
  73.9 0.0 copy-start.3
  73.9 1.9 collective-permute-start.3
  75.8 0.0 collective-permute-done.5.refs_5_.refs_9_
  75.8 0.0 copy-start.5
  75.8 0.0 collective-permute-done.6.refs_6_.refs_10_
  75.8 0.0 copy-start.7
  75.9 0.0 copy-done.3
  75.9 0.7 copy-done.5
  76.6 0.1 copy-done.7
  76.7 15.6 %shard_map.71 = (bf16[4,64,1024]{2,1,0:T(8,128)(2,1)}, bf16[4,64,1024]{2,1,0:T(8,128)(2,1)}, f32[1024,512]{1,0:T(8,128)}) custom-call(s32[3]{0:T(128)} %pad_add_fusion.place_ref.refs_0_, bf16[1024,640]{1,0:T(8,128)(2,1)} %bitcast.14, bf16[512,1024]{1,0:T(8,128)(2,1)} %refs_2_.5, bf16[128,6144]{1,0:T(8,128)(2,1)} %refs_3_.7, bf16[128,1280]{1,0:T(8,128)(2,1)} %copy-done.3, ...), custom_call_target="tpu_custom_call" | custom-call | flops 6442450944 | bytes 12582912 | tf_op jit(solution)/shard_map/pallas_call | solution.py:189
  92.3 0.0 collective-permute-done.1.refs_4_.refs_8_
  92.3 0.0 copy-start.4
  92.3 0.0 collective-permute-done.2.refs_5_.refs_9_
  92.3 0.0 copy-start.6
  92.3 0.0 collective-permute-done.3.refs_6_.refs_10_
  92.3 0.0 copy-start.8
  92.3 0.0 all-to-all-done.1
  92.4 0.0 copy-start.1
  92.4 0.7 copy-done.4
  93.0 0.1 copy-done.6
  93.2 0.1 copy-done.8
  93.3 0.4 copy-done.1
  93.7 16.3 %shard_map.72 = (bf16[4,2,64,1024]{3,2,1,0:T(8,128)(2,1)}, bf16[4,2,64,1024]{3,2,1,0:T(8,128)(2,1)}, bf16[256,512]{1,0:T(8,128)(2,1)}, bf16[256,512]{1,0:T(8,128...) custom-call(s32[3]{0:T(128)} %pad_add_fusion.place_ref.refs_0_, bf16[1024,640]{1,0:T(8,128)(2,1)} %bitcast.15, ...), custom_call_target="tpu_custom_call" | custom-call | flops 6442450944 | bytes 12582912 | tf_op jit(solution)/shard_map/pallas_call | solution.py:189
  110.0 1.9 collective-permute-start.11
  112.0 2.8 %collective-permute-done.11 = bf16[4,2,64,1024]{3,2,1,0:T(8,128)(2,1)S(1)} collective-permute-done((bf16[4,2,64,1024]{3,2,1,0:T(8,128)(2,1)}, bf16[4,2,64,1024]{3,2,1,0:T(8,128)(2,1)S(1)}, u32[]{:S(2)}, u32[]{:S(2)}) %collective-permute-start.11) | collective-permute-done | bytes 1048608 | tf_op jit(solution)/shard_map/ppermute | solution.py:273
  114.8 2.7 %add_convert_fusion = bf16[4,2,64,1024]{3,2,1,0:T(8,128)(2,1)} fusion(bf16[4,2,64,1024]{3,2,1,0:T(8,128)(2,1)S(1)} %collective-permute-done.11, bf16[4,2,64,1024]{3,2,1,0:T(8,128)(2,1)} %get-tuple-element.31), kind=kLoop, calls=%fused_computation | loop fusion | flops 2097152 | bytes 3145728 | tf_op jit(solution)/shard_map/convert_element_type | solution.py:313
  117.5 4.8 %all-to-all-start.2 = ((bf16[4,2,64,1024]{3,2,1,0:T(8,128)(2,1)}), bf16[4,2,64,1024]{3,2,1,0:T(8,128)(2,1)S(1)}, u32[]{:S(2)}, u32[]{:S(2)}) async-start(bf16[4,2,64,1024]{3,2,1,0:T(8,128)(2,1)} %add_convert_fusion), calls=%async_computation.2 | async-start | bytes 2097152 | tf_op jit(solution)/shard_map/all_to_all | solution.py:277
  122.3 0.0 copy-done.11
  122.3 5.1 %collective-permute-start.7 = (bf16[256,512]{1,0:T(8,128)(2,1)S(1)}, bf16[256,512]{1,0:T(8,128)(2,1)S(1)}, u32[]{:S(2)}, u32[]{:S(2)}) collective-permute-start(bf16[256,512]{1,0:T(8,128)(2,1)S(1)} %copy-done.11), channel_id=1, source_target_pairs={{0,2},{2,4},{4,6},{6,0},{1,3},{3,5},{5,7},{7,1},{8,10},{10,12},{12... | collective-permute-start | bytes 786440 | tf_op jit(solution)/shard_map/ppermute | solution.py:273
  127.4 0.0 copy-done.10
  127.4 2.3 %collective-permute-start.8 = (bf16[256,512]{1,0:T(8,128)(2,1)S(1)}, bf16[256,512]{1,0:T(8,128)(2,1)S(1)}, u32[]{:S(2)}, u32[]{:S(2)}) collective-permute-start(bf16[256,512]{1,0:T(8,128)(2,1)S(1)} %copy-done.10), channel_id=1, source_target_pairs={{0,4},{2,6},{4,0},{6,2},{1,5},{3,7},{5,1},{7,3},{8,12},{10,14},{12... | collective-permute-start | bytes 786440 | tf_op jit(solution)/shard_map/ppermute | solution.py:273
  129.7 0.0 copy-done.9
  129.7 3.0 %collective-permute-start.9 = (bf16[256,512]{1,0:T(8,128)(2,1)S(1)}, bf16[256,512]{1,0:T(8,128)(2,1)S(1)}, u32[]{:S(2)}, u32[]{:S(2)}) collective-permute-start(bf16[256,512]{1,0:T(8,128)(2,1)S(1)} %copy-done.9), channel_id=1, source_target_pairs={{0,6},{2,0},{4,2},{6,4},{1,7},{3,1},{5,3},{7,5},{8,14},{10,8},{12,... | collective-permute-start | bytes 786440 | tf_op jit(solution)/shard_map/ppermute | solution.py:273
  132.7 5.6 %collective-permute-done.7 = bf16[256,512]{1,0:T(8,128)(2,1)S(1)} collective-permute-done((bf16[256,512]{1,0:T(8,128)(2,1)S(1)}, bf16[256,512]{1,0:T(8,128)(2,1)S(1)}, u32[]{:S(2)}, u32[]{:S(2)}) %collective-permute-start.7) | collective-permute-done | bytes 262176 | tf_op jit(solution)/shard_map/ppermute | solution.py:273
  138.3 1.8 collective-permute-done.8
  140.1 3.8 %collective-permute-done.9 = bf16[256,512]{1,0:T(8,128)(2,1)S(1)} collective-permute-done((bf16[256,512]{1,0:T(8,128)(2,1)S(1)}, bf16[256,512]{1,0:T(8,128)(2,1)S(1)}, u32[]{:S(2)}, u32[]{:S(2)}) %collective-permute-start.9) | collective-permute-done | bytes 262176 | tf_op jit(solution)/shard_map/ppermute | solution.py:273
  144.0 0.0 copy-done.2
  144.0 0.1 convert_add_fusion
  144.1 0.0 all-to-all-done.2
  144.1 0.9 reduce_sum.21
  145.1 45.6 %all-to-all-start.3 = ((bf16[16,8,1024]{2,1,0:T(8,128)(2,1)}), bf16[16,8,1024]{2,1,0:T(8,128)(2,1)S(1)}, u32[]{:S(2)}, u32[]{:S(2)}) async-start(bf16[16,8,1024]{2,1,0:T(8,128)(2,1)} %bitcast.9), calls=%async_computation.3 | async-start | bytes 524288 | tf_op jit(solution)/shard_map/all_to_all | solution.py:277
  190.7 12.5 %collective-permute-start.10 = (bf16[128,512]{1,0:T(8,128)(2,1)S(1)}, bf16[128,512]{1,0:T(8,128)(2,1)S(1)}, u32[]{:S(2)}, u32[]{:S(2)}) collective-permute-start(bf16[128,512]{1,0:T(8,128)(2,1)S(1)} %fusion), channel_id=1, source_target_pairs={{0,1},{1,0},{2,3},{3,2},{4,5},{5,4},{6,7},{7,6},{8,9},{9,8},{10,11... | collective-permute-start | bytes 393224 | tf_op jit(solution)/shard_map/ppermute | solution.py:273
  203.3 21.1 %collective-permute-done.10 = bf16[128,512]{1,0:T(8,128)(2,1)S(1)} collective-permute-done((bf16[128,512]{1,0:T(8,128)(2,1)S(1)}, bf16[128,512]{1,0:T(8,128)(2,1)S(1)}, u32[]{:S(2)}, u32[]{:S(2)}) %collective-permute-start.10) | collective-permute-done | bytes 131104 | tf_op jit(solution)/shard_map/ppermute | solution.py:273
  224.3 0.7 bitcast_add_fusion
  225.1 0.0 all-to-all-done.3
  225.1 0.6 broadcast_multiply_fusion
  (7 shorter events, 0.1 us)
Async XLA Ops:
  2.7 55.4 %all-to-all-start = ((bf16[8,128,640]{2,1,0:T(8,128)(2,1)}), bf16[8,128,640]{2,1,0:T(8,128)(2,1)S(1)}, u32[]{:S(2)}, u32[]{:S(2)}) async-start(bf16[8,128,640]{2,1,0:T(8,128)(2,1)} %shard_map.68), calls=%async_computation | async-start | bytes 2621440 | tf_op jit(solution)/shard_map/all_to_all | solution.py:277
  21.6 36.5 %collective-permute-start = (bf16[64,1024]{1,0:T(8,128)(2,1)S(1)}, bf16[64,1024]{1,0:T(8,128)(2,1)S(1)}, u32[]{:S(2)}, u32[]{:S(2)}) collective-permute-start(bf16[64,1024]{1,0:T(8,128)(2,1)S(1)} %constant_dynamic-slice_fusion), channel_id=1, source_target_pairs={{0,1},{1,0},{2,3},{3,2},{4,5},{5,4},{6,7},{7,6},{8,9},{9,8},{10,11... | collective-permute-start | bytes 393224 | tf_op jit(solution)/shard_map/ppermute | solution.py:273
  37.2 36.7 %collective-permute-start.4 = (bf16[128,1280]{1,0:T(8,128)(2,1)}, bf16[128,1280]{1,0:T(8,128)(2,1)S(1)}, u32[]{:S(2)}, u32[]{:S(2)}) collective-permute-start(bf16[128,1280]{1,0:T(8,128)(2,1)} %get-tuple-element.21), channel_id=1, source_target_pairs={{0,2},{2,4},{4,6},{6,0},{1,3},{3,5},{5,7},{7,1},{8,10},{10,12},{12... | collective-permute-start | bytes 983048 | tf_op jit(solution)/shard_map/ppermute | solution.py:273
  39.7 36.2 %collective-permute-start.5 = (bf16[128,1280]{1,0:T(8,128)(2,1)}, bf16[128,1280]{1,0:T(8,128)(2,1)S(1)}, u32[]{:S(2)}, u32[]{:S(2)}) collective-permute-start(bf16[128,1280]{1,0:T(8,128)(2,1)} %get-tuple-element.22), channel_id=1, source_target_pairs={{0,4},{2,6},{4,0},{6,2},{1,5},{3,7},{5,1},{7,3},{8,12},{10,14},{12... | collective-permute-start | bytes 983048 | tf_op jit(solution)/shard_map/ppermute | solution.py:273
  43.9 31.9 %collective-permute-start.6 = (bf16[128,1280]{1,0:T(8,128)(2,1)}, bf16[128,1280]{1,0:T(8,128)(2,1)S(1)}, u32[]{:S(2)}, u32[]{:S(2)}) collective-permute-start(bf16[128,1280]{1,0:T(8,128)(2,1)} %get-tuple-element.23), channel_id=1, source_target_pairs={{0,6},{2,0},{4,2},{6,4},{1,7},{3,1},{5,3},{7,5},{8,14},{10,8},{12,... | collective-permute-start | bytes 983048 | tf_op jit(solution)/shard_map/ppermute | solution.py:273
  58.1 9.0 %copy-start = (bf16[8,128,640]{2,1,0:T(8,128)(2,1)}, bf16[8,128,640]{2,1,0:T(8,128)(2,1)S(1)}, u32[]{:S(2)}) copy-start(bf16[8,128,640]{2,1,0:T(8,128)(2,1)S(1)} %all-to-all-done) | copy-start | bytes 3932164
  59.3 33.0 %all-to-all-start.1 = ((bf16[8,64,1024]{2,1,0:T(8,128)(2,1)}), bf16[8,64,1024]{2,1,0:T(8,128)(2,1)S(1)}, u32[]{:S(2)}, u32[]{:S(2)}) async-start(bf16[8,64,1024]{2,1,0:T(8,128)(2,1)} %broadcast_in_dim.2), calls=%async_computation.1 | async-start | bytes 2097152 | tf_op jit(solution)/shard_map/all_to_all | solution.py:277
  67.1 25.2 %collective-permute-start.1 = (bf16[128,1280]{1,0:T(8,128)(2,1)}, bf16[128,1280]{1,0:T(8,128)(2,1)S(1)}, u32[]{:S(2)}, u32[]{:S(2)}) collective-permute-start(bf16[128,1280]{1,0:T(8,128)(2,1)} %get-tuple-element.18), channel_id=1, source_target_pairs={{0,2},{2,4},{4,6},{6,0},{1,3},{3,5},{5,7},{7,1},{8,10},{10,12},{12... | collective-permute-start | bytes 983048 | tf_op jit(solution)/shard_map/ppermute | solution.py:273
  70.0 22.3 %collective-permute-start.2 = (bf16[128,1280]{1,0:T(8,128)(2,1)}, bf16[128,1280]{1,0:T(8,128)(2,1)S(1)}, u32[]{:S(2)}, u32[]{:S(2)}) collective-permute-start(bf16[128,1280]{1,0:T(8,128)(2,1)} %get-tuple-element.19), channel_id=1, source_target_pairs={{0,4},{2,6},{4,0},{6,2},{1,5},{3,7},{5,1},{7,3},{8,12},{10,14},{12... | collective-permute-start | bytes 983048 | tf_op jit(solution)/shard_map/ppermute | solution.py:273
  73.9 2.0 copy-start.3
  73.9 18.4 %collective-permute-start.3 = (bf16[128,1280]{1,0:T(8,128)(2,1)}, bf16[128,1280]{1,0:T(8,128)(2,1)S(1)}, u32[]{:S(2)}, u32[]{:S(2)}) collective-permute-start(bf16[128,1280]{1,0:T(8,128)(2,1)} %get-tuple-element.20), channel_id=1, source_target_pairs={{0,6},{2,0},{4,2},{6,4},{1,7},{3,1},{5,3},{7,5},{8,14},{10,8},{12,... | collective-permute-start | bytes 983048 | tf_op jit(solution)/shard_map/ppermute | solution.py:273
  75.8 0.7 copy-start.5
  75.8 0.8 copy-start.7
  92.3 0.8 copy-start.4
  92.3 0.9 copy-start.6
  92.3 1.0 copy-start.8
  92.4 1.4 copy-start.1
  110.0 4.8 %collective-permute-start.11 = (bf16[4,2,64,1024]{3,2,1,0:T(8,128)(2,1)}, bf16[4,2,64,1024]{3,2,1,0:T(8,128)(2,1)S(1)}, u32[]{:S(2)}, u32[]{:S(2)}) collective-permute-start(bf16[4,2,64,1024]{3,2,1,0:T(8,128)(2,1)} %get-tuple-element.32), channel_id=1, source_target_pairs={{0,8},{8,0},{1,9},{9,1},{2,10},{10,2},{3,11},{11,3},{4,12},{12,4},... | collective-permute-start | bytes 3145736 | tf_op jit(solution)/shard_map/ppermute | solution.py:273
  114.8 7.5 %copy-start.11 = (bf16[256,512]{1,0:T(8,128)(2,1)S(1)}, bf16[256,512]{1,0:T(8,128)(2,1)}, u32[]{:S(2)}) copy-start(bf16[256,512]{1,0:T(8,128)(2,1)} %get-tuple-element.28) | copy-start | bytes 786436
  114.8 12.6 %copy-start.10 = (bf16[256,512]{1,0:T(8,128)(2,1)S(1)}, bf16[256,512]{1,0:T(8,128)(2,1)}, u32[]{:S(2)}) copy-start(bf16[256,512]{1,0:T(8,128)(2,1)} %get-tuple-element.29) | copy-start | bytes 786436
  114.8 14.9 %copy-start.9 = (bf16[256,512]{1,0:T(8,128)(2,1)S(1)}, bf16[256,512]{1,0:T(8,128)(2,1)}, u32[]{:S(2)}) copy-start(bf16[256,512]{1,0:T(8,128)(2,1)} %get-tuple-element.30) | copy-start | bytes 786436
  114.8 29.2 %copy-start.2 = (bf16[256,512]{1,0:T(8,128)(2,1)S(1)}, bf16[256,512]{1,0:T(8,128)(2,1)}, u32[]{:S(2)}) copy-start(bf16[256,512]{1,0:T(8,128)(2,1)} %get-tuple-element.27) | copy-start | bytes 786436
  117.5 26.6 %all-to-all-start.2 = ((bf16[4,2,64,1024]{3,2,1,0:T(8,128)(2,1)}), bf16[4,2,64,1024]{3,2,1,0:T(8,128)(2,1)S(1)}, u32[]{:S(2)}, u32[]{:S(2)}) async-start(bf16[4,2,64,1024]{3,2,1,0:T(8,128)(2,1)} %add_convert_fusion), calls=%async_computation.2 | async-start | bytes 2097152 | tf_op jit(solution)/shard_map/all_to_all | solution.py:277
  122.3 16.0 %collective-permute-start.7 = (bf16[256,512]{1,0:T(8,128)(2,1)S(1)}, bf16[256,512]{1,0:T(8,128)(2,1)S(1)}, u32[]{:S(2)}, u32[]{:S(2)}) collective-permute-start(bf16[256,512]{1,0:T(8,128)(2,1)S(1)} %copy-done.11), channel_id=1, source_target_pairs={{0,2},{2,4},{4,6},{6,0},{1,3},{3,5},{5,7},{7,1},{8,10},{10,12},{12... | collective-permute-start | bytes 786440 | tf_op jit(solution)/shard_map/ppermute | solution.py:273
  127.4 12.7 %collective-permute-start.8 = (bf16[256,512]{1,0:T(8,128)(2,1)S(1)}, bf16[256,512]{1,0:T(8,128)(2,1)S(1)}, u32[]{:S(2)}, u32[]{:S(2)}) collective-permute-start(bf16[256,512]{1,0:T(8,128)(2,1)S(1)} %copy-done.10), channel_id=1, source_target_pairs={{0,4},{2,6},{4,0},{6,2},{1,5},{3,7},{5,1},{7,3},{8,12},{10,14},{12... | collective-permute-start | bytes 786440 | tf_op jit(solution)/shard_map/ppermute | solution.py:273
  129.7 14.2 %collective-permute-start.9 = (bf16[256,512]{1,0:T(8,128)(2,1)S(1)}, bf16[256,512]{1,0:T(8,128)(2,1)S(1)}, u32[]{:S(2)}, u32[]{:S(2)}) collective-permute-start(bf16[256,512]{1,0:T(8,128)(2,1)S(1)} %copy-done.9), channel_id=1, source_target_pairs={{0,6},{2,0},{4,2},{6,4},{1,7},{3,1},{5,3},{7,5},{8,14},{10,8},{12,... | collective-permute-start | bytes 786440 | tf_op jit(solution)/shard_map/ppermute | solution.py:273
  145.1 80.0 %all-to-all-start.3 = ((bf16[16,8,1024]{2,1,0:T(8,128)(2,1)}), bf16[16,8,1024]{2,1,0:T(8,128)(2,1)S(1)}, u32[]{:S(2)}, u32[]{:S(2)}) async-start(bf16[16,8,1024]{2,1,0:T(8,128)(2,1)} %bitcast.9), calls=%async_computation.3 | async-start | bytes 524288 | tf_op jit(solution)/shard_map/all_to_all | solution.py:277
  190.7 33.6 %collective-permute-start.10 = (bf16[128,512]{1,0:T(8,128)(2,1)S(1)}, bf16[128,512]{1,0:T(8,128)(2,1)S(1)}, u32[]{:S(2)}, u32[]{:S(2)}) collective-permute-start(bf16[128,512]{1,0:T(8,128)(2,1)S(1)} %fusion), channel_id=1, source_target_pairs={{0,1},{1,0},{2,3},{3,2},{4,5},{5,4},{6,7},{7,6},{8,9},{9,8},{10,11... | collective-permute-start | bytes 393224 | tf_op jit(solution)/shard_map/ppermute | solution.py:273

commit v2 on v1

v2 whole, which is shorter than its diff:
```python
import functools
import math

import jax
import jax.numpy as jnp
from jax import lax
from jax.experimental import pallas as pl
from jax.experimental.pallas import tpu as pltpu
from jax.sharding import Mesh
from jax.sharding import PartitionSpec as P

NOPE = 128
ROPE = 64
VDIM = 128
QW = NOPE + ROPE
KVW = NOPE + VDIM
RANK = 512
SCALE = QW ** (-0.5)
BF16 = jnp.bfloat16
F32 = jnp.float32
NT = (((1,), (1,)), ((), ()))


def head_pair(kv, rope, q2, g2, w, bias, lat_t):
    length = kv.shape[0]
    half = length // 2
    weight_parts = []
    latent_sum = None
    for h in range(2):
        keys = kv[:, h * KVW : h * KVW + NOPE]
        values = kv[:, h * KVW + NOPE : (h + 1) * KVW]
        keys_full = jnp.concatenate([keys, rope], axis=1)
        query = q2[:, h * QW : (h + 1) * QW]
        query_nope = query[:, :NOPE]
        grad = g2[:, h * VDIM : (h + 1) * VDIM]
        key_grad = [None, None]
        value_grad = [None, None]
        rows_each = half // 2
        for part in range(2):
            rows = slice(part * rows_each, (part + 1) * rows_each)
            n_keys = half * (part + 1)
            scores = lax.dot_general(
                keys_full[:n_keys], query[rows], NT, preferred_element_type=F32
            )
            masked = scores[n_keys - half :] + bias
            scores = masked if part == 0 else jnp.concatenate([scores[:half], masked], axis=0)
            row_max = jnp.max(scores, axis=0, keepdims=True)
            expo = jnp.exp2((scores - row_max) * (SCALE * math.log2(math.e)))
            probs = expo * (1.0 / jnp.sum(expo, axis=0, keepdims=True))
            probs_rounded = probs.astype(BF16)
            prob_grad = lax.dot_general(
                values[:n_keys], grad[rows], NT, preferred_element_type=F32
            )
            row_dot = jnp.sum(probs * prob_grad, axis=0, keepdims=True)
            score_grad = (probs * (prob_grad - row_dot)).astype(BF16)
            for block in range(part + 1):
                cut = slice(block * half, (block + 1) * half)
                value_part = jnp.dot(probs_rounded[cut], grad[rows], preferred_element_type=F32)
                key_part = jnp.dot(score_grad[cut], query_nope[rows], preferred_element_type=F32)
                if value_grad[block] is None:
                    value_grad[block], key_grad[block] = value_part, key_part
                else:
                    value_grad[block] = value_grad[block] + value_part
                    key_grad[block] = key_grad[block] + key_part
        grad_cols = jnp.concatenate(
            [
                jnp.concatenate([key_grad[b] * SCALE, value_grad[b]], axis=1).astype(BF16)
                for b in range(2)
            ],
            axis=0,
        )
        weight_parts.append(jnp.dot(lat_t, grad_cols, preferred_element_type=F32).astype(BF16))
        latent_part = lax.dot_general(
            grad_cols, w[:, h * KVW : (h + 1) * KVW], NT, preferred_element_type=F32
        )
        latent_sum = latent_part if latent_sum is None else latent_sum + latent_part
    return weight_parts, latent_sum


def attention_kernel(n_core, n_x, n_zl, n_y, place_ref, *refs):
    mine_ref, lat_refs, refs = refs[0], refs[1 : n_y + 1], refs[n_y + 1 :]
    q_ref, g_ref, own_w_ref, other_w_ref, keep_ref, send_ref = refs[:6]
    lg_refs = refs[6 : n_y + 6]
    lat, bias, lat_t, total, weight = refs[n_y + 6 :]
    step = pl.program_id(0)
    zh, y, core = place_ref[0], place_ref[1], place_ref[2]
    rows = total.shape[0] // n_y
    tokens = rows // 2

    @pl.when(step == 0)
    def _():
        for k in range(n_y):
            start = pl.multiple_of((k * 2 + zh) * tokens, tokens)
            lat[pl.ds(start, tokens), :] = mine_ref[k * tokens : (k + 1) * tokens]
            start = pl.multiple_of((((y + n_y - k) % n_y) * 2 + 1 - zh) * tokens, tokens)
            lat[pl.ds(start, tokens), :] = lat_refs[k][...]
        key_pos = lax.broadcasted_iota(jnp.int32, bias.shape, 0)
        lane = lax.broadcasted_iota(jnp.int32, bias.shape, 1)
        block = jnp.where(lane >= 128, 2, 0) + zh
        query_pos = block * 128 + (lane & 127)
        bias[...] = jnp.where(key_pos <= query_pos, F32(0.0), F32(-1e30))
        rows_each = RANK // (n_core * n_x * n_zl)
        row = lax.broadcasted_iota(jnp.int32, (RANK, RANK), 0)
        col = lax.broadcasted_iota(jnp.int32, (RANK, RANK), 1)
        inner = row % rows_each
        zl = (row // rows_each) % n_zl
        x = (row // (rows_each * n_zl)) % n_x
        away = row // (rows_each * n_zl * n_x)
        owner = core + away * (1 - 2 * core)
        wanted = ((x * n_zl + zl) * n_core + owner) * rows_each + inner
        pick = jnp.where(wanted == col, F32(1.0), F32(0.0)).astype(BF16)
        lat_t[...] = lax.dot_general(pick, lat[:, :RANK], NT, preferred_element_type=F32).astype(
            BF16
        )
        total[...] = jnp.zeros_like(total)

    held = step // (pl.num_programs(0) // 2) == zh

    @pl.when(held)
    def _():
        weight[...] = own_w_ref[...]

    @pl.when(jnp.logical_not(held))
    def _():
        weight[...] = other_w_ref[...]

    w = weight[...]
    kv = jnp.dot(lat[:, :RANK], w, preferred_element_type=F32).astype(BF16)
    weight_parts, latent_sum = head_pair(
        kv, lat[:, RANK : RANK + ROPE], q_ref[...], g_ref[...], w, bias[...], lat_t[...]
    )
    half = RANK // n_core
    for away, ref in enumerate((keep_ref, send_ref)):
        for h in range(2):
            part = weight_parts[h][away * half : (away + 1) * half].reshape(n_x, -1, KVW)
            ref[:, 0, :, h * KVW : (h + 1) * KVW] = part
    total[...] += latent_sum

    @pl.when(step == pl.num_programs(0) - 1)
    def _():
        for k in range(n_y):
            start = pl.multiple_of(((y + k) % n_y) * rows, rows)
            lg_refs[k][...] = total[pl.ds(start, rows), :].astype(BF16)


def attention(place, latents, query_grad, own_weight, other_weight, sizes):
    n_core, n_x, n_zl = sizes
    n_y = len(latents)
    q_rows, width = query_grad.shape[0], latents[0].shape[1]
    length = 2 * q_rows
    heads = 2 * own_weight.shape[1] // KVW
    steps = heads // 2
    g_blocks = heads * QW // (2 * VDIM)
    rows = RANK // (n_core * n_x)
    lat_spec = pl.BlockSpec((q_rows // n_y, width), lambda i, p: (0, 0))
    lat_block = heads * (QW + VDIM) // width
    w_spec = pl.BlockSpec((RANK, 2 * KVW), lambda i, p: (0, i % (steps // 2)))
    grad_spec = pl.BlockSpec(
        (n_x, 1, rows, 2 * KVW), lambda i, p: (0, i // (steps // 2), 0, i % (steps // 2))
    )
    grad_shape = jax.ShapeDtypeStruct((n_x, 2, rows, heads * KVW // 2), BF16)
    part_spec = pl.BlockSpec((length // n_y, RANK), lambda i, p: (0, 0))
    part_shape = jax.ShapeDtypeStruct((length // n_y, RANK), BF16)
    flops = heads * (3 * 2 * length * RANK * KVW + 4 * 2 * length * q_rows * 192)
    keep, send, *parts = pl.pallas_call(
        functools.partial(attention_kernel, n_core, n_x, n_zl, n_y),
        grid_spec=pltpu.PrefetchScalarGridSpec(
            num_scalar_prefetch=1,
            grid=(steps,),
            in_specs=[
                pl.BlockSpec((q_rows, width), lambda i, p: (0, lat_block)),
                *[lat_spec] * n_y,
                pl.BlockSpec((q_rows, 2 * QW), lambda i, p: (0, i)),
                pl.BlockSpec((q_rows, 2 * VDIM), lambda i, p: (0, g_blocks + i)),
                w_spec,
                w_spec,
            ],
            out_specs=[grad_spec, grad_spec, *[part_spec] * n_y],
            scratch_shapes=[
                pltpu.VMEM((length, width), BF16),
                pltpu.VMEM((length // 2, length // 4), F32),
                pltpu.VMEM((RANK, length), BF16),
                pltpu.VMEM((length, RANK), F32),
                pltpu.VMEM((RANK, 2 * KVW), BF16),
            ],
        ),
        out_shape=[grad_shape, grad_shape, *[part_shape] * n_y],
        compiler_params=pltpu.CompilerParams(
            dimension_semantics=("arbitrary",), vmem_limit_bytes=56 * 2**20
        ),
        cost_estimate=pl.CostEstimate(
            flops=flops, bytes_accessed=16 * 2**20, transcendentals=heads * length * q_rows
        ),
    )(place, query_grad, *latents, query_grad, query_grad, own_weight, other_weight)
    return keep, send, parts


def split_kernel(queries_ref, grads_ref, latent_ref, out_ref):
    offset = 0
    for ref in (queries_ref, grads_ref, latent_ref):
        out_ref[0, :, offset : offset + ref.shape[1]] = ref[...]
        offset += ref.shape[1]


def split_heads(queries, out_grad, packed, n_y):
    tokens = queries.shape[0]
    widths = (queries.shape[1] // n_y, out_grad.shape[1] // n_y, RANK + 2 * ROPE)
    shape = (n_y, tokens, sum(widths))
    return pl.pallas_call(
        split_kernel,
        grid=(n_y,),
        in_specs=[
            pl.BlockSpec((tokens, widths[0]), lambda i: (0, i)),
            pl.BlockSpec((tokens, widths[1]), lambda i: (0, i)),
            pl.BlockSpec((tokens, widths[2]), lambda i: (0, 0)),
        ],
        out_specs=pl.BlockSpec((1,) + shape[1:], lambda i: (i, 0, 0)),
        out_shape=jax.ShapeDtypeStruct(shape, BF16),
        cost_estimate=pl.CostEstimate(
            flops=0, bytes_accessed=4 * math.prod(shape), transcendentals=0
        ),
    )(queries, out_grad, packed)


def pack_kernel(place_ref, latent_ref, rope_ref, weight_ref, out_ref):
    tokens, rank = latent_ref.shape
    rope = rope_ref[...].astype(F32).T.astype(BF16)
    out_ref[:, :rank] = latent_ref[...]
    out_ref[:, rank : rank + 2 * ROPE] = jnp.concatenate([rope, jnp.zeros_like(rope)], axis=1)
    rows, width = weight_ref.shape
    for half in range(tokens // rows):
        columns = weight_ref[:, half * width // 2 : (half + 1) * width // 2]
        out_ref[half * rows : (half + 1) * rows, rank + 2 * ROPE :] = columns


def pack(place, latent, rope, weight, pieces):
    tokens, rank = latent.shape
    rows, width = weight.shape[0] // pieces, weight.shape[1]
    shape = (tokens, rank + 2 * ROPE + width // 2)
    return pl.pallas_call(
        pack_kernel,
        grid_spec=pltpu.PrefetchScalarGridSpec(
            num_scalar_prefetch=1,
            grid=(1,),
            in_specs=[
                pl.BlockSpec((tokens, rank), lambda i, p: (0, 0)),
                pl.BlockSpec((ROPE, tokens), lambda i, p: (0, 0)),
                pl.BlockSpec((rows, width), lambda i, p: (p[3], 0)),
            ],
            out_specs=pl.BlockSpec(shape, lambda i, p: (0, 0)),
        ),
        out_shape=jax.ShapeDtypeStruct(shape, BF16),
        cost_estimate=pl.CostEstimate(
            flops=0, bytes_accessed=4 * math.prod(shape), transcendentals=0
        ),
    )(place, latent, rope.T, weight)


def unpack_kernel(other_ref, lat_ref, weight_ref):
    width = lat_ref.shape[1]
    lat_ref[...] = other_ref[:, :width]
    count, rows, columns = weight_ref.shape
    for k in range(count):
        for half in range(2):
            part = other_ref[half * rows : (half + 1) * rows, width:]
            weight_ref[k, :, half * columns // 2 : (half + 1) * columns // 2] = part


def unpack(other, count, piece_rows):
    tokens, width = other.shape
    latent_width = RANK + 2 * ROPE
    piece = (count, piece_rows, (width - latent_width) * tokens // piece_rows)
    return pl.pallas_call(
        unpack_kernel,
        out_shape=[
            jax.ShapeDtypeStruct((tokens, latent_width), BF16),
            jax.ShapeDtypeStruct(piece, BF16),
        ],
        cost_estimate=pl.CostEstimate(
            flops=0, bytes_accessed=3 * math.prod(piece), transcendentals=0
        ),
    )(other)


def rotate(array, axis, shift):
    n = lax.axis_size(axis)
    return lax.ppermute(array, axis, [(i, (i + shift) % n) for i in range(n)])


def exchange(pieces, axes):
    return lax.all_to_all(pieces, axes, split_axis=0, concat_axis=0, tiled=True)


def add_up(pieces, dtype=BF16):
    return jnp.sum(pieces.astype(F32), axis=0).astype(dtype)


def per_device(queries, latent, key_rope, up_weight, out_grad):
    n_x, n_zl, n_core = lax.axis_size("x"), lax.axis_size("zl"), lax.axis_size("core")
    n_y, n_zh = lax.axis_size("y"), lax.axis_size("zh")
    zh, y, core = lax.axis_index("zh"), lax.axis_index("y"), lax.axis_index("core")
    mine = lax.axis_index("x") * n_core + core
    place = jnp.stack([zh, y, core, mine]).astype(jnp.int32)
    tokens = latent.shape[0]
    pieces = n_x * n_core

    packed = pack(place, latent, key_rope, up_weight, pieces)
    sent = split_heads(queries, out_grad, packed, n_y)
    query_grad = exchange(sent, "y").reshape(n_y * tokens, -1)
    latents, piece = unpack(rotate(packed, "zh", 1), pieces, RANK // pieces)
    latents = [latents] + [rotate(latents, "y", k + 1) for k in range(n_y - 1)]
    piece, query_grad = lax.optimization_barrier((piece, query_grad))
    other_weight = exchange(piece, ("x", "core")).reshape(up_weight.shape)

    sizes = (n_core, n_x, n_zl)
    keep, send, parts = attention(place, latents, query_grad, up_weight, other_weight, sizes)
    on_chip = (keep.astype(F32) + rotate(send, "core", 1).astype(F32)).astype(BF16)
    arrived = [parts[0]] + [rotate(a, "y", k + 1) for k, a in enumerate(parts[1:])]

    latent_sum = sum(a.astype(F32) for a in arrived).reshape(n_zh, tokens, RANK)
    sent = lax.dynamic_index_in_dim(latent_sum, 1 - zh, 0, keepdims=False).astype(BF16)
    kept = lax.dynamic_index_in_dim(latent_sum, zh, 0, keepdims=False)
    sent = rotate(sent, "zh", 1)
    latent_grad = kept + sent.astype(F32)

    over_x, _ = lax.optimization_barrier((add_up(exchange(on_chip, "x")), sent))
    over_x = over_x.reshape(n_zh, n_zl, -1, over_x.shape[2]).swapaxes(0, 1)
    over_x = over_x.reshape(n_zh * n_zl, -1, over_x.shape[3])
    weight_grad = add_up(exchange(over_x, ("zl", "zh")), F32)
    return latent_grad, weight_grad * (1.0 / (n_x * n_zl * n_core))


def solution(mesh):
    replicas, parts = mesh.shape["dp"], mesh.shape["seq"]
    shape = (replicas // 16, 8, 2, parts // 2, 2)
    names = ("x", "zl", "core", "y", "zh")
    torus = Mesh(mesh.devices.reshape(shape), names)
    rows = P(names, None)
    in_specs = (rows, rows, rows, P(None, ("y", "zh")), rows)
    out_specs = (rows, P(("x", "zl", "core"), ("y", "zh")))
    return jax.shard_map(
        per_device, mesh=torus, in_specs=in_specs, out_specs=out_specs, check_vma=False
    )
```

time: 227 us -> 192 us (0.85)
  the two profiles are of different devices: /device:TPU:26 before, /device:TPU:40 now
where the time goes in v2:
time: 192 us
  waiting for transfers between devices  75.5 us (39%)
  starting transfers between devices  73.7 us (38%)
  Pallas kernels  35.2 us (18%)
  other arithmetic  4.98 us (3%)
    ppermute x9, waiting for transfers between devices, rotate(): return lax.ppermute(array, axis, [(i, (i + shift) % n) for i in range(n)])  55.5 us
    ppermute x9, starting transfers between devices, rotate(): return lax.ppermute(array, axis, [(i, (i + shift) % n) for i in range(n)])  49 us
    pallas_call x1, Pallas kernels, attention(): pl.pallas_call(functools.partial(attention_kernel, n_core, n_x, n_zl, n_y...  26.5 us
    all_to_all x4, starting transfers between devices, exchange(): return lax.all_to_all(pieces, axes, split_axis=0, concat_axis=0, tiled=True)  24.7 us
    all_to_all x4, waiting for transfers between devices, exchange(): return lax.all_to_all(pieces, axes, split_axis=0, concat_axis=0, tiled=True)  20 us
    pallas_call x1, Pallas kernels, split_heads(): pl.pallas_call(split_kernel, grid=(n_y,), in_specs=[pl.BlockSpec((tokens,...  4.15 us
  transfers between devices with their start and end apart: 13, of which 9 were waited for; matrix products, arithmetic and copies ran while one was open for 1% of the time, Pallas kernels for 1%

profile of v2, /device:TPU:40, one launch (start us, length us, event | category | flops | bytes accessed | tf_op | source)
XLA Modules:
  0.0 191.6 jit_solution(3403651328620193965)
XLA Ops:
  0.6 0.6 pad_add_fusion.place_ref
  1.2 2.5 %shard_map.68.latent_ref = bf16[128,1152]{1,0:T(8,128)(2,1)} custom-call(s32[4]{0:T(128)} %pad_add_fusion.place_ref, bf16[128,512]{1,0:T(8,128)(2,1)} %latent_ref.1, bf16[64,128]{1,0:T(8,128)(2,1)} %bitcast.22, bf16[512,1024]{1,0:T(8,128)(2,1)} %refs_7_.1), custom_call_target="tpu_custom_call" | custom-call | bytes 589824 | tf_op jit(solution)/shard_map/pallas_call | solution.py:240
  3.7 4.1 %shard_map.70 = bf16[4,128,3200]{2,1,0:T(8,128)(2,1)} custom-call(bf16[128,6144]{1,0:T(8,128)(2,1)} %queries_ref.1, bf16[128,4096]{1,0:T(8,128)(2,1)} %grads_ref.1, bf16[128,1152]{1,0:T(8,128)(2,1)} %shard_map.68.latent_ref), custom_call_target="tpu_custom_call" | custom-call | bytes 6553600 | tf_op jit(solution)/shard_map/pallas_call | solution.py:209
  7.8 4.9 %all-to-all-start = ((bf16[4,128,3200]{2,1,0:T(8,128)(2,1)}), bf16[4,128,3200]{2,1,0:T(8,128)(2,1)S(1)}, u32[]{:S(2)}, u32[]{:S(2)}) async-start(bf16[4,128,3200]{2,1,0:T(8,128)(2,1)} %shard_map.70), calls=%async_computation | async-start | bytes 6553600 | tf_op jit(solution)/shard_map/all_to_all | solution.py:291
  12.7 14.8 %collective-permute-start = (bf16[128,1152]{1,0:T(8,128)(2,1)}, bf16[128,1152]{1,0:T(8,128)(2,1)}, u32[]{:S(2)}, u32[]{:S(2)}) collective-permute-start(bf16[128,1152]{1,0:T(8,128)(2,1)} %shard_map.68.latent_ref), channel_id=1, source_target_pairs={{0,1},{1,0},{2,3},{3,2},{4,5},{5,4},{6,7},{7,6},{8,9},{9,8},{10,11... | collective-permute-start | bytes 884744 | tf_op jit(solution)/shard_map/ppermute | solution.py:287
  27.5 25.4 %collective-permute-done.other_ref = bf16[128,1152]{1,0:T(8,128)(2,1)} collective-permute-done((bf16[128,1152]{1,0:T(8,128)(2,1)}, bf16[128,1152]{1,0:T(8,128)(2,1)}, u32[]{:S(2)}, u32[]{:S(2)}) %collective-permute-start) | collective-permute-done | bytes 294944 | tf_op jit(solution)/shard_map/ppermute | solution.py:287
  53.0 2.1 %shard_map.69 = (bf16[128,640]{1,0:T(8,128)(2,1)}, bf16[8,64,1024]{2,1,0:T(8,128)(2,1)}) custom-call(bf16[128,1152]{1,0:T(8,128)(2,1)} %collective-permute-done.other_ref), custom_call_target="tpu_custom_call" | custom-call | bytes 1572864 | tf_op jit(solution)/shard_map/pallas_call | solution.py:273
  55.0 0.0 copy-start.5
  55.0 0.0 all-to-all-done
  55.0 0.0 copy-start
  55.0 4.4 %all-to-all-start.1 = ((bf16[8,64,1024]{2,1,0:T(8,128)(2,1)}), bf16[8,64,1024]{2,1,0:T(8,128)(2,1)}, u32[]{:S(2)}, u32[]{:S(2)}) async-start(bf16[8,64,1024]{2,1,0:T(8,128)(2,1)} %get-tuple-element.16), calls=%async_computation.1 | async-start | bytes 2097152 | tf_op jit(solution)/shard_map/all_to_all | solution.py:291
  59.5 0.0 copy-done.5
  59.5 3.4 %collective-permute-start.1 = (bf16[128,640]{1,0:T(8,128)(2,1)S(1)}, bf16[128,640]{1,0:T(8,128)(2,1)S(1)}, u32[]{:S(2)}, u32[]{:S(2)}) collective-permute-start(bf16[128,640]{1,0:T(8,128)(2,1)S(1)} %copy-done.5), channel_id=1, source_target_pairs={{0,2},{2,4},{4,6},{6,0},{1,3},{3,5},{5,7},{7,1},{8,10},{10,12},{12... | collective-permute-start | bytes 491528 | tf_op jit(solution)/shard_map/ppermute | solution.py:287
  62.9 2.8 %collective-permute-start.2 = (bf16[128,640]{1,0:T(8,128)(2,1)S(1)}, bf16[128,640]{1,0:T(8,128)(2,1)S(1)}, u32[]{:S(2)}, u32[]{:S(2)}) collective-permute-start(bf16[128,640]{1,0:T(8,128)(2,1)S(1)} %copy-done.5), channel_id=1, source_target_pairs={{0,4},{2,6},{4,0},{6,2},{1,5},{3,7},{5,1},{7,3},{8,12},{10,14},{12... | collective-permute-start | bytes 491528 | tf_op jit(solution)/shard_map/ppermute | solution.py:287
  65.7 4.3 %collective-permute-start.3 = (bf16[128,640]{1,0:T(8,128)(2,1)S(1)}, bf16[128,640]{1,0:T(8,128)(2,1)}, u32[]{:S(2)}, u32[]{:S(2)}) collective-permute-start(bf16[128,640]{1,0:T(8,128)(2,1)S(1)} %copy-done.5), channel_id=1, source_target_pairs={{0,6},{2,0},{4,2},{6,4},{1,7},{3,1},{5,3},{7,5},{8,14},{10,8},{12,... | collective-permute-start | bytes 491528 | tf_op jit(solution)/shard_map/ppermute | solution.py:287
  69.9 0.0 collective-permute-done.1.refs_2_
  70.0 0.0 copy-start.6
  70.0 3.4 %collective-permute-done.2.refs_3_ = bf16[128,640]{1,0:T(8,128)(2,1)S(1)} collective-permute-done((bf16[128,640]{1,0:T(8,128)(2,1)S(1)}, bf16[128,640]{1,0:T(8,128)(2,1)S(1)}, u32[]{:S(2)}, u32[]{:S(2)}) %collective-permute-start.2) | collective-permute-done | bytes 163872 | tf_op jit(solution)/shard_map/ppermute | solution.py:287
  73.3 0.0 copy-done.6
  73.3 0.0 copy-start.7
  73.3 0.7 copy-done.7
  74.0 2.2 %collective-permute-done.3.refs_4_ = bf16[128,640]{1,0:T(8,128)(2,1)} collective-permute-done((bf16[128,640]{1,0:T(8,128)(2,1)S(1)}, bf16[128,640]{1,0:T(8,128)(2,1)}, u32[]{:S(2)}, u32[]{:S(2)}) %collective-permute-start.3) | collective-permute-done | bytes 163872 | tf_op jit(solution)/shard_map/ppermute | solution.py:287
  76.2 0.0 all-to-all-done.1
  76.2 0.0 copy-done
  76.2 26.5 %shard_map.71 = (bf16[4,2,64,1024]{3,2,1,0:T(8,128)(2,1)}, bf16[4,2,64,1024]{3,2,1,0:T(8,128)(2,1)}, bf16[256,512]{1,0:T(8,128)(2,1)}, bf16[256,512]{1,0:T(8,128...) custom-call(s32[4]{0:T(128)} %pad_add_fusion.place_ref, bf16[512,3200]{1,0:T(8,128)(2,1)} %bitcast.16, ...), custom_call_target="tpu_custom_call" | custom-call | flops 12884901888 | bytes 16777216 | tf_op jit(solution)/shard_map/pallas_call | solution.py:165
  102.7 1.9 %collective-permute-start.8 = (bf16[4,2,64,1024]{3,2,1,0:T(8,128)(2,1)}, bf16[4,2,64,1024]{3,2,1,0:T(8,128)(2,1)S(1)}, u32[]{:S(2)}, u32[]{:S(2)}) collective-permute-start(bf16[4,2,64,1024]{3,2,1,0:T(8,128)(2,1)} %get-tuple-element.22), channel_id=1, source_target_pairs={{0,8},{8,0},{1,9},{9,1},{2,10},{10,2},{3,11},{11,3},{4,12},{12,4},... | collective-permute-start | bytes 3145736 | tf_op jit(solution)/shard_map/ppermute | solution.py:287
  104.7 2.8 %collective-permute-done.8 = bf16[4,2,64,1024]{3,2,1,0:T(8,128)(2,1)S(1)} collective-permute-done((bf16[4,2,64,1024]{3,2,1,0:T(8,128)(2,1)}, bf16[4,2,64,1024]{3,2,1,0:T(8,128)(2,1)S(1)}, u32[]{:S(2)}, u32[]{:S(2)}) %collective-permute-start.8) | collective-permute-done | bytes 1048608 | tf_op jit(solution)/shard_map/ppermute | solution.py:287
  107.5 0.0 copy-start.4
  107.5 0.0 copy-start.3
  107.5 0.0 copy-start.2
  107.5 0.0 copy-start.1
  107.5 2.7 %add_convert_fusion = bf16[4,2,64,1024]{3,2,1,0:T(8,128)(2,1)} fusion(bf16[4,2,64,1024]{3,2,1,0:T(8,128)(2,1)S(1)} %collective-permute-done.8, bf16[4,2,64,1024]{3,2,1,0:T(8,128)(2,1)} %get-tuple-element.21), kind=kLoop, calls=%fused_computation | loop fusion | flops 2097152 | bytes 3145728 | tf_op jit(solution)/shard_map/convert_element_type | solution.py:317
  110.2 4.4 %all-to-all-start.2 = ((bf16[4,2,64,1024]{3,2,1,0:T(8,128)(2,1)}), bf16[4,2,64,1024]{3,2,1,0:T(8,128)(2,1)S(1)}, u32[]{:S(2)}, u32[]{:S(2)}) async-start(bf16[4,2,64,1024]{3,2,1,0:T(8,128)(2,1)} %add_convert_fusion), calls=%async_computation.2 | async-start | bytes 2097152 | tf_op jit(solution)/shard_map/all_to_all | solution.py:291
  114.6 0.0 copy-done.4
  114.6 2.5 %collective-permute-start.4 = (bf16[256,512]{1,0:T(8,128)(2,1)S(1)}, bf16[256,512]{1,0:T(8,128)(2,1)S(1)}, u32[]{:S(2)}, u32[]{:S(2)}) collective-permute-start(bf16[256,512]{1,0:T(8,128)(2,1)S(1)} %copy-done.4), channel_id=1, source_target_pairs={{0,2},{2,4},{4,6},{6,0},{1,3},{3,5},{5,7},{7,1},{8,10},{10,12},{12... | collective-permute-start | bytes 786440 | tf_op jit(solution)/shard_map/ppermute | solution.py:287
  117.1 0.0 copy-done.3
  117.1 3.2 %collective-permute-start.5 = (bf16[256,512]{1,0:T(8,128)(2,1)S(1)}, bf16[256,512]{1,0:T(8,128)(2,1)S(1)}, u32[]{:S(2)}, u32[]{:S(2)}) collective-permute-start(bf16[256,512]{1,0:T(8,128)(2,1)S(1)} %copy-done.3), channel_id=1, source_target_pairs={{0,4},{2,6},{4,0},{6,2},{1,5},{3,7},{5,1},{7,3},{8,12},{10,14},{12... | collective-permute-start | bytes 786440 | tf_op jit(solution)/shard_map/ppermute | solution.py:287
  120.4 0.0 copy-done.2
  120.4 4.0 %collective-permute-start.6 = (bf16[256,512]{1,0:T(8,128)(2,1)S(1)}, bf16[256,512]{1,0:T(8,128)(2,1)S(1)}, u32[]{:S(2)}, u32[]{:S(2)}) collective-permute-start(bf16[256,512]{1,0:T(8,128)(2,1)S(1)} %copy-done.2), channel_id=1, source_target_pairs={{0,6},{2,0},{4,2},{6,4},{1,7},{3,1},{5,3},{7,5},{8,14},{10,8},{12,... | collective-permute-start | bytes 786440 | tf_op jit(solution)/shard_map/ppermute | solution.py:287
  124.4 1.3 collective-permute-done.4
  125.7 4.1 %collective-permute-done.5 = bf16[256,512]{1,0:T(8,128)(2,1)S(1)} collective-permute-done((bf16[256,512]{1,0:T(8,128)(2,1)S(1)}, bf16[256,512]{1,0:T(8,128)(2,1)S(1)}, u32[]{:S(2)}, u32[]{:S(2)}) %collective-permute-start.5) | collective-permute-done | bytes 262176 | tf_op jit(solution)/shard_map/ppermute | solution.py:287
  129.8 4.1 %collective-permute-done.6 = bf16[256,512]{1,0:T(8,128)(2,1)S(1)} collective-permute-done((bf16[256,512]{1,0:T(8,128)(2,1)S(1)}, bf16[256,512]{1,0:T(8,128)(2,1)S(1)}, u32[]{:S(2)}, u32[]{:S(2)}) %collective-permute-start.6) | collective-permute-done | bytes 262176 | tf_op jit(solution)/shard_map/ppermute | solution.py:287
  133.9 0.0 copy-done.1
  133.9 0.1 convert_add_fusion
  134.1 12.1 %collective-permute-start.7 = (bf16[128,512]{1,0:T(8,128)(2,1)S(1)}, bf16[128,512]{1,0:T(8,128)(2,1)S(1)}, u32[]{:S(2)}, u32[]{:S(2)}) collective-permute-start(bf16[128,512]{1,0:T(8,128)(2,1)S(1)} %fusion), channel_id=1, source_target_pairs={{0,1},{1,0},{2,3},{3,2},{4,5},{5,4},{6,7},{7,6},{8,9},{9,8},{10,11... | collective-permute-start | bytes 393224 | tf_op jit(solution)/shard_map/ppermute | solution.py:287
  146.2 0.0 all-to-all-done.2
  146.2 0.2 reduce_sum.21
  146.4 12.2 %collective-permute-done.7 = bf16[128,512]{1,0:T(8,128)(2,1)S(1)} collective-permute-done((bf16[128,512]{1,0:T(8,128)(2,1)S(1)}, bf16[128,512]{1,0:T(8,128)(2,1)S(1)}, u32[]{:S(2)}, u32[]{:S(2)}) %collective-permute-start.7) | collective-permute-done | bytes 131104 | tf_op jit(solution)/shard_map/ppermute | solution.py:287
  158.6 0.7 copy.7
  159.3 10.9 %all-to-all-start.3 = ((bf16[16,8,1024]{2,1,0:T(8,128)(2,1)}), bf16[16,8,1024]{2,1,0:T(8,128)(2,1)S(1)}, u32[]{:S(2)}, u32[]{:S(2)}) async-start(bf16[16,8,1024]{2,1,0:T(8,128)(2,1)} %bitcast.12), calls=%async_computation.3 | async-start | bytes 524288 | tf_op jit(solution)/shard_map/all_to_all | solution.py:291
  170.2 0.7 bitcast_add_fusion
  171.0 20.0 %all-to-all-done.3 = bf16[16,8,1024]{2,1,0:T(8,128)(2,1)S(1)} async-done(((bf16[16,8,1024]{2,1,0:T(8,128)(2,1)}), bf16[16,8,1024]{2,1,0:T(8,128)(2,1)S(1)}, u32[]{:S(2)}, u32[]{:S(2)}) %all-to-all-start.3) | async-done | bytes 262176 | tf_op jit(solution)/shard_map/all_to_all | solution.py:291
  191.0 0.6 broadcast_multiply_fusion
  (2 shorter events, 0.1 us)
Async XLA Ops:
  7.8 47.2 %all-to-all-start = ((bf16[4,128,3200]{2,1,0:T(8,128)(2,1)}), bf16[4,128,3200]{2,1,0:T(8,128)(2,1)S(1)}, u32[]{:S(2)}, u32[]{:S(2)}) async-start(bf16[4,128,3200]{2,1,0:T(8,128)(2,1)} %shard_map.70), calls=%async_computation | async-start | bytes 6553600 | tf_op jit(solution)/shard_map/all_to_all | solution.py:291
  12.7 40.2 %collective-permute-start = (bf16[128,1152]{1,0:T(8,128)(2,1)}, bf16[128,1152]{1,0:T(8,128)(2,1)}, u32[]{:S(2)}, u32[]{:S(2)}) collective-permute-start(bf16[128,1152]{1,0:T(8,128)(2,1)} %shard_map.68.latent_ref), channel_id=1, source_target_pairs={{0,1},{1,0},{2,3},{3,2},{4,5},{5,4},{6,7},{7,6},{8,9},{9,8},{10,11... | collective-permute-start | bytes 884744 | tf_op jit(solution)/shard_map/ppermute | solution.py:287
  55.0 4.5 %copy-start.5 = (bf16[128,640]{1,0:T(8,128)(2,1)S(1)}, bf16[128,640]{1,0:T(8,128)(2,1)}, u32[]{:S(2)}) copy-start(bf16[128,640]{1,0:T(8,128)(2,1)} %get-tuple-element.15.refs_1_) | copy-start | bytes 491524
  55.0 21.2 %copy-start = (bf16[4,128,3200]{2,1,0:T(8,128)(2,1)}, bf16[4,128,3200]{2,1,0:T(8,128)(2,1)S(1)}, u32[]{:S(2)}) copy-start(bf16[4,128,3200]{2,1,0:T(8,128)(2,1)S(1)} %all-to-all-done) | copy-start | bytes 9830404
  55.0 21.2 %all-to-all-start.1 = ((bf16[8,64,1024]{2,1,0:T(8,128)(2,1)}), bf16[8,64,1024]{2,1,0:T(8,128)(2,1)}, u32[]{:S(2)}, u32[]{:S(2)}) async-start(bf16[8,64,1024]{2,1,0:T(8,128)(2,1)} %get-tuple-element.16), calls=%async_computation.1 | async-start | bytes 2097152 | tf_op jit(solution)/shard_map/all_to_all | solution.py:291
  59.5 10.5 %collective-permute-start.1 = (bf16[128,640]{1,0:T(8,128)(2,1)S(1)}, bf16[128,640]{1,0:T(8,128)(2,1)S(1)}, u32[]{:S(2)}, u32[]{:S(2)}) collective-permute-start(bf16[128,640]{1,0:T(8,128)(2,1)S(1)} %copy-done.5), channel_id=1, source_target_pairs={{0,2},{2,4},{4,6},{6,0},{1,3},{3,5},{5,7},{7,1},{8,10},{10,12},{12... | collective-permute-start | bytes 491528 | tf_op jit(solution)/shard_map/ppermute | solution.py:287
  62.9 10.5 %collective-permute-start.2 = (bf16[128,640]{1,0:T(8,128)(2,1)S(1)}, bf16[128,640]{1,0:T(8,128)(2,1)S(1)}, u32[]{:S(2)}, u32[]{:S(2)}) collective-permute-start(bf16[128,640]{1,0:T(8,128)(2,1)S(1)} %copy-done.5), channel_id=1, source_target_pairs={{0,4},{2,6},{4,0},{6,2},{1,5},{3,7},{5,1},{7,3},{8,12},{10,14},{12... | collective-permute-start | bytes 491528 | tf_op jit(solution)/shard_map/ppermute | solution.py:287
  65.7 10.5 %collective-permute-start.3 = (bf16[128,640]{1,0:T(8,128)(2,1)S(1)}, bf16[128,640]{1,0:T(8,128)(2,1)}, u32[]{:S(2)}, u32[]{:S(2)}) collective-permute-start(bf16[128,640]{1,0:T(8,128)(2,1)S(1)} %copy-done.5), channel_id=1, source_target_pairs={{0,6},{2,0},{4,2},{6,4},{1,7},{3,1},{5,3},{7,5},{8,14},{10,8},{12,... | collective-permute-start | bytes 491528 | tf_op jit(solution)/shard_map/ppermute | solution.py:287
  70.0 3.4 %copy-start.6 = (bf16[128,640]{1,0:T(8,128)(2,1)}, bf16[128,640]{1,0:T(8,128)(2,1)S(1)}, u32[]{:S(2)}) copy-start(bf16[128,640]{1,0:T(8,128)(2,1)S(1)} %collective-permute-done.1.refs_2_) | copy-start | bytes 491524
  73.3 0.7 copy-start.7
  102.7 4.8 %collective-permute-start.8 = (bf16[4,2,64,1024]{3,2,1,0:T(8,128)(2,1)}, bf16[4,2,64,1024]{3,2,1,0:T(8,128)(2,1)S(1)}, u32[]{:S(2)}, u32[]{:S(2)}) collective-permute-start(bf16[4,2,64,1024]{3,2,1,0:T(8,128)(2,1)} %get-tuple-element.22), channel_id=1, source_target_pairs={{0,8},{8,0},{1,9},{9,1},{2,10},{10,2},{3,11},{11,3},{4,12},{12,4},... | collective-permute-start | bytes 3145736 | tf_op jit(solution)/shard_map/ppermute | solution.py:287
  107.5 7.1 %copy-start.4 = (bf16[256,512]{1,0:T(8,128)(2,1)S(1)}, bf16[256,512]{1,0:T(8,128)(2,1)}, u32[]{:S(2)}) copy-start(bf16[256,512]{1,0:T(8,128)(2,1)} %get-tuple-element.18) | copy-start | bytes 786436
  107.5 9.6 %copy-start.3 = (bf16[256,512]{1,0:T(8,128)(2,1)S(1)}, bf16[256,512]{1,0:T(8,128)(2,1)}, u32[]{:S(2)}) copy-start(bf16[256,512]{1,0:T(8,128)(2,1)} %get-tuple-element.19) | copy-start | bytes 786436
  107.5 12.9 %copy-start.2 = (bf16[256,512]{1,0:T(8,128)(2,1)S(1)}, bf16[256,512]{1,0:T(8,128)(2,1)}, u32[]{:S(2)}) copy-start(bf16[256,512]{1,0:T(8,128)(2,1)} %get-tuple-element.20) | copy-start | bytes 786436
  107.5 26.4 %copy-start.1 = (bf16[256,512]{1,0:T(8,128)(2,1)S(1)}, bf16[256,512]{1,0:T(8,128)(2,1)}, u32[]{:S(2)}) copy-start(bf16[256,512]{1,0:T(8,128)(2,1)} %get-tuple-element.17) | copy-start | bytes 786436
  110.2 36.0 %all-to-all-start.2 = ((bf16[4,2,64,1024]{3,2,1,0:T(8,128)(2,1)}), bf16[4,2,64,1024]{3,2,1,0:T(8,128)(2,1)S(1)}, u32[]{:S(2)}, u32[]{:S(2)}) async-start(bf16[4,2,64,1024]{3,2,1,0:T(8,128)(2,1)} %add_convert_fusion), calls=%async_computation.2 | async-start | bytes 2097152 | tf_op jit(solution)/shard_map/all_to_all | solution.py:291
  114.6 11.1 %collective-permute-start.4 = (bf16[256,512]{1,0:T(8,128)(2,1)S(1)}, bf16[256,512]{1,0:T(8,128)(2,1)S(1)}, u32[]{:S(2)}, u32[]{:S(2)}) collective-permute-start(bf16[256,512]{1,0:T(8,128)(2,1)S(1)} %copy-done.4), channel_id=1, source_target_pairs={{0,2},{2,4},{4,6},{6,0},{1,3},{3,5},{5,7},{7,1},{8,10},{10,12},{12... | collective-permute-start | bytes 786440 | tf_op jit(solution)/shard_map/ppermute | solution.py:287
  117.1 12.7 %collective-permute-start.5 = (bf16[256,512]{1,0:T(8,128)(2,1)S(1)}, bf16[256,512]{1,0:T(8,128)(2,1)S(1)}, u32[]{:S(2)}, u32[]{:S(2)}) collective-permute-start(bf16[256,512]{1,0:T(8,128)(2,1)S(1)} %copy-done.3), channel_id=1, source_target_pairs={{0,4},{2,6},{4,0},{6,2},{1,5},{3,7},{5,1},{7,3},{8,12},{10,14},{12... | collective-permute-start | bytes 786440 | tf_op jit(solution)/shard_map/ppermute | solution.py:287
  120.4 13.5 %collective-permute-start.6 = (bf16[256,512]{1,0:T(8,128)(2,1)S(1)}, bf16[256,512]{1,0:T(8,128)(2,1)S(1)}, u32[]{:S(2)}, u32[]{:S(2)}) collective-permute-start(bf16[256,512]{1,0:T(8,128)(2,1)S(1)} %copy-done.2), channel_id=1, source_target_pairs={{0,6},{2,0},{4,2},{6,4},{1,7},{3,1},{5,3},{7,5},{8,14},{10,8},{12,... | collective-permute-start | bytes 786440 | tf_op jit(solution)/shard_map/ppermute | solution.py:287
  134.1 24.5 %collective-permute-start.7 = (bf16[128,512]{1,0:T(8,128)(2,1)S(1)}, bf16[128,512]{1,0:T(8,128)(2,1)S(1)}, u32[]{:S(2)}, u32[]{:S(2)}) collective-permute-start(bf16[128,512]{1,0:T(8,128)(2,1)S(1)} %fusion), channel_id=1, source_target_pairs={{0,1},{1,0},{2,3},{3,2},{4,5},{5,4},{6,7},{7,6},{8,9},{9,8},{10,11... | collective-permute-start | bytes 393224 | tf_op jit(solution)/shard_map/ppermute | solution.py:287
  159.3 31.6 %all-to-all-start.3 = ((bf16[16,8,1024]{2,1,0:T(8,128)(2,1)}), bf16[16,8,1024]{2,1,0:T(8,128)(2,1)S(1)}, u32[]{:S(2)}, u32[]{:S(2)}) async-start(bf16[16,8,1024]{2,1,0:T(8,128)(2,1)} %bitcast.12), calls=%async_computation.3 | async-start | bytes 524288 | tf_op jit(solution)/shard_map/all_to_all | solution.py:291

commit v3 on v2

--- a/solution.py
+++ b/solution.py
@@ -22,66 +22,70 @@
 
 
 def head_pair(kv, rope, q2, g2, w, bias, lat_t):
-    length = kv.shape[0]
-    half = length // 2
+    half = kv.shape[0] // 2
+    rows_each = half // 2
+    grad_cols = [[[None, None], [None, None]] for _ in range(2)]
+
+    def products(h, part):
+        n_keys = half * (part + 1)
+        rows = slice(part * rows_each, (part + 1) * rows_each)
+        keys = jnp.concatenate([kv[:n_keys, h * KVW : h * KVW + NOPE], rope[:n_keys]], axis=1)
+        values = kv[:n_keys, h * KVW + NOPE : (h + 1) * KVW]
+        query = q2[rows, h * QW : (h + 1) * QW]
+        grad = g2[rows, h * VDIM : (h + 1) * VDIM]
+        scores = lax.dot_general(keys, query, NT, preferred_element_type=F32)
+        prob_grad = lax.dot_general(values, grad, NT, preferred_element_type=F32)
+        return scores, prob_grad, query[:, :NOPE], grad
+
+    def softmax(part, scores, prob_grad):
+        if part == 0:
+            scores = scores + bias
+        else:
+            scores = jnp.concatenate([scores[:half], scores[half:] + bias], axis=0)
+        row_max = jnp.max(scores, axis=0, keepdims=True)
+        expo = jnp.exp2((scores - row_max) * (SCALE * math.log2(math.e)))
+        probs = expo * (1.0 / jnp.sum(expo, axis=0, keepdims=True))
+        row_dot = jnp.sum(probs * prob_grad, axis=0, keepdims=True)
+        return probs.astype(BF16), (probs * (prob_grad - row_dot)).astype(BF16)
+
+    def accumulate(h, part, probs, score_grad, query_nope, grad):
+        for block in range(part + 1):
+            cut = slice(block * half, (block + 1) * half)
+            for which, (left, right) in enumerate(((score_grad, query_nope), (probs, grad))):
+                product = jnp.dot(left[cut], right, preferred_element_type=F32)
+                before = grad_cols[h][block][which]
+                grad_cols[h][block][which] = product if before is None else before + product
+
+    units = [(h, part) for h in range(2) for part in (1, 0)]
+    ready = products(*units[0])
+    for n, (h, part) in enumerate(units):
+        scores, prob_grad, query_nope, grad = ready
+        if n + 1 < len(units):
+            ready = products(*units[n + 1])
+        probs, score_grad = softmax(part, scores, prob_grad)
+        accumulate(h, part, probs, score_grad, query_nope, grad)
     weight_parts = []
     latent_sum = None
     for h in range(2):
-        keys = kv[:, h * KVW : h * KVW + NOPE]
-        values = kv[:, h * KVW + NOPE : (h + 1) * KVW]
-        keys_full = jnp.concatenate([keys, rope], axis=1)
-        query = q2[:, h * QW : (h + 1) * QW]
-        query_nope = query[:, :NOPE]
-        grad = g2[:, h * VDIM : (h + 1) * VDIM]
-        key_grad = [None, None]
-        value_grad = [None, None]
-        rows_each = half // 2
-        for part in range(2):
-            rows = slice(part * rows_each, (part + 1) * rows_each)
-            n_keys = half * (part + 1)
-            scores = lax.dot_general(
-                keys_full[:n_keys], query[rows], NT, preferred_element_type=F32
-            )
-            masked = scores[n_keys - half :] + bias
-            scores = masked if part == 0 else jnp.concatenate([scores[:half], masked], axis=0)
-            row_max = jnp.max(scores, axis=0, keepdims=True)
-            expo = jnp.exp2((scores - row_max) * (SCALE * math.log2(math.e)))
-            probs = expo * (1.0 / jnp.sum(expo, axis=0, keepdims=True))
-            probs_rounded = probs.astype(BF16)
-            prob_grad = lax.dot_general(
-                values[:n_keys], grad[rows], NT, preferred_element_type=F32
-            )
-            row_dot = jnp.sum(probs * prob_grad, axis=0, keepdims=True)
-            score_grad = (probs * (prob_grad - row_dot)).astype(BF16)
-            for block in range(part + 1):
-                cut = slice(block * half, (block + 1) * half)
-                value_part = jnp.dot(probs_rounded[cut], grad[rows], preferred_element_type=F32)
-                key_part = jnp.dot(score_grad[cut], query_nope[rows], preferred_element_type=F32)
-                if value_grad[block] is None:
-                    value_grad[block], key_grad[block] = value_part, key_part
-                else:
-                    value_grad[block] = value_grad[block] + value_part
-                    key_grad[block] = key_grad[block] + key_part
-        grad_cols = jnp.concatenate(
+        columns = jnp.concatenate(
             [
-                jnp.concatenate([key_grad[b] * SCALE, value_grad[b]], axis=1).astype(BF16)
-                for b in range(2)
+                jnp.concatenate([key_grad * SCALE, value_grad], axis=1).astype(BF16)
+                for key_grad, value_grad in grad_cols[h]
             ],
             axis=0,
         )
-        weight_parts.append(jnp.dot(lat_t, grad_cols, preferred_element_type=F32).astype(BF16))
-        latent_part = lax.dot_general(
-            grad_cols, w[:, h * KVW : (h + 1) * KVW], NT, preferred_element_type=F32
+        weight_parts.append(jnp.dot(lat_t, columns, preferred_element_type=F32).astype(BF16))
+        part = lax.dot_general(
+            columns, w[:, h * KVW : (h + 1) * KVW], NT, preferred_element_type=F32
         )
-        latent_sum = latent_part if latent_sum is None else latent_sum + latent_part
+        latent_sum = part if latent_sum is None else latent_sum + part
     return weight_parts, latent_sum
 
 
 def attention_kernel(n_core, n_x, n_zl, n_y, place_ref, *refs):
     mine_ref, lat_refs, refs = refs[0], refs[1 : n_y + 1], refs[n_y + 1 :]
     q_ref, g_ref, own_w_ref, other_w_ref, keep_ref, send_ref = refs[:6]
-    lg_refs = refs[6 : n_y + 6]
-    lat, bias, lat_t, total, weight = refs[n_y + 6 :]
+    lg_ref, lat, bias, lat_t, total, weight = refs[6:]
     step = pl.program_id(0)
     zh, y, core = place_ref[0], place_ref[1], place_ref[2]
     rows = total.shape[0] // n_y
@@ -94,17 +98,17 @@
             lat[pl.ds(start, tokens), :] = mine_ref[k * tokens : (k + 1) * tokens]
             start = pl.multiple_of((((y + n_y - k) % n_y) * 2 + 1 - zh) * tokens, tokens)
             lat[pl.ds(start, tokens), :] = lat_refs[k][...]
-        key_pos = lax.broadcasted_iota(jnp.int32, bias.shape, 0)
-        lane = lax.broadcasted_iota(jnp.int32, bias.shape, 1)
+        key_pos = lax.broadcasted_iota(jnp.int32, (bias.shape[0], 1), 0)
+        lane = lax.broadcasted_iota(jnp.int32, (1, bias.shape[1]), 1)
         block = jnp.where(lane >= 128, 2, 0) + zh
         query_pos = block * 128 + (lane & 127)
         bias[...] = jnp.where(key_pos <= query_pos, F32(0.0), F32(-1e30))
         rows_each = RANK // (n_core * n_x * n_zl)
-        row = lax.broadcasted_iota(jnp.int32, (RANK, RANK), 0)
-        col = lax.broadcasted_iota(jnp.int32, (RANK, RANK), 1)
+        row = lax.broadcasted_iota(jnp.int32, (RANK, 1), 0)
+        col = lax.broadcasted_iota(jnp.int32, (1, RANK), 1)
         inner = row % rows_each
         zl = (row // rows_each) % n_zl
-        x = (row // (rows_each * n_zl)) % n_x
+        x = (row // (rows_each * n_zl) + place_ref[3] // n_core) % n_x
         away = row // (rows_each * n_zl * n_x)
         owner = core + away * (1 - 2 * core)
         wanted = ((x * n_zl + zl) * n_core + owner) * rows_each + inner
@@ -138,9 +142,7 @@
 
     @pl.when(step == pl.num_programs(0) - 1)
     def _():
-        for k in range(n_y):
-            start = pl.multiple_of(((y + k) % n_y) * rows, rows)
-            lg_refs[k][...] = total[pl.ds(start, rows), :].astype(BF16)
+        lg_ref[...] = total[...].astype(BF16)
 
 
 def attention(place, latents, query_grad, own_weight, other_weight, sizes):
@@ -159,10 +161,10 @@
         (n_x, 1, rows, 2 * KVW), lambda i, p: (0, i // (steps // 2), 0, i % (steps // 2))
     )
     grad_shape = jax.ShapeDtypeStruct((n_x, 2, rows, heads * KVW // 2), BF16)
-    part_spec = pl.BlockSpec((length // n_y, RANK), lambda i, p: (0, 0))
-    part_shape = jax.ShapeDtypeStruct((length // n_y, RANK), BF16)
+    latent_spec = pl.BlockSpec((length, RANK), lambda i, p: (0, 0))
+    latent_shape = jax.ShapeDtypeStruct((length, RANK), BF16)
     flops = heads * (3 * 2 * length * RANK * KVW + 4 * 2 * length * q_rows * 192)
-    keep, send, *parts = pl.pallas_call(
+    return pl.pallas_call(
         functools.partial(attention_kernel, n_core, n_x, n_zl, n_y),
         grid_spec=pltpu.PrefetchScalarGridSpec(
             num_scalar_prefetch=1,
@@ -175,7 +177,7 @@
                 w_spec,
                 w_spec,
             ],
-            out_specs=[grad_spec, grad_spec, *[part_spec] * n_y],
+            out_specs=[grad_spec, grad_spec, latent_spec],
             scratch_shapes=[
                 pltpu.VMEM((length, width), BF16),
                 pltpu.VMEM((length // 2, length // 4), F32),
@@ -184,7 +186,7 @@
                 pltpu.VMEM((RANK, 2 * KVW), BF16),
             ],
         ),
-        out_shape=[grad_shape, grad_shape, *[part_shape] * n_y],
+        out_shape=[grad_shape, grad_shape, latent_shape],
         compiler_params=pltpu.CompilerParams(
             dimension_semantics=("arbitrary",), vmem_limit_bytes=56 * 2**20
         ),
@@ -192,7 +194,6 @@
             flops=flops, bytes_accessed=16 * 2**20, transcendentals=heads * length * q_rows
         ),
     )(place, query_grad, *latents, query_grad, query_grad, own_weight, other_weight)
-    return keep, send, parts
 
 
 def split_kernel(queries_ref, grads_ref, latent_ref, out_ref):
@@ -313,17 +314,20 @@
     other_weight = exchange(piece, ("x", "core")).reshape(up_weight.shape)
 
     sizes = (n_core, n_x, n_zl)
-    keep, send, parts = attention(place, latents, query_grad, up_weight, other_weight, sizes)
-    on_chip = (keep.astype(F32) + rotate(send, "core", 1).astype(F32)).astype(BF16)
-    arrived = [parts[0]] + [rotate(a, "y", k + 1) for k, a in enumerate(parts[1:])]
-
-    latent_sum = sum(a.astype(F32) for a in arrived).reshape(n_zh, tokens, RANK)
+    keep, send, latent_part = attention(place, latents, query_grad, up_weight, other_weight, sizes)
+    away = rotate(send, "core", 1)
+    on_chip = [(keep[k].astype(F32) + away[k].astype(F32)).astype(BF16) for k in range(n_x)]
+
+    arrived = exchange(latent_part.reshape(n_y, n_zh * tokens, RANK), "y")
+    latent_sum = add_up(arrived, F32).reshape(n_zh, tokens, RANK)
     sent = lax.dynamic_index_in_dim(latent_sum, 1 - zh, 0, keepdims=False).astype(BF16)
     kept = lax.dynamic_index_in_dim(latent_sum, zh, 0, keepdims=False)
     sent = rotate(sent, "zh", 1)
     latent_grad = kept + sent.astype(F32)
 
-    over_x, _ = lax.optimization_barrier((add_up(exchange(on_chip, "x")), sent))
+    over_x = [on_chip[0]] + [rotate(a, "x", k + 1) for k, a in enumerate(on_chip[1:])]
+    over_x = sum(a.astype(F32) for a in over_x).astype(BF16)
+    over_x, _ = lax.optimization_barrier((over_x, sent))
     over_x = over_x.reshape(n_zh, n_zl, -1, over_x.shape[2]).swapaxes(0, 1)
     over_x = over_x.reshape(n_zh * n_zl, -1, over_x.shape[3])
     weight_grad = add_up(exchange(over_x, ("zl", "zh")), F32)

time: 192 us -> 182 us (0.948)
  the two profiles are of different devices: /device:TPU:40 before, /device:TPU:38 now
where the time goes in v3:
time: 182 us; the launch traced here: 181 us
  starting transfers between devices  74.3 us (41%)
  waiting for transfers between devices  66.1 us (36%)
  Pallas kernels  34.4 us (19%)
  other arithmetic  4.93 us (3%)
    ppermute x9, starting transfers between devices, rotate(): return lax.ppermute(array, axis, [(i, (i + shift) % n) for i in range(n)])  49.1 us
    ppermute x9, waiting for transfers between devices, rotate(): return lax.ppermute(array, axis, [(i, (i + shift) % n) for i in range(n)])  40.7 us
    pallas_call x1, Pallas kernels, attention(): pl.pallas_call(functools.partial(attention_kernel, n_core, n_x, n_zl, n_y...  25.7 us
    all_to_all x4, waiting for transfers between devices, exchange(): return lax.all_to_all(pieces, axes, split_axis=0, concat_axis=0, tiled=True)  25.3 us
    all_to_all x4, starting transfers between devices, exchange(): return lax.all_to_all(pieces, axes, split_axis=0, concat_axis=0, tiled=True)  25.2 us
    pallas_call x1, Pallas kernels, split_heads(): pl.pallas_call(split_kernel, grid=(n_y,), in_specs=[pl.BlockSpec((tokens,...  4.16 us
  transfers between devices with their start and end apart: 13, of which 6 were waited for; matrix products, arithmetic and copies ran while one was open for 2% of the time, Pallas kernels for 1%

profile of v3, /device:TPU:38, one launch (start us, length us, event | category | flops | bytes accessed | tf_op | source)
XLA Modules:
  0.0 181.3 jit_solution(284888127064993141)
XLA Ops:
  0.6 0.6 pad_add_fusion.place_ref
  1.2 2.5 %shard_map.68.latent_ref = bf16[128,1152]{1,0:T(8,128)(2,1)} custom-call(s32[4]{0:T(128)} %pad_add_fusion.place_ref, bf16[128,512]{1,0:T(8,128)(2,1)} %latent_ref.1, bf16[64,128]{1,0:T(8,128)(2,1)} %bitcast.35, bf16[512,1024]{1,0:T(8,128)(2,1)} %refs_7_.1), custom_call_target="tpu_custom_call" | custom-call | bytes 589824 | tf_op jit(solution)/shard_map/pallas_call | solution.py:241
  3.7 4.2 %shard_map.70 = bf16[4,128,3200]{2,1,0:T(8,128)(2,1)} custom-call(bf16[128,6144]{1,0:T(8,128)(2,1)} %queries_ref.1, bf16[128,4096]{1,0:T(8,128)(2,1)} %grads_ref.1, bf16[128,1152]{1,0:T(8,128)(2,1)} %shard_map.68.latent_ref), custom_call_target="tpu_custom_call" | custom-call | bytes 6553600 | tf_op jit(solution)/shard_map/pallas_call | solution.py:210
  7.8 4.5 %all-to-all-start = ((bf16[4,128,3200]{2,1,0:T(8,128)(2,1)}), bf16[4,128,3200]{2,1,0:T(8,128)(2,1)S(1)}, u32[]{:S(2)}, u32[]{:S(2)}) async-start(bf16[4,128,3200]{2,1,0:T(8,128)(2,1)} %shard_map.70), calls=%async_computation | async-start | bytes 6553600 | tf_op jit(solution)/shard_map/all_to_all | solution.py:292
  12.3 14.8 %collective-permute-start = (bf16[128,1152]{1,0:T(8,128)(2,1)}, bf16[128,1152]{1,0:T(8,128)(2,1)}, u32[]{:S(2)}, u32[]{:S(2)}) collective-permute-start(bf16[128,1152]{1,0:T(8,128)(2,1)} %shard_map.68.latent_ref), channel_id=1, source_target_pairs={{0,1},{1,0},{2,3},{3,2},{4,5},{5,4},{6,7},{7,6},{8,9},{9,8},{10,11... | collective-permute-start | bytes 884744 | tf_op jit(solution)/shard_map/ppermute | solution.py:288
  27.1 25.7 %collective-permute-done.other_ref = bf16[128,1152]{1,0:T(8,128)(2,1)} collective-permute-done((bf16[128,1152]{1,0:T(8,128)(2,1)}, bf16[128,1152]{1,0:T(8,128)(2,1)}, u32[]{:S(2)}, u32[]{:S(2)}) %collective-permute-start) | collective-permute-done | bytes 294944 | tf_op jit(solution)/shard_map/ppermute | solution.py:288
  52.8 2.0 %shard_map.69 = (bf16[128,640]{1,0:T(8,128)(2,1)}, bf16[8,64,1024]{2,1,0:T(8,128)(2,1)}) custom-call(bf16[128,1152]{1,0:T(8,128)(2,1)} %collective-permute-done.other_ref), custom_call_target="tpu_custom_call" | custom-call | bytes 1572864 | tf_op jit(solution)/shard_map/pallas_call | solution.py:274
  54.9 0.0 all-to-all-done
  54.9 0.0 copy-start
  54.9 4.8 %all-to-all-start.1 = ((bf16[8,64,1024]{2,1,0:T(8,128)(2,1)}), bf16[8,64,1024]{2,1,0:T(8,128)(2,1)}, u32[]{:S(2)}, u32[]{:S(2)}) async-start(bf16[8,64,1024]{2,1,0:T(8,128)(2,1)} %get-tuple-element.13), calls=%async_computation.1 | async-start | bytes 2097152 | tf_op jit(solution)/shard_map/all_to_all | solution.py:292
  59.7 3.6 %collective-permute-start.1 = (bf16[128,640]{1,0:T(8,128)(2,1)}, bf16[128,640]{1,0:T(8,128)(2,1)S(1)}, u32[]{:S(2)}, u32[]{:S(2)}) collective-permute-start(bf16[128,640]{1,0:T(8,128)(2,1)} %get-tuple-element.12.refs_1_), channel_id=1, source_target_pairs={{0,2},{2,4},{4,6},{6,0},{1,3},{3,5},{5,7},{7,1},{8,10},{10,12},{12... | collective-permute-start | bytes 491528 | tf_op jit(solution)/shard_map/ppermute | solution.py:288
  63.3 4.6 %collective-permute-start.2 = (bf16[128,640]{1,0:T(8,128)(2,1)}, bf16[128,640]{1,0:T(8,128)(2,1)}, u32[]{:S(2)}, u32[]{:S(2)}) collective-permute-start(bf16[128,640]{1,0:T(8,128)(2,1)} %get-tuple-element.12.refs_1_), channel_id=1, source_target_pairs={{0,4},{2,6},{4,0},{6,2},{1,5},{3,7},{5,1},{7,3},{8,12},{10,14},{12... | collective-permute-start | bytes 491528 | tf_op jit(solution)/shard_map/ppermute | solution.py:288
  67.9 3.4 %collective-permute-start.3 = (bf16[128,640]{1,0:T(8,128)(2,1)}, bf16[128,640]{1,0:T(8,128)(2,1)}, u32[]{:S(2)}, u32[]{:S(2)}) collective-permute-start(bf16[128,640]{1,0:T(8,128)(2,1)} %get-tuple-element.12.refs_1_), channel_id=1, source_target_pairs={{0,6},{2,0},{4,2},{6,4},{1,7},{3,1},{5,3},{7,5},{8,14},{10,8},{12,... | collective-permute-start | bytes 491528 | tf_op jit(solution)/shard_map/ppermute | solution.py:288
  71.3 0.0 collective-permute-done.1.refs_2_
  71.3 0.0 copy-start.1
  71.3 2.7 %collective-permute-done.2.refs_3_ = bf16[128,640]{1,0:T(8,128)(2,1)} collective-permute-done((bf16[128,640]{1,0:T(8,128)(2,1)}, bf16[128,640]{1,0:T(8,128)(2,1)}, u32[]{:S(2)}, u32[]{:S(2)}) %collective-permute-start.2) | collective-permute-done | bytes 163872 | tf_op jit(solution)/shard_map/ppermute | solution.py:288
  74.0 1.8 collective-permute-done.3.refs_4_
  75.8 0.0 all-to-all-done.1
  75.8 0.0 copy-done
  75.8 0.0 copy-done.1
  75.8 25.7 %shard_map.71 = (bf16[4,2,64,1024]{3,2,1,0:T(8,128)(2,1)}, bf16[4,2,64,1024]{3,2,1,0:T(8,128)(2,1)}, bf16[1024,512]{1,0:T(8,128)(2,1)}) custom-call(s32[4]{0:T(128)} %pad_add_fusion.place_ref, bf16[512,3200]{1,0:T(8,128)(2,1)} %bitcast.28, bf16[128,640]{1,0:T(8,128)(2,1)} %get-tuple-element.12.refs_1_, bf16[128,640]{1,0:T(8,128)(2,1)} %copy-done.1, ...), custom_call_target="tpu_custom_call" | custom-call | flops 12884901888 | bytes 16777216 | tf_op jit(solution)/shard_map/pallas_call | solution.py:167
  101.5 1.9 %collective-permute-start.5 = (bf16[4,2,64,1024]{3,2,1,0:T(8,128)(2,1)}, bf16[4,2,64,1024]{3,2,1,0:T(8,128)(2,1)S(1)}, u32[]{:S(2)}, u32[]{:S(2)}) collective-permute-start(bf16[4,2,64,1024]{3,2,1,0:T(8,128)(2,1)} %get-tuple-element.16), channel_id=1, source_target_pairs={{0,8},{8,0},{1,9},{9,1},{2,10},{10,2},{3,11},{11,3},{4,12},{12,4},... | collective-permute-start | bytes 3145736 | tf_op jit(solution)/shard_map/ppermute | solution.py:288
  103.5 4.0 %all-to-all-start.2 = ((bf16[4,256,512]{2,1,0:T(8,128)(2,1)}), bf16[4,256,512]{2,1,0:T(8,128)(2,1)S(1)}, u32[]{:S(2)}, u32[]{:S(2)}) async-start(bf16[4,256,512]{2,1,0:T(8,128)(2,1)} %bitcast.33), calls=%async_computation.2 | async-start | bytes 2097152 | tf_op jit(solution)/shard_map/all_to_all | solution.py:292
  107.5 0.0 collective-permute-done.5
  107.5 1.4 fusion.4
  108.9 2.3 %collective-permute-start.6 = (bf16[2,64,1024]{2,1,0:T(8,128)(2,1)S(1)}, bf16[2,64,1024]{2,1,0:T(8,128)(2,1)}, u32[]{:S(2)}, u32[]{:S(2)}) collective-permute-start(bf16[2,64,1024]{2,1,0:T(8,128)(2,1)S(1)} %get-tuple-element.18), channel_id=1, source_target_pairs={{0,128},{128,256},{256,384},{384,0},{1,129},{129,257},{257,385},{3... | collective-permute-start | bytes 786440 | tf_op jit(solution)/shard_map/ppermute | solution.py:288
  111.2 4.4 %collective-permute-start.7 = (bf16[2,64,1024]{2,1,0:T(8,128)(2,1)S(1)}, bf16[2,64,1024]{2,1,0:T(8,128)(2,1)}, u32[]{:S(2)}, u32[]{:S(2)}) collective-permute-start(bf16[2,64,1024]{2,1,0:T(8,128)(2,1)S(1)} %get-tuple-element.20), channel_id=1, source_target_pairs={{0,256},{128,384},{256,0},{384,128},{1,257},{129,385},{257,1},{385... | collective-permute-start | bytes 786440 | tf_op jit(solution)/shard_map/ppermute | solution.py:288
  115.7 1.9 %collective-permute-start.8 = (bf16[2,64,1024]{2,1,0:T(8,128)(2,1)S(1)}, bf16[2,64,1024]{2,1,0:T(8,128)(2,1)}, u32[]{:S(2)}, u32[]{:S(2)}) collective-permute-start(bf16[2,64,1024]{2,1,0:T(8,128)(2,1)S(1)} %get-tuple-element.19), channel_id=1, source_target_pairs={{0,384},{128,0},{256,128},{384,256},{1,385},{129,1},{257,129},{385... | collective-permute-start | bytes 786440 | tf_op jit(solution)/shard_map/ppermute | solution.py:288
  117.6 5.7 %all-to-all-done.2 = bf16[4,256,512]{2,1,0:T(8,128)(2,1)S(1)} async-done(((bf16[4,256,512]{2,1,0:T(8,128)(2,1)}), bf16[4,256,512]{2,1,0:T(8,128)(2,1)S(1)}, u32[]{:S(2)}, u32[]{:S(2)}) %all-to-all-start.2) | async-done | bytes 1048608 | tf_op jit(solution)/shard_map/all_to_all | solution.py:292
  123.3 0.1 convert_reduce_fusion
  123.4 12.2 %collective-permute-start.4 = (bf16[128,512]{1,0:T(8,128)(2,1)S(1)}, bf16[128,512]{1,0:T(8,128)(2,1)S(1)}, u32[]{:S(2)}, u32[]{:S(2)}) collective-permute-start(bf16[128,512]{1,0:T(8,128)(2,1)S(1)} %fusion.7), channel_id=1, source_target_pairs={{0,1},{1,0},{2,3},{3,2},{4,5},{5,4},{6,7},{7,6},{8,9},{9,8},{10,11... | collective-permute-start | bytes 393224 | tf_op jit(solution)/shard_map/ppermute | solution.py:288
  135.6 0.0 collective-permute-done.6
  135.6 0.0 collective-permute-done.7
  135.6 0.0 collective-permute-done.8
  135.6 1.4 fusion.2
  137.0 10.5 %collective-permute-done.4 = bf16[128,512]{1,0:T(8,128)(2,1)S(1)} collective-permute-done((bf16[128,512]{1,0:T(8,128)(2,1)S(1)}, bf16[128,512]{1,0:T(8,128)(2,1)S(1)}, u32[]{:S(2)}, u32[]{:S(2)}) %collective-permute-start.4) | collective-permute-done | bytes 131104 | tf_op jit(solution)/shard_map/ppermute | solution.py:288
  147.6 0.7 copy.7
  148.3 11.9 %all-to-all-start.3 = ((bf16[16,8,1024]{2,1,0:T(8,128)(2,1)}), bf16[16,8,1024]{2,1,0:T(8,128)(2,1)S(1)}, u32[]{:S(2)}, u32[]{:S(2)}) async-start(bf16[16,8,1024]{2,1,0:T(8,128)(2,1)} %bitcast.17), calls=%async_computation.3 | async-start | bytes 524288 | tf_op jit(solution)/shard_map/all_to_all | solution.py:292
  160.2 0.7 bitcast_add_fusion
  160.9 19.7 %all-to-all-done.3 = bf16[16,8,1024]{2,1,0:T(8,128)(2,1)S(1)} async-done(((bf16[16,8,1024]{2,1,0:T(8,128)(2,1)}), bf16[16,8,1024]{2,1,0:T(8,128)(2,1)S(1)}, u32[]{:S(2)}, u32[]{:S(2)}) %all-to-all-start.3) | async-done | bytes 262176 | tf_op jit(solution)/shard_map/all_to_all | solution.py:292
  180.6 0.6 broadcast_multiply_fusion
  (2 shorter events, 0.1 us)
Async XLA Ops:
  7.8 47.0 %all-to-all-start = ((bf16[4,128,3200]{2,1,0:T(8,128)(2,1)}), bf16[4,128,3200]{2,1,0:T(8,128)(2,1)S(1)}, u32[]{:S(2)}, u32[]{:S(2)}) async-start(bf16[4,128,3200]{2,1,0:T(8,128)(2,1)} %shard_map.70), calls=%async_computation | async-start | bytes 6553600 | tf_op jit(solution)/shard_map/all_to_all | solution.py:292
  12.3 40.5 %collective-permute-start = (bf16[128,1152]{1,0:T(8,128)(2,1)}, bf16[128,1152]{1,0:T(8,128)(2,1)}, u32[]{:S(2)}, u32[]{:S(2)}) collective-permute-start(bf16[128,1152]{1,0:T(8,128)(2,1)} %shard_map.68.latent_ref), channel_id=1, source_target_pairs={{0,1},{1,0},{2,3},{3,2},{4,5},{5,4},{6,7},{7,6},{8,9},{9,8},{10,11... | collective-permute-start | bytes 884744 | tf_op jit(solution)/shard_map/ppermute | solution.py:288
  54.9 20.9 %copy-start = (bf16[4,128,3200]{2,1,0:T(8,128)(2,1)}, bf16[4,128,3200]{2,1,0:T(8,128)(2,1)S(1)}, u32[]{:S(2)}) copy-start(bf16[4,128,3200]{2,1,0:T(8,128)(2,1)S(1)} %all-to-all-done) | copy-start | bytes 9830404
  54.9 20.9 %all-to-all-start.1 = ((bf16[8,64,1024]{2,1,0:T(8,128)(2,1)}), bf16[8,64,1024]{2,1,0:T(8,128)(2,1)}, u32[]{:S(2)}, u32[]{:S(2)}) async-start(bf16[8,64,1024]{2,1,0:T(8,128)(2,1)} %get-tuple-element.13), calls=%async_computation.1 | async-start | bytes 2097152 | tf_op jit(solution)/shard_map/all_to_all | solution.py:292
  59.7 11.6 %collective-permute-start.1 = (bf16[128,640]{1,0:T(8,128)(2,1)}, bf16[128,640]{1,0:T(8,128)(2,1)S(1)}, u32[]{:S(2)}, u32[]{:S(2)}) collective-permute-start(bf16[128,640]{1,0:T(8,128)(2,1)} %get-tuple-element.12.refs_1_), channel_id=1, source_target_pairs={{0,2},{2,4},{4,6},{6,0},{1,3},{3,5},{5,7},{7,1},{8,10},{10,12},{12... | collective-permute-start | bytes 491528 | tf_op jit(solution)/shard_map/ppermute | solution.py:288
  63.3 10.7 %collective-permute-start.2 = (bf16[128,640]{1,0:T(8,128)(2,1)}, bf16[128,640]{1,0:T(8,128)(2,1)}, u32[]{:S(2)}, u32[]{:S(2)}) collective-permute-start(bf16[128,640]{1,0:T(8,128)(2,1)} %get-tuple-element.12.refs_1_), channel_id=1, source_target_pairs={{0,4},{2,6},{4,0},{6,2},{1,5},{3,7},{5,1},{7,3},{8,12},{10,14},{12... | collective-permute-start | bytes 491528 | tf_op jit(solution)/shard_map/ppermute | solution.py:288
  67.9 7.9 %collective-permute-start.3 = (bf16[128,640]{1,0:T(8,128)(2,1)}, bf16[128,640]{1,0:T(8,128)(2,1)}, u32[]{:S(2)}, u32[]{:S(2)}) collective-permute-start(bf16[128,640]{1,0:T(8,128)(2,1)} %get-tuple-element.12.refs_1_), channel_id=1, source_target_pairs={{0,6},{2,0},{4,2},{6,4},{1,7},{3,1},{5,3},{7,5},{8,14},{10,8},{12,... | collective-permute-start | bytes 491528 | tf_op jit(solution)/shard_map/ppermute | solution.py:288
  71.3 4.5 %copy-start.1 = (bf16[128,640]{1,0:T(8,128)(2,1)}, bf16[128,640]{1,0:T(8,128)(2,1)S(1)}, u32[]{:S(2)}) copy-start(bf16[128,640]{1,0:T(8,128)(2,1)S(1)} %collective-permute-done.1.refs_2_) | copy-start | bytes 491524
  101.5 6.0 %collective-permute-start.5 = (bf16[4,2,64,1024]{3,2,1,0:T(8,128)(2,1)}, bf16[4,2,64,1024]{3,2,1,0:T(8,128)(2,1)S(1)}, u32[]{:S(2)}, u32[]{:S(2)}) collective-permute-start(bf16[4,2,64,1024]{3,2,1,0:T(8,128)(2,1)} %get-tuple-element.16), channel_id=1, source_target_pairs={{0,8},{8,0},{1,9},{9,1},{2,10},{10,2},{3,11},{11,3},{4,12},{12,4},... | collective-permute-start | bytes 3145736 | tf_op jit(solution)/shard_map/ppermute | solution.py:288
  103.5 19.8 %all-to-all-start.2 = ((bf16[4,256,512]{2,1,0:T(8,128)(2,1)}), bf16[4,256,512]{2,1,0:T(8,128)(2,1)S(1)}, u32[]{:S(2)}, u32[]{:S(2)}) async-start(bf16[4,256,512]{2,1,0:T(8,128)(2,1)} %bitcast.33), calls=%async_computation.2 | async-start | bytes 2097152 | tf_op jit(solution)/shard_map/all_to_all | solution.py:292
  108.9 26.7 %collective-permute-start.6 = (bf16[2,64,1024]{2,1,0:T(8,128)(2,1)S(1)}, bf16[2,64,1024]{2,1,0:T(8,128)(2,1)}, u32[]{:S(2)}, u32[]{:S(2)}) collective-permute-start(bf16[2,64,1024]{2,1,0:T(8,128)(2,1)S(1)} %get-tuple-element.18), channel_id=1, source_target_pairs={{0,128},{128,256},{256,384},{384,0},{1,129},{129,257},{257,385},{3... | collective-permute-start | bytes 786440 | tf_op jit(solution)/shard_map/ppermute | solution.py:288
  111.2 24.4 %collective-permute-start.7 = (bf16[2,64,1024]{2,1,0:T(8,128)(2,1)S(1)}, bf16[2,64,1024]{2,1,0:T(8,128)(2,1)}, u32[]{:S(2)}, u32[]{:S(2)}) collective-permute-start(bf16[2,64,1024]{2,1,0:T(8,128)(2,1)S(1)} %get-tuple-element.20), channel_id=1, source_target_pairs={{0,256},{128,384},{256,0},{384,128},{1,257},{129,385},{257,1},{385... | collective-permute-start | bytes 786440 | tf_op jit(solution)/shard_map/ppermute | solution.py:288
  115.7 20.0 %collective-permute-start.8 = (bf16[2,64,1024]{2,1,0:T(8,128)(2,1)S(1)}, bf16[2,64,1024]{2,1,0:T(8,128)(2,1)}, u32[]{:S(2)}, u32[]{:S(2)}) collective-permute-start(bf16[2,64,1024]{2,1,0:T(8,128)(2,1)S(1)} %get-tuple-element.19), channel_id=1, source_target_pairs={{0,384},{128,0},{256,128},{384,256},{1,385},{129,1},{257,129},{385... | collective-permute-start | bytes 786440 | tf_op jit(solution)/shard_map/ppermute | solution.py:288
  123.4 24.1 %collective-permute-start.4 = (bf16[128,512]{1,0:T(8,128)(2,1)S(1)}, bf16[128,512]{1,0:T(8,128)(2,1)S(1)}, u32[]{:S(2)}, u32[]{:S(2)}) collective-permute-start(bf16[128,512]{1,0:T(8,128)(2,1)S(1)} %fusion.7), channel_id=1, source_target_pairs={{0,1},{1,0},{2,3},{3,2},{4,5},{5,4},{6,7},{7,6},{8,9},{9,8},{10,11... | collective-permute-start | bytes 393224 | tf_op jit(solution)/shard_map/ppermute | solution.py:288
  148.3 32.3 %all-to-all-start.3 = ((bf16[16,8,1024]{2,1,0:T(8,128)(2,1)}), bf16[16,8,1024]{2,1,0:T(8,128)(2,1)S(1)}, u32[]{:S(2)}, u32[]{:S(2)}) async-start(bf16[16,8,1024]{2,1,0:T(8,128)(2,1)} %bitcast.17), calls=%async_computation.3 | async-start | bytes 524288 | tf_op jit(solution)/shard_map/all_to_all | solution.py:292

commit v4 on v3

--- a/solution.py
+++ b/solution.py
@@ -196,38 +196,42 @@
     )(place, query_grad, *latents, query_grad, query_grad, own_weight, other_weight)
 
 
-def split_kernel(queries_ref, grads_ref, latent_ref, out_ref):
-    offset = 0
-    for ref in (queries_ref, grads_ref, latent_ref):
-        out_ref[0, :, offset : offset + ref.shape[1]] = ref[...]
-        offset += ref.shape[1]
-
-
-def split_heads(queries, out_grad, packed, n_y):
-    tokens = queries.shape[0]
-    widths = (queries.shape[1] // n_y, out_grad.shape[1] // n_y, RANK + 2 * ROPE)
-    shape = (n_y, tokens, sum(widths))
+def latent_columns(latent_ref, rope_ref):
+    rope = rope_ref[...].astype(F32).T.astype(BF16)
+    return jnp.concatenate([latent_ref[...], rope, jnp.zeros_like(rope)], axis=1)
+
+
+def split_kernel(queries_ref, grads_ref, latent_ref, rope_ref, out_ref):
+    q_width, g_width = queries_ref.shape[1], grads_ref.shape[1]
+    out_ref[0, :, :q_width] = queries_ref[...]
+    out_ref[0, :, q_width : q_width + g_width] = grads_ref[...]
+    out_ref[0, :, q_width + g_width :] = latent_columns(latent_ref, rope_ref)
+
+
+def split_heads(queries, out_grad, latent, rope, n_y):
+    tokens, rank = latent.shape
+    widths = (queries.shape[1] // n_y, out_grad.shape[1] // n_y)
+    shape = (n_y, tokens, sum(widths) + rank + 2 * ROPE)
     return pl.pallas_call(
         split_kernel,
         grid=(n_y,),
         in_specs=[
             pl.BlockSpec((tokens, widths[0]), lambda i: (0, i)),
             pl.BlockSpec((tokens, widths[1]), lambda i: (0, i)),
-            pl.BlockSpec((tokens, widths[2]), lambda i: (0, 0)),
+            pl.BlockSpec((tokens, rank), lambda i: (0, 0)),
+            pl.BlockSpec((ROPE, tokens), lambda i: (0, 0)),
         ],
         out_specs=pl.BlockSpec((1,) + shape[1:], lambda i: (i, 0, 0)),
         out_shape=jax.ShapeDtypeStruct(shape, BF16),
         cost_estimate=pl.CostEstimate(
             flops=0, bytes_accessed=4 * math.prod(shape), transcendentals=0
         ),
-    )(queries, out_grad, packed)
+    )(queries, out_grad, latent, rope.T)
 
 
 def pack_kernel(place_ref, latent_ref, rope_ref, weight_ref, out_ref):
     tokens, rank = latent_ref.shape
-    rope = rope_ref[...].astype(F32).T.astype(BF16)
-    out_ref[:, :rank] = latent_ref[...]
-    out_ref[:, rank : rank + 2 * ROPE] = jnp.concatenate([rope, jnp.zeros_like(rope)], axis=1)
+    out_ref[:, : rank + 2 * ROPE] = latent_columns(latent_ref, rope_ref)
     rows, width = weight_ref.shape
     for half in range(tokens // rows):
         columns = weight_ref[:, half * width // 2 : (half + 1) * width // 2]
@@ -306,7 +310,7 @@
     pieces = n_x * n_core
 
     packed = pack(place, latent, key_rope, up_weight, pieces)
-    sent = split_heads(queries, out_grad, packed, n_y)
+    sent = split_heads(queries, out_grad, latent, key_rope, n_y)
     query_grad = exchange(sent, "y").reshape(n_y * tokens, -1)
     latents, piece = unpack(rotate(packed, "zh", 1), pieces, RANK // pieces)
     latents = [latents] + [rotate(latents, "y", k + 1) for k in range(n_y - 1)]
@@ -323,14 +327,16 @@
     sent = lax.dynamic_index_in_dim(latent_sum, 1 - zh, 0, keepdims=False).astype(BF16)
     kept = lax.dynamic_index_in_dim(latent_sum, zh, 0, keepdims=False)
     sent = rotate(sent, "zh", 1)
-    latent_grad = kept + sent.astype(F32)
-
     over_x = [on_chip[0]] + [rotate(a, "x", k + 1) for k, a in enumerate(on_chip[1:])]
     over_x = sum(a.astype(F32) for a in over_x).astype(BF16)
-    over_x, _ = lax.optimization_barrier((over_x, sent))
-    over_x = over_x.reshape(n_zh, n_zl, -1, over_x.shape[2]).swapaxes(0, 1)
-    over_x = over_x.reshape(n_zh * n_zl, -1, over_x.shape[3])
-    weight_grad = add_up(exchange(over_x, ("zl", "zh")), F32)
+    rows = over_x.shape[1] // n_zl
+    pieces = over_x.reshape(n_zh, n_zl, rows, -1).swapaxes(0, 1)
+    over_zl = add_up(exchange(pieces, "zl"), F32)
+    over_zl, sent = lax.optimization_barrier((over_zl, sent))
+    latent_grad = kept + sent.astype(F32)
+    own = lax.dynamic_index_in_dim(over_zl, zh, 0, keepdims=False)
+    other = lax.dynamic_index_in_dim(over_zl, 1 - zh, 0, keepdims=False)
+    weight_grad = own + rotate(other, "zh", 1)
     return latent_grad, weight_grad * (1.0 / (n_x * n_zl * n_core))
 
 

time: 182 us -> 187 us (1.027)
  the two profiles are of different devices: /device:TPU:38 before, /device:TPU:136 now
where the time goes in v4:
time: 187 us; the launch traced here: 186 us
  starting transfers between devices  74.3 us (40%)
  waiting for transfers between devices  70.5 us (38%)
  Pallas kernels  34.5 us (18%)
  other arithmetic  5.48 us (3%)
    ppermute x10, waiting for transfers between devices, rotate(): return lax.ppermute(array, axis, [(i, (i + shift) % n) for i in range(n)])  60 us
    ppermute x10, starting transfers between devices, rotate(): return lax.ppermute(array, axis, [(i, (i + shift) % n) for i in range(n)])  48.2 us
    all_to_all x4, starting transfers between devices, exchange(): return lax.all_to_all(pieces, axes, split_axis=0, concat_axis=0, tiled=True)  26.1 us
    pallas_call x1, Pallas kernels, attention(): pl.pallas_call(functools.partial(attention_kernel, n_core, n_x, n_zl, n_y...  25.7 us
    all_to_all x4, waiting for transfers between devices, exchange(): return lax.all_to_all(pieces, axes, split_axis=0, concat_axis=0, tiled=True)  10.5 us
    pallas_call x1, Pallas kernels, split_heads(): pl.pallas_call(split_kernel, grid=(n_y,), in_specs=[pl.BlockSpec((tokens,...  4.28 us
  transfers between devices with their start and end apart: 14, of which 9 were waited for; matrix products, arithmetic and copies ran while one was open for 3% of the time, Pallas kernels for 2%

profile of v4, /device:TPU:136, one launch (start us, length us, event | category | flops | bytes accessed | tf_op | source)
XLA Modules:
  0.0 185.7 jit_solution(6994823812773814999)
XLA Ops:
  0.6 4.3 %shard_map.70 = bf16[4,128,3200]{2,1,0:T(8,128)(2,1)} custom-call(bf16[128,6144]{1,0:T(8,128)(2,1)} %queries_ref.1, bf16[128,4096]{1,0:T(8,128)(2,1)} %grads_ref.1, bf16[128,512]{1,0:T(8,128)(2,1)} %latent_ref.3, bf16[64,128]{1,0:T(8,128)(2,1)} %bitcast.44), custom_call_target="tpu_custom_call" | custom-call | bytes 6553600 | tf_op jit(solution)/shard_map/pallas_call | solution.py:215
  4.9 4.9 %all-to-all-start = ((bf16[4,128,3200]{2,1,0:T(8,128)(2,1)}), bf16[4,128,3200]{2,1,0:T(8,128)(2,1)S(1)}, u32[]{:S(2)}, u32[]{:S(2)}) async-start(bf16[4,128,3200]{2,1,0:T(8,128)(2,1)} %shard_map.70), calls=%async_computation | async-start | bytes 6553600 | tf_op jit(solution)/shard_map/all_to_all | solution.py:296
  9.8 0.7 pad_add_fusion.place_ref
  10.5 2.5 %shard_map.68 = bf16[128,1152]{1,0:T(8,128)(2,1)} custom-call(s32[4]{0:T(128)} %pad_add_fusion.place_ref, bf16[128,512]{1,0:T(8,128)(2,1)} %latent_ref.3, bf16[64,128]{1,0:T(8,128)(2,1)} %bitcast.45, bf16[512,1024]{1,0:T(8,128)(2,1)} %refs_7_.1), custom_call_target="tpu_custom_call" | custom-call | bytes 589824 | tf_op jit(solution)/shard_map/pallas_call | solution.py:245
  13.0 10.9 %collective-permute-start = (bf16[128,1152]{1,0:T(8,128)(2,1)}, bf16[128,1152]{1,0:T(8,128)(2,1)}, u32[]{:S(2)}, u32[]{:S(2)}) collective-permute-start(bf16[128,1152]{1,0:T(8,128)(2,1)} %shard_map.68), channel_id=1, source_target_pairs={{0,1},{1,0},{2,3},{3,2},{4,5},{5,4},{6,7},{7,6},{8,9},{9,8},{10,11... | collective-permute-start | bytes 884744 | tf_op jit(solution)/shard_map/ppermute | solution.py:292
  23.9 23.4 %collective-permute-done.other_ref = bf16[128,1152]{1,0:T(8,128)(2,1)} collective-permute-done((bf16[128,1152]{1,0:T(8,128)(2,1)}, bf16[128,1152]{1,0:T(8,128)(2,1)}, u32[]{:S(2)}, u32[]{:S(2)}) %collective-permute-start) | collective-permute-done | bytes 294944 | tf_op jit(solution)/shard_map/ppermute | solution.py:292
  47.3 2.1 %shard_map.69 = (bf16[128,640]{1,0:T(8,128)(2,1)}, bf16[8,64,1024]{2,1,0:T(8,128)(2,1)}) custom-call(bf16[128,1152]{1,0:T(8,128)(2,1)} %collective-permute-done.other_ref), custom_call_target="tpu_custom_call" | custom-call | bytes 1572864 | tf_op jit(solution)/shard_map/pallas_call | solution.py:278
  49.3 0.0 all-to-all-done
  49.3 0.0 copy-start
  49.3 4.3 %all-to-all-start.1 = ((bf16[8,64,1024]{2,1,0:T(8,128)(2,1)}), bf16[8,64,1024]{2,1,0:T(8,128)(2,1)}, u32[]{:S(2)}, u32[]{:S(2)}) async-start(bf16[8,64,1024]{2,1,0:T(8,128)(2,1)} %get-tuple-element.14), calls=%async_computation.1 | async-start | bytes 2097152 | tf_op jit(solution)/shard_map/all_to_all | solution.py:296
  53.6 3.4 %collective-permute-start.1 = (bf16[128,640]{1,0:T(8,128)(2,1)}, bf16[128,640]{1,0:T(8,128)(2,1)S(1)}, u32[]{:S(2)}, u32[]{:S(2)}) collective-permute-start(bf16[128,640]{1,0:T(8,128)(2,1)} %get-tuple-element.13.refs_1_), channel_id=1, source_target_pairs={{0,2},{2,4},{4,6},{6,0},{1,3},{3,5},{5,7},{7,1},{8,10},{10,12},{12... | collective-permute-start | bytes 491528 | tf_op jit(solution)/shard_map/ppermute | solution.py:292
  57.0 2.8 %collective-permute-start.2 = (bf16[128,640]{1,0:T(8,128)(2,1)}, bf16[128,640]{1,0:T(8,128)(2,1)}, u32[]{:S(2)}, u32[]{:S(2)}) collective-permute-start(bf16[128,640]{1,0:T(8,128)(2,1)} %get-tuple-element.13.refs_1_), channel_id=1, source_target_pairs={{0,4},{2,6},{4,0},{6,2},{1,5},{3,7},{5,1},{7,3},{8,12},{10,14},{12... | collective-permute-start | bytes 491528 | tf_op jit(solution)/shard_map/ppermute | solution.py:292
  59.8 4.3 %collective-permute-start.3 = (bf16[128,640]{1,0:T(8,128)(2,1)}, bf16[128,640]{1,0:T(8,128)(2,1)}, u32[]{:S(2)}, u32[]{:S(2)}) collective-permute-start(bf16[128,640]{1,0:T(8,128)(2,1)} %get-tuple-element.13.refs_1_), channel_id=1, source_target_pairs={{0,6},{2,0},{4,2},{6,4},{1,7},{3,1},{5,3},{7,5},{8,14},{10,8},{12,... | collective-permute-start | bytes 491528 | tf_op jit(solution)/shard_map/ppermute | solution.py:292
  64.1 0.0 collective-permute-done.1.refs_2_
  64.1 0.0 copy-start.1
  64.1 3.7 %collective-permute-done.2.refs_3_ = bf16[128,640]{1,0:T(8,128)(2,1)} collective-permute-done((bf16[128,640]{1,0:T(8,128)(2,1)}, bf16[128,640]{1,0:T(8,128)(2,1)}, u32[]{:S(2)}, u32[]{:S(2)}) %collective-permute-start.2) | collective-permute-done | bytes 163872 | tf_op jit(solution)/shard_map/ppermute | solution.py:292
  67.8 2.8 %collective-permute-done.3.refs_4_ = bf16[128,640]{1,0:T(8,128)(2,1)} collective-permute-done((bf16[128,640]{1,0:T(8,128)(2,1)}, bf16[128,640]{1,0:T(8,128)(2,1)}, u32[]{:S(2)}, u32[]{:S(2)}) %collective-permute-start.3) | collective-permute-done | bytes 163872 | tf_op jit(solution)/shard_map/ppermute | solution.py:292
  70.6 0.0 all-to-all-done.1
  70.6 0.0 copy-done
  70.6 0.0 copy-done.1
  70.6 25.7 %shard_map.71 = (bf16[4,2,64,1024]{3,2,1,0:T(8,128)(2,1)}, bf16[4,2,64,1024]{3,2,1,0:T(8,128)(2,1)}, bf16[1024,512]{1,0:T(8,128)(2,1)}) custom-call(s32[4]{0:T(128)} %pad_add_fusion.place_ref, bf16[512,3200]{1,0:T(8,128)(2,1)} %bitcast.38, bf16[128,640]{1,0:T(8,128)(2,1)} %get-tuple-element.13.refs_1_, bf16[128,640]{1,0:T(8,128)(2,1)} %copy-done.1, ...), custom_call_target="tpu_custom_call" | custom-call | flops 12884901888 | bytes 16777216 | tf_op jit(solution)/shard_map/pallas_call | solution.py:167
  96.3 1.9 %collective-permute-start.4 = (bf16[4,2,64,1024]{3,2,1,0:T(8,128)(2,1)}, bf16[4,2,64,1024]{3,2,1,0:T(8,128)(2,1)S(1)}, u32[]{:S(2)}, u32[]{:S(2)}) collective-permute-start(bf16[4,2,64,1024]{3,2,1,0:T(8,128)(2,1)} %get-tuple-element.17), channel_id=1, source_target_pairs={{0,8},{8,0},{1,9},{9,1},{2,10},{10,2},{3,11},{11,3},{4,12},{12,4},... | collective-permute-start | bytes 3145736 | tf_op jit(solution)/shard_map/ppermute | solution.py:292
  98.2 3.9 %all-to-all-start.2 = ((bf16[4,256,512]{2,1,0:T(8,128)(2,1)}), bf16[4,256,512]{2,1,0:T(8,128)(2,1)S(1)}, u32[]{:S(2)}, u32[]{:S(2)}) async-start(bf16[4,256,512]{2,1,0:T(8,128)(2,1)} %bitcast.43), calls=%async_computation.2 | async-start | bytes 2097152 | tf_op jit(solution)/shard_map/all_to_all | solution.py:296
  102.2 0.0 collective-permute-done.4
  102.2 1.4 fusion.4
  103.6 4.8 %collective-permute-start.7 = (bf16[2,64,1024]{2,1,0:T(8,128)(2,1)S(1)}, bf16[2,64,1024]{2,1,0:T(8,128)(2,1)S(1)}, u32[]{:S(2)}, u32[]{:S(2)}) collective-permute-start(bf16[2,64,1024]{2,1,0:T(8,128)(2,1)S(1)} %get-tuple-element.21), channel_id=1, source_target_pairs={{0,384},{128,0},{256,128},{384,256},{1,385},{129,1},{257,129},{385... | collective-permute-start | bytes 786440 | tf_op jit(solution)/shard_map/ppermute | solution.py:292
  108.3 2.8 %collective-permute-start.6 = (bf16[2,64,1024]{2,1,0:T(8,128)(2,1)S(1)}, bf16[2,64,1024]{2,1,0:T(8,128)(2,1)S(1)}, u32[]{:S(2)}, u32[]{:S(2)}) collective-permute-start(bf16[2,64,1024]{2,1,0:T(8,128)(2,1)S(1)} %get-tuple-element.22), channel_id=1, source_target_pairs={{0,256},{128,384},{256,0},{384,128},{1,257},{129,385},{257,1},{385... | collective-permute-start | bytes 786440 | tf_op jit(solution)/shard_map/ppermute | solution.py:292
  111.1 2.8 %collective-permute-start.5 = (bf16[2,64,1024]{2,1,0:T(8,128)(2,1)S(1)}, bf16[2,64,1024]{2,1,0:T(8,128)(2,1)S(1)}, u32[]{:S(2)}, u32[]{:S(2)}) collective-permute-start(bf16[2,64,1024]{2,1,0:T(8,128)(2,1)S(1)} %get-tuple-element.20), channel_id=1, source_target_pairs={{0,128},{128,256},{256,384},{384,0},{1,129},{129,257},{257,385},{3... | collective-permute-start | bytes 786440 | tf_op jit(solution)/shard_map/ppermute | solution.py:292
  113.9 5.9 %collective-permute-done.7 = bf16[2,64,1024]{2,1,0:T(8,128)(2,1)S(1)} collective-permute-done((bf16[2,64,1024]{2,1,0:T(8,128)(2,1)S(1)}, bf16[2,64,1024]{2,1,0:T(8,128)(2,1)S(1)}, u32[]{:S(2)}, u32[]{:S(2)}) %collective-permute-start.7) | collective-permute-done | bytes 262176 | tf_op jit(solution)/shard_map/ppermute | solution.py:292
  119.8 1.2 collective-permute-done.6
  121.0 4.4 %collective-permute-done.5 = bf16[2,64,1024]{2,1,0:T(8,128)(2,1)S(1)} collective-permute-done((bf16[2,64,1024]{2,1,0:T(8,128)(2,1)S(1)}, bf16[2,64,1024]{2,1,0:T(8,128)(2,1)S(1)}, u32[]{:S(2)}, u32[]{:S(2)}) %collective-permute-start.5) | collective-permute-done | bytes 262176 | tf_op jit(solution)/shard_map/ppermute | solution.py:292
  125.4 1.9 %copy_bitcast_fusion = bf16[8,2,8,1024]{3,2,1,0:T(8,128)(2,1)} fusion(bf16[2,64,1024]{2,1,0:T(8,128)(2,1)S(1)} %collective-permute-done.7, bf16[2,64,1024]{2,1,0:T(8,128)(2,1)S(1)} %collective-permute-done.6, bf16[2,64,1024]{2,1,0:T(8,128)(2,1)S(1)} %collective-permute-done.5, bf16[4,2,64,1024]{3,2,1,0:T(8,128)(2,1)S(1)} %collective-permute-done.4, ...), kind=kLoop, calls=%fused_computation.16 | loop fusion | flops 1572864 | bytes 1572864 | tf_op jit(solution)/shard_map/transpose | solution.py:333
  127.3 0.0 all-to-all-done.2
  127.3 13.0 %all-to-all-start.3 = ((bf16[8,2,8,1024]{3,2,1,0:T(8,128)(2,1)}), bf16[8,2,8,1024]{3,2,1,0:T(8,128)(2,1)S(1)}, u32[]{:S(2)}, u32[]{:S(2)}) async-start(bf16[8,2,8,1024]{3,2,1,0:T(8,128)(2,1)} %copy_bitcast_fusion), calls=%async_computation.3 | async-start | bytes 524288 | tf_op jit(solution)/shard_map/all_to_all | solution.py:296
  140.2 0.1 convert_reduce_fusion
  140.4 9.8 %collective-permute-start.8 = (bf16[128,512]{1,0:T(8,128)(2,1)S(1)}, bf16[128,512]{1,0:T(8,128)(2,1)S(1)}, u32[]{:S(2)}, u32[]{:S(2)}) collective-permute-start(bf16[128,512]{1,0:T(8,128)(2,1)S(1)} %fusion.8), channel_id=1, source_target_pairs={{0,1},{1,0},{2,3},{3,2},{4,5},{5,4},{6,7},{7,6},{8,9},{9,8},{10,11... | collective-permute-start | bytes 393224 | tf_op jit(solution)/shard_map/ppermute | solution.py:292
  150.3 10.5 %all-to-all-done.3 = bf16[8,2,8,1024]{3,2,1,0:T(8,128)(2,1)S(1)} async-done(((bf16[8,2,8,1024]{3,2,1,0:T(8,128)(2,1)}), bf16[8,2,8,1024]{3,2,1,0:T(8,128)(2,1)S(1)}, u32[]{:S(2)}, u32[]{:S(2)}) %all-to-all-start.3) | async-done | bytes 262176 | tf_op jit(solution)/shard_map/all_to_all | solution.py:296
  160.8 9.7 %collective-permute-done.8 = bf16[128,512]{1,0:T(8,128)(2,1)S(1)} collective-permute-done((bf16[128,512]{1,0:T(8,128)(2,1)S(1)}, bf16[128,512]{1,0:T(8,128)(2,1)S(1)}, u32[]{:S(2)}, u32[]{:S(2)}) %collective-permute-start.8) | collective-permute-done | bytes 131104 | tf_op jit(solution)/shard_map/ppermute | solution.py:292
  170.5 4.9 %collective-permute-start.9 = (f32[8,1024]{1,0:T(8,128)S(1)}, f32[8,1024]{1,0:T(8,128)S(1)}, u32[]{:S(2)}, u32[]{:S(2)}) collective-permute-start(f32[8,1024]{1,0:T(8,128)S(1)} %dynamic-slice_bitcast_fusion), channel_id=1, source_target_pairs={{0,1},{1,0},{2,3},{3,2},{4,5},{5,4},{6,7},{7,6},{8,9},{9,8},{10,11... | collective-permute-start | bytes 98312 | tf_op jit(solution)/shard_map/ppermute | solution.py:292
  175.4 0.7 bitcast_add_fusion
  176.1 8.9 %collective-permute-done.9 = f32[8,1024]{1,0:T(8,128)S(1)} collective-permute-done((f32[8,1024]{1,0:T(8,128)S(1)}, f32[8,1024]{1,0:T(8,128)S(1)}, u32[]{:S(2)}, u32[]{:S(2)}) %collective-permute-start.9) | collective-permute-done | bytes 32800 | tf_op jit(solution)/shard_map/ppermute | solution.py:292
  185.0 0.6 fusion.9
  (3 shorter events, 0.1 us)
Async XLA Ops:
  4.9 44.4 %all-to-all-start = ((bf16[4,128,3200]{2,1,0:T(8,128)(2,1)}), bf16[4,128,3200]{2,1,0:T(8,128)(2,1)S(1)}, u32[]{:S(2)}, u32[]{:S(2)}) async-start(bf16[4,128,3200]{2,1,0:T(8,128)(2,1)} %shard_map.70), calls=%async_computation | async-start | bytes 6553600 | tf_op jit(solution)/shard_map/all_to_all | solution.py:296
  13.0 34.3 %collective-permute-start = (bf16[128,1152]{1,0:T(8,128)(2,1)}, bf16[128,1152]{1,0:T(8,128)(2,1)}, u32[]{:S(2)}, u32[]{:S(2)}) collective-permute-start(bf16[128,1152]{1,0:T(8,128)(2,1)} %shard_map.68), channel_id=1, source_target_pairs={{0,1},{1,0},{2,3},{3,2},{4,5},{5,4},{6,7},{7,6},{8,9},{9,8},{10,11... | collective-permute-start | bytes 884744 | tf_op jit(solution)/shard_map/ppermute | solution.py:292
  49.3 21.2 %copy-start = (bf16[4,128,3200]{2,1,0:T(8,128)(2,1)}, bf16[4,128,3200]{2,1,0:T(8,128)(2,1)S(1)}, u32[]{:S(2)}) copy-start(bf16[4,128,3200]{2,1,0:T(8,128)(2,1)S(1)} %all-to-all-done) | copy-start | bytes 9830404
  49.3 21.2 %all-to-all-start.1 = ((bf16[8,64,1024]{2,1,0:T(8,128)(2,1)}), bf16[8,64,1024]{2,1,0:T(8,128)(2,1)}, u32[]{:S(2)}, u32[]{:S(2)}) async-start(bf16[8,64,1024]{2,1,0:T(8,128)(2,1)} %get-tuple-element.14), calls=%async_computation.1 | async-start | bytes 2097152 | tf_op jit(solution)/shard_map/all_to_all | solution.py:296
  53.6 10.4 %collective-permute-start.1 = (bf16[128,640]{1,0:T(8,128)(2,1)}, bf16[128,640]{1,0:T(8,128)(2,1)S(1)}, u32[]{:S(2)}, u32[]{:S(2)}) collective-permute-start(bf16[128,640]{1,0:T(8,128)(2,1)} %get-tuple-element.13.refs_1_), channel_id=1, source_target_pairs={{0,2},{2,4},{4,6},{6,0},{1,3},{3,5},{5,7},{7,1},{8,10},{10,12},{12... | collective-permute-start | bytes 491528 | tf_op jit(solution)/shard_map/ppermute | solution.py:292
  57.0 10.8 %collective-permute-start.2 = (bf16[128,640]{1,0:T(8,128)(2,1)}, bf16[128,640]{1,0:T(8,128)(2,1)}, u32[]{:S(2)}, u32[]{:S(2)}) collective-permute-start(bf16[128,640]{1,0:T(8,128)(2,1)} %get-tuple-element.13.refs_1_), channel_id=1, source_target_pairs={{0,4},{2,6},{4,0},{6,2},{1,5},{3,7},{5,1},{7,3},{8,12},{10,14},{12... | collective-permute-start | bytes 491528 | tf_op jit(solution)/shard_map/ppermute | solution.py:292
  59.8 10.8 %collective-permute-start.3 = (bf16[128,640]{1,0:T(8,128)(2,1)}, bf16[128,640]{1,0:T(8,128)(2,1)}, u32[]{:S(2)}, u32[]{:S(2)}) collective-permute-start(bf16[128,640]{1,0:T(8,128)(2,1)} %get-tuple-element.13.refs_1_), channel_id=1, source_target_pairs={{0,6},{2,0},{4,2},{6,4},{1,7},{3,1},{5,3},{7,5},{8,14},{10,8},{12,... | collective-permute-start | bytes 491528 | tf_op jit(solution)/shard_map/ppermute | solution.py:292
  64.1 6.5 %copy-start.1 = (bf16[128,640]{1,0:T(8,128)(2,1)}, bf16[128,640]{1,0:T(8,128)(2,1)S(1)}, u32[]{:S(2)}) copy-start(bf16[128,640]{1,0:T(8,128)(2,1)S(1)} %collective-permute-done.1.refs_2_) | copy-start | bytes 491524
  96.3 5.9 %collective-permute-start.4 = (bf16[4,2,64,1024]{3,2,1,0:T(8,128)(2,1)}, bf16[4,2,64,1024]{3,2,1,0:T(8,128)(2,1)S(1)}, u32[]{:S(2)}, u32[]{:S(2)}) collective-permute-start(bf16[4,2,64,1024]{3,2,1,0:T(8,128)(2,1)} %get-tuple-element.17), channel_id=1, source_target_pairs={{0,8},{8,0},{1,9},{9,1},{2,10},{10,2},{3,11},{11,3},{4,12},{12,4},... | collective-permute-start | bytes 3145736 | tf_op jit(solution)/shard_map/ppermute | solution.py:292
  98.2 29.1 %all-to-all-start.2 = ((bf16[4,256,512]{2,1,0:T(8,128)(2,1)}), bf16[4,256,512]{2,1,0:T(8,128)(2,1)S(1)}, u32[]{:S(2)}, u32[]{:S(2)}) async-start(bf16[4,256,512]{2,1,0:T(8,128)(2,1)} %bitcast.43), calls=%async_computation.2 | async-start | bytes 2097152 | tf_op jit(solution)/shard_map/all_to_all | solution.py:296
  103.6 16.2 %collective-permute-start.7 = (bf16[2,64,1024]{2,1,0:T(8,128)(2,1)S(1)}, bf16[2,64,1024]{2,1,0:T(8,128)(2,1)S(1)}, u32[]{:S(2)}, u32[]{:S(2)}) collective-permute-start(bf16[2,64,1024]{2,1,0:T(8,128)(2,1)S(1)} %get-tuple-element.21), channel_id=1, source_target_pairs={{0,384},{128,0},{256,128},{384,256},{1,385},{129,1},{257,129},{385... | collective-permute-start | bytes 786440 | tf_op jit(solution)/shard_map/ppermute | solution.py:292
  108.3 12.6 %collective-permute-start.6 = (bf16[2,64,1024]{2,1,0:T(8,128)(2,1)S(1)}, bf16[2,64,1024]{2,1,0:T(8,128)(2,1)S(1)}, u32[]{:S(2)}, u32[]{:S(2)}) collective-permute-start(bf16[2,64,1024]{2,1,0:T(8,128)(2,1)S(1)} %get-tuple-element.22), channel_id=1, source_target_pairs={{0,256},{128,384},{256,0},{384,128},{1,257},{129,385},{257,1},{385... | collective-permute-start | bytes 786440 | tf_op jit(solution)/shard_map/ppermute | solution.py:292
  111.1 14.3 %collective-permute-start.5 = (bf16[2,64,1024]{2,1,0:T(8,128)(2,1)S(1)}, bf16[2,64,1024]{2,1,0:T(8,128)(2,1)S(1)}, u32[]{:S(2)}, u32[]{:S(2)}) collective-permute-start(bf16[2,64,1024]{2,1,0:T(8,128)(2,1)S(1)} %get-tuple-element.20), channel_id=1, source_target_pairs={{0,128},{128,256},{256,384},{384,0},{1,129},{129,257},{257,385},{3... | collective-permute-start | bytes 786440 | tf_op jit(solution)/shard_map/ppermute | solution.py:292
  127.3 33.5 %all-to-all-start.3 = ((bf16[8,2,8,1024]{3,2,1,0:T(8,128)(2,1)}), bf16[8,2,8,1024]{3,2,1,0:T(8,128)(2,1)S(1)}, u32[]{:S(2)}, u32[]{:S(2)}) async-start(bf16[8,2,8,1024]{3,2,1,0:T(8,128)(2,1)} %copy_bitcast_fusion), calls=%async_computation.3 | async-start | bytes 524288 | tf_op jit(solution)/shard_map/all_to_all | solution.py:296
  140.4 30.1 %collective-permute-start.8 = (bf16[128,512]{1,0:T(8,128)(2,1)S(1)}, bf16[128,512]{1,0:T(8,128)(2,1)S(1)}, u32[]{:S(2)}, u32[]{:S(2)}) collective-permute-start(bf16[128,512]{1,0:T(8,128)(2,1)S(1)} %fusion.8), channel_id=1, source_target_pairs={{0,1},{1,0},{2,3},{3,2},{4,5},{5,4},{6,7},{7,6},{8,9},{9,8},{10,11... | collective-permute-start | bytes 393224 | tf_op jit(solution)/shard_map/ppermute | solution.py:292
  170.5 14.5 %collective-permute-start.9 = (f32[8,1024]{1,0:T(8,128)S(1)}, f32[8,1024]{1,0:T(8,128)S(1)}, u32[]{:S(2)}, u32[]{:S(2)}) collective-permute-start(f32[8,1024]{1,0:T(8,128)S(1)} %dynamic-slice_bitcast_fusion), channel_id=1, source_target_pairs={{0,1},{1,0},{2,3},{3,2},{4,5},{5,4},{6,7},{7,6},{8,9},{9,8},{10,11... | collective-permute-start | bytes 98312 | tf_op jit(solution)/shard_map/ppermute | solution.py:292

commit v5 on v4

--- a/solution.py
+++ b/solution.py
@@ -18,6 +18,8 @@
 SCALE = QW ** (-0.5)
 BF16 = jnp.bfloat16
 F32 = jnp.float32
+ZL = ("zm", "zn")
+HOLDERS = ("x", "zn", "core")
 NT = (((1,), (1,)), ((), ()))
 
 
@@ -108,7 +110,7 @@
         col = lax.broadcasted_iota(jnp.int32, (1, RANK), 1)
         inner = row % rows_each
         zl = (row // rows_each) % n_zl
-        x = (row // (rows_each * n_zl) + place_ref[3] // n_core) % n_x
+        x = (row // (rows_each * n_zl) + place_ref[4]) % n_x
         away = row // (rows_each * n_zl * n_x)
         owner = core + away * (1 - 2 * core)
         wanted = ((x * n_zl + zl) * n_core + owner) * rows_each + inner
@@ -233,15 +235,16 @@
     tokens, rank = latent_ref.shape
     out_ref[:, : rank + 2 * ROPE] = latent_columns(latent_ref, rope_ref)
     rows, width = weight_ref.shape
-    for half in range(tokens // rows):
-        columns = weight_ref[:, half * width // 2 : (half + 1) * width // 2]
-        out_ref[half * rows : (half + 1) * rows, rank + 2 * ROPE :] = columns
+    width = width * rows // tokens
+    for k in range(tokens // rows):
+        columns = weight_ref[:, k * width : (k + 1) * width]
+        out_ref[k * rows : (k + 1) * rows, rank + 2 * ROPE :] = columns
 
 
 def pack(place, latent, rope, weight, pieces):
     tokens, rank = latent.shape
     rows, width = weight.shape[0] // pieces, weight.shape[1]
-    shape = (tokens, rank + 2 * ROPE + width // 2)
+    shape = (tokens, rank + 2 * ROPE + width * rows // tokens)
     return pl.pallas_call(
         pack_kernel,
         grid_spec=pltpu.PrefetchScalarGridSpec(
@@ -265,10 +268,12 @@
     width = lat_ref.shape[1]
     lat_ref[...] = other_ref[:, :width]
     count, rows, columns = weight_ref.shape
+    blocks = lat_ref.shape[0] // rows
+    columns = columns // blocks
     for k in range(count):
-        for half in range(2):
-            part = other_ref[half * rows : (half + 1) * rows, width:]
-            weight_ref[k, :, half * columns // 2 : (half + 1) * columns // 2] = part
+        for block in range(blocks):
+            part = other_ref[block * rows : (block + 1) * rows, width:]
+            weight_ref[k, :, block * columns : (block + 1) * columns] = part
 
 
 def unpack(other, count, piece_rows):
@@ -301,13 +306,13 @@
 
 
 def per_device(queries, latent, key_rope, up_weight, out_grad):
-    n_x, n_zl, n_core = lax.axis_size("x"), lax.axis_size("zl"), lax.axis_size("core")
+    n_x, n_zl, n_core = lax.axis_size("x"), lax.axis_size(ZL), lax.axis_size("core")
     n_y, n_zh = lax.axis_size("y"), lax.axis_size("zh")
     zh, y, core = lax.axis_index("zh"), lax.axis_index("y"), lax.axis_index("core")
-    mine = lax.axis_index("x") * n_core + core
-    place = jnp.stack([zh, y, core, mine]).astype(jnp.int32)
+    mine = lax.axis_index(HOLDERS)
+    place = jnp.stack([zh, y, core, mine, lax.axis_index("x")]).astype(jnp.int32)
     tokens = latent.shape[0]
-    pieces = n_x * n_core
+    pieces = lax.axis_size(HOLDERS)
 
     packed = pack(place, latent, key_rope, up_weight, pieces)
     sent = split_heads(queries, out_grad, latent, key_rope, n_y)
@@ -315,7 +320,7 @@
     latents, piece = unpack(rotate(packed, "zh", 1), pieces, RANK // pieces)
     latents = [latents] + [rotate(latents, "y", k + 1) for k in range(n_y - 1)]
     piece, query_grad = lax.optimization_barrier((piece, query_grad))
-    other_weight = exchange(piece, ("x", "core")).reshape(up_weight.shape)
+    other_weight = exchange(piece, HOLDERS).reshape(up_weight.shape)
 
     sizes = (n_core, n_x, n_zl)
     keep, send, latent_part = attention(place, latents, query_grad, up_weight, other_weight, sizes)
@@ -331,8 +336,7 @@
     over_x = sum(a.astype(F32) for a in over_x).astype(BF16)
     rows = over_x.shape[1] // n_zl
     pieces = over_x.reshape(n_zh, n_zl, rows, -1).swapaxes(0, 1)
-    over_zl = add_up(exchange(pieces, "zl"), F32)
-    over_zl, sent = lax.optimization_barrier((over_zl, sent))
+    over_zl = add_up(exchange(pieces, ZL), F32)
     latent_grad = kept + sent.astype(F32)
     own = lax.dynamic_index_in_dim(over_zl, zh, 0, keepdims=False)
     other = lax.dynamic_index_in_dim(over_zl, 1 - zh, 0, keepdims=False)
@@ -342,12 +346,12 @@
 
 def solution(mesh):
     replicas, parts = mesh.shape["dp"], mesh.shape["seq"]
-    shape = (replicas // 16, 8, 2, parts // 2, 2)
-    names = ("x", "zl", "core", "y", "zh")
+    shape = (replicas // 16, 4, 2, 2, parts // 2, 2)
+    names = ("x", *ZL, "core", "y", "zh")
     torus = Mesh(mesh.devices.reshape(shape), names)
     rows = P(names, None)
     in_specs = (rows, rows, rows, P(None, ("y", "zh")), rows)
-    out_specs = (rows, P(("x", "zl", "core"), ("y", "zh")))
+    out_specs = (rows, P(("x", *ZL, "core"), ("y", "zh")))
     return jax.shard_map(
         per_device, mesh=torus, in_specs=in_specs, out_specs=out_specs, check_vma=False
     )

time: 187 us -> 181 us (0.968)
  the two profiles are of different devices: /device:TPU:136 before, /device:TPU:40 now
where the time goes in v5:
time: 181 us; the launch traced here: 180 us
  starting transfers between devices  79.3 us (44%)
  waiting for transfers between devices  58.9 us (33%)
  Pallas kernels  34.5 us (19%)
  other arithmetic  4.82 us (3%)
    ppermute x10, starting transfers between devices, rotate(): return lax.ppermute(array, axis, [(i, (i + shift) % n) for i in range(n)])  55 us
    ppermute x10, waiting for transfers between devices, rotate(): return lax.ppermute(array, axis, [(i, (i + shift) % n) for i in range(n)])  42.1 us
    pallas_call x1, Pallas kernels, attention(): pl.pallas_call(functools.partial(attention_kernel, n_core, n_x, n_zl, n_y...  25.8 us
    all_to_all x4, starting transfers between devices, exchange(): return lax.all_to_all(pieces, axes, split_axis=0, concat_axis=0, tiled=True)  24.2 us
    all_to_all x4, waiting for transfers between devices, exchange(): return lax.all_to_all(pieces, axes, split_axis=0, concat_axis=0, tiled=True)  16.7 us
    pallas_call x1, Pallas kernels, split_heads(): pl.pallas_call(split_kernel, grid=(n_y,), in_specs=[pl.BlockSpec((tokens,...  4.26 us
  transfers between devices with their start and end apart: 14, of which 8 were waited for; matrix products, arithmetic and copies ran while one was open for 3% of the time, Pallas kernels for 2%

profile of v5, /device:TPU:40, one launch (start us, length us, event | category | flops | bytes accessed | tf_op | source)
XLA Modules:
  0.0 179.6 jit_solution(13601857905648159957)
XLA Ops:
  0.6 4.3 %shard_map.70 = bf16[4,128,3200]{2,1,0:T(8,128)(2,1)} custom-call(bf16[128,6144]{1,0:T(8,128)(2,1)} %queries_ref.1, bf16[128,4096]{1,0:T(8,128)(2,1)} %grads_ref.1, bf16[128,512]{1,0:T(8,128)(2,1)} %latent_ref.3, bf16[64,128]{1,0:T(8,128)(2,1)} %bitcast.45), custom_call_target="tpu_custom_call" | custom-call | bytes 6553600 | tf_op jit(solution)/shard_map/pallas_call | solution.py:217
  4.9 4.9 %all-to-all-start = ((bf16[4,128,3200]{2,1,0:T(8,128)(2,1)}), bf16[4,128,3200]{2,1,0:T(8,128)(2,1)S(1)}, u32[]{:S(2)}, u32[]{:S(2)}) async-start(bf16[4,128,3200]{2,1,0:T(8,128)(2,1)} %shard_map.70), calls=%async_computation | async-start | bytes 6553600 | tf_op jit(solution)/shard_map/all_to_all | solution.py:301
  9.8 0.7 stack.23.place_ref
  10.5 2.4 %shard_map.68 = bf16[128,896]{1,0:T(8,128)(2,1)} custom-call(s32[5]{0:T(128)} %stack.23.place_ref, bf16[128,512]{1,0:T(8,128)(2,1)} %latent_ref.3, bf16[64,128]{1,0:T(8,128)(2,1)} %bitcast.46, bf16[512,1024]{1,0:T(8,128)(2,1)} %refs_7_.1), custom_call_target="tpu_custom_call" | custom-call | bytes 458752 | tf_op jit(solution)/shard_map/pallas_call | solution.py:248
  12.9 14.8 %collective-permute-start = (bf16[128,896]{1,0:T(8,128)(2,1)}, bf16[128,896]{1,0:T(8,128)(2,1)S(1)}, u32[]{:S(2)}, u32[]{:S(2)}) collective-permute-start(bf16[128,896]{1,0:T(8,128)(2,1)} %shard_map.68), channel_id=1, source_target_pairs={{0,1},{1,0},{2,3},{3,2},{4,5},{5,4},{6,7},{7,6},{8,9},{9,8},{10,11... | collective-permute-start | bytes 688136 | tf_op jit(solution)/shard_map/ppermute | solution.py:297
  27.7 20.3 %collective-permute-done.other_ref = bf16[128,896]{1,0:T(8,128)(2,1)S(1)} collective-permute-done((bf16[128,896]{1,0:T(8,128)(2,1)}, bf16[128,896]{1,0:T(8,128)(2,1)S(1)}, u32[]{:S(2)}, u32[]{:S(2)}) %collective-permute-start) | collective-permute-done | bytes 229408 | tf_op jit(solution)/shard_map/ppermute | solution.py:297
  47.9 0.0 copy-start.1
  47.9 0.7 copy-done.1
  48.6 2.1 %shard_map.69 = (bf16[128,640]{1,0:T(8,128)(2,1)}, bf16[16,32,1024]{2,1,0:T(8,128)(2,1)}) custom-call(bf16[128,896]{1,0:T(8,128)(2,1)} %copy-done.1), custom_call_target="tpu_custom_call" | custom-call | bytes 1572864 | tf_op jit(solution)/shard_map/pallas_call | solution.py:283
  50.7 0.0 all-to-all-done
  50.7 0.0 copy-start
  50.7 5.8 %all-to-all-start.1 = ((bf16[16,32,1024]{2,1,0:T(8,128)(2,1)}), bf16[16,32,1024]{2,1,0:T(8,128)(2,1)}, u32[]{:S(2)}, u32[]{:S(2)}) async-start(bf16[16,32,1024]{2,1,0:T(8,128)(2,1)} %get-tuple-element.12), calls=%async_computation.1 | async-start | bytes 2097152 | tf_op jit(solution)/shard_map/all_to_all | solution.py:301
  56.5 3.4 %collective-permute-start.1 = (bf16[128,640]{1,0:T(8,128)(2,1)}, bf16[128,640]{1,0:T(8,128)(2,1)S(1)}, u32[]{:S(2)}, u32[]{:S(2)}) collective-permute-start(bf16[128,640]{1,0:T(8,128)(2,1)} %get-tuple-element.11.refs_1_), channel_id=1, source_target_pairs={{0,2},{2,4},{4,6},{6,0},{1,3},{3,5},{5,7},{7,1},{8,10},{10,12},{12... | collective-permute-start | bytes 491528 | tf_op jit(solution)/shard_map/ppermute | solution.py:297
  59.9 2.8 %collective-permute-start.2 = (bf16[128,640]{1,0:T(8,128)(2,1)}, bf16[128,640]{1,0:T(8,128)(2,1)}, u32[]{:S(2)}, u32[]{:S(2)}) collective-permute-start(bf16[128,640]{1,0:T(8,128)(2,1)} %get-tuple-element.11.refs_1_), channel_id=1, source_target_pairs={{0,4},{2,6},{4,0},{6,2},{1,5},{3,7},{5,1},{7,3},{8,12},{10,14},{12... | collective-permute-start | bytes 491528 | tf_op jit(solution)/shard_map/ppermute | solution.py:297
  62.7 4.3 %collective-permute-start.3 = (bf16[128,640]{1,0:T(8,128)(2,1)}, bf16[128,640]{1,0:T(8,128)(2,1)}, u32[]{:S(2)}, u32[]{:S(2)}) collective-permute-start(bf16[128,640]{1,0:T(8,128)(2,1)} %get-tuple-element.11.refs_1_), channel_id=1, source_target_pairs={{0,6},{2,0},{4,2},{6,4},{1,7},{3,1},{5,3},{7,5},{8,14},{10,8},{12,... | collective-permute-start | bytes 491528 | tf_op jit(solution)/shard_map/ppermute | solution.py:297
  66.9 0.0 collective-permute-done.1.refs_2_
  66.9 0.0 copy-start.2
  66.9 3.7 %collective-permute-done.2.refs_3_ = bf16[128,640]{1,0:T(8,128)(2,1)} collective-permute-done((bf16[128,640]{1,0:T(8,128)(2,1)}, bf16[128,640]{1,0:T(8,128)(2,1)}, u32[]{:S(2)}, u32[]{:S(2)}) %collective-permute-start.2) | collective-permute-done | bytes 163872 | tf_op jit(solution)/shard_map/ppermute | solution.py:297
  70.6 2.4 %collective-permute-done.3.refs_4_ = bf16[128,640]{1,0:T(8,128)(2,1)} collective-permute-done((bf16[128,640]{1,0:T(8,128)(2,1)}, bf16[128,640]{1,0:T(8,128)(2,1)}, u32[]{:S(2)}, u32[]{:S(2)}) %collective-permute-start.3) | collective-permute-done | bytes 163872 | tf_op jit(solution)/shard_map/ppermute | solution.py:297
  73.1 0.0 all-to-all-done.1
  73.1 0.0 copy-done
  73.1 0.0 copy-done.2
  73.1 25.8 %shard_map.71 = (bf16[4,2,64,1024]{3,2,1,0:T(8,128)(2,1)}, bf16[4,2,64,1024]{3,2,1,0:T(8,128)(2,1)}, bf16[1024,512]{1,0:T(8,128)(2,1)}) custom-call(s32[5]{0:T(128)} %stack.23.place_ref, bf16[512,3200]{1,0:T(8,128)(2,1)} %bitcast.39, bf16[128,640]{1,0:T(8,128)(2,1)} %get-tuple-element.11.refs_1_, bf16[128,640]{1,0:T(8,128)(2,1)} %copy-done.2, ...), custom_call_target="tpu_custom_call" | custom-call | flops 12884901888 | bytes 16777216 | tf_op jit(solution)/shard_map/pallas_call | solution.py:169
  98.8 1.9 %collective-permute-start.5 = (bf16[4,2,64,1024]{3,2,1,0:T(8,128)(2,1)}, bf16[4,2,64,1024]{3,2,1,0:T(8,128)(2,1)S(1)}, u32[]{:S(2)}, u32[]{:S(2)}) collective-permute-start(bf16[4,2,64,1024]{3,2,1,0:T(8,128)(2,1)} %get-tuple-element.15), channel_id=1, source_target_pairs={{0,8},{8,0},{1,9},{9,1},{2,10},{10,2},{3,11},{11,3},{4,12},{12,4},... | collective-permute-start | bytes 3145736 | tf_op jit(solution)/shard_map/ppermute | solution.py:297
  100.7 3.9 %all-to-all-start.2 = ((bf16[4,256,512]{2,1,0:T(8,128)(2,1)}), bf16[4,256,512]{2,1,0:T(8,128)(2,1)S(1)}, u32[]{:S(2)}, u32[]{:S(2)}) async-start(bf16[4,256,512]{2,1,0:T(8,128)(2,1)} %bitcast.44), calls=%async_computation.2 | async-start | bytes 2097152 | tf_op jit(solution)/shard_map/all_to_all | solution.py:301
  104.7 0.0 collective-permute-done.5
  104.7 1.4 fusion.4
  106.1 4.6 %collective-permute-start.8 = (bf16[2,64,1024]{2,1,0:T(8,128)(2,1)S(1)}, bf16[2,64,1024]{2,1,0:T(8,128)(2,1)S(1)}, u32[]{:S(2)}, u32[]{:S(2)}) collective-permute-start(bf16[2,64,1024]{2,1,0:T(8,128)(2,1)S(1)} %get-tuple-element.17), channel_id=1, source_target_pairs={{0,384},{128,0},{256,128},{384,256},{1,385},{129,1},{257,129},{385... | collective-permute-start | bytes 786440 | tf_op jit(solution)/shard_map/ppermute | solution.py:297
  110.7 2.8 %collective-permute-start.7 = (bf16[2,64,1024]{2,1,0:T(8,128)(2,1)S(1)}, bf16[2,64,1024]{2,1,0:T(8,128)(2,1)S(1)}, u32[]{:S(2)}, u32[]{:S(2)}) collective-permute-start(bf16[2,64,1024]{2,1,0:T(8,128)(2,1)S(1)} %get-tuple-element.18), channel_id=1, source_target_pairs={{0,256},{128,384},{256,0},{384,128},{1,257},{129,385},{257,1},{385... | collective-permute-start | bytes 786440 | tf_op jit(solution)/shard_map/ppermute | solution.py:297
  113.4 2.8 %collective-permute-start.6 = (bf16[2,64,1024]{2,1,0:T(8,128)(2,1)S(1)}, bf16[2,64,1024]{2,1,0:T(8,128)(2,1)S(1)}, u32[]{:S(2)}, u32[]{:S(2)}) collective-permute-start(bf16[2,64,1024]{2,1,0:T(8,128)(2,1)S(1)} %get-tuple-element.16), channel_id=1, source_target_pairs={{0,128},{128,256},{256,384},{384,0},{1,129},{129,257},{257,385},{3... | collective-permute-start | bytes 786440 | tf_op jit(solution)/shard_map/ppermute | solution.py:297
  116.2 5.9 %collective-permute-done.8 = bf16[2,64,1024]{2,1,0:T(8,128)(2,1)S(1)} collective-permute-done((bf16[2,64,1024]{2,1,0:T(8,128)(2,1)S(1)}, bf16[2,64,1024]{2,1,0:T(8,128)(2,1)S(1)}, u32[]{:S(2)}, u32[]{:S(2)}) %collective-permute-start.8) | collective-permute-done | bytes 262176 | tf_op jit(solution)/shard_map/ppermute | solution.py:297
  122.1 1.2 collective-permute-done.7
  123.3 4.4 %collective-permute-done.6 = bf16[2,64,1024]{2,1,0:T(8,128)(2,1)S(1)} collective-permute-done((bf16[2,64,1024]{2,1,0:T(8,128)(2,1)S(1)}, bf16[2,64,1024]{2,1,0:T(8,128)(2,1)S(1)}, u32[]{:S(2)}, u32[]{:S(2)}) %collective-permute-start.6) | collective-permute-done | bytes 262176 | tf_op jit(solution)/shard_map/ppermute | solution.py:297
  127.7 1.9 %copy_bitcast_fusion = bf16[8,2,8,1024]{3,2,1,0:T(8,128)(2,1)} fusion(bf16[2,64,1024]{2,1,0:T(8,128)(2,1)S(1)} %collective-permute-done.8, bf16[2,64,1024]{2,1,0:T(8,128)(2,1)S(1)} %collective-permute-done.7, bf16[2,64,1024]{2,1,0:T(8,128)(2,1)S(1)} %collective-permute-done.6, bf16[4,2,64,1024]{3,2,1,0:T(8,128)(2,1)S(1)} %collective-permute-done.5, ...), kind=kLoop, calls=%fused_computation.16 | loop fusion | flops 1572864 | bytes 1572864 | tf_op jit(solution)/shard_map/transpose | solution.py:338
  129.6 0.0 all-to-all-done.2
  129.6 9.7 %all-to-all-start.3 = ((bf16[8,2,8,1024]{3,2,1,0:T(8,128)(2,1)}), bf16[8,2,8,1024]{3,2,1,0:T(8,128)(2,1)S(1)}, u32[]{:S(2)}, u32[]{:S(2)}) async-start(bf16[8,2,8,1024]{3,2,1,0:T(8,128)(2,1)} %copy_bitcast_fusion), calls=%async_computation.3 | async-start | bytes 524288 | tf_op jit(solution)/shard_map/all_to_all | solution.py:301
  139.3 0.1 convert_reduce_fusion
  139.4 8.2 %collective-permute-start.4 = (bf16[128,512]{1,0:T(8,128)(2,1)S(1)}, bf16[128,512]{1,0:T(8,128)(2,1)S(1)}, u32[]{:S(2)}, u32[]{:S(2)}) collective-permute-start(bf16[128,512]{1,0:T(8,128)(2,1)S(1)} %fusion.8), channel_id=1, source_target_pairs={{0,1},{1,0},{2,3},{3,2},{4,5},{5,4},{6,7},{7,6},{8,9},{9,8},{10,11... | collective-permute-start | bytes 393224 | tf_op jit(solution)/shard_map/ppermute | solution.py:297
  147.7 16.7 %all-to-all-done.3 = bf16[8,2,8,1024]{3,2,1,0:T(8,128)(2,1)S(1)} async-done(((bf16[8,2,8,1024]{3,2,1,0:T(8,128)(2,1)}), bf16[8,2,8,1024]{3,2,1,0:T(8,128)(2,1)S(1)}, u32[]{:S(2)}, u32[]{:S(2)}) %all-to-all-start.3) | async-done | bytes 262176 | tf_op jit(solution)/shard_map/all_to_all | solution.py:301
  164.5 9.5 %collective-permute-start.9 = (f32[8,1024]{1,0:T(8,128)S(1)}, f32[8,1024]{1,0:T(8,128)S(1)}, u32[]{:S(2)}, u32[]{:S(2)}) collective-permute-start(f32[8,1024]{1,0:T(8,128)S(1)} %dynamic-slice_bitcast_fusion), channel_id=1, source_target_pairs={{0,1},{1,0},{2,3},{3,2},{4,5},{5,4},{6,7},{7,6},{8,9},{9,8},{10,11... | collective-permute-start | bytes 98312 | tf_op jit(solution)/shard_map/ppermute | solution.py:297
  174.0 0.0 collective-permute-done.4
  174.0 0.7 bitcast_add_fusion
  174.8 4.2 %collective-permute-done.9 = f32[8,1024]{1,0:T(8,128)S(1)} collective-permute-done((f32[8,1024]{1,0:T(8,128)S(1)}, f32[8,1024]{1,0:T(8,128)S(1)}, u32[]{:S(2)}, u32[]{:S(2)}) %collective-permute-start.9) | collective-permute-done | bytes 32800 | tf_op jit(solution)/shard_map/ppermute | solution.py:297
  179.0 0.6 fusion.9
  (3 shorter events, 0.1 us)
Async XLA Ops:
  4.9 45.8 %all-to-all-start = ((bf16[4,128,3200]{2,1,0:T(8,128)(2,1)}), bf16[4,128,3200]{2,1,0:T(8,128)(2,1)S(1)}, u32[]{:S(2)}, u32[]{:S(2)}) async-start(bf16[4,128,3200]{2,1,0:T(8,128)(2,1)} %shard_map.70), calls=%async_computation | async-start | bytes 6553600 | tf_op jit(solution)/shard_map/all_to_all | solution.py:301
  12.9 35.1 %collective-permute-start = (bf16[128,896]{1,0:T(8,128)(2,1)}, bf16[128,896]{1,0:T(8,128)(2,1)S(1)}, u32[]{:S(2)}, u32[]{:S(2)}) collective-permute-start(bf16[128,896]{1,0:T(8,128)(2,1)} %shard_map.68), channel_id=1, source_target_pairs={{0,1},{1,0},{2,3},{3,2},{4,5},{5,4},{6,7},{7,6},{8,9},{9,8},{10,11... | collective-permute-start | bytes 688136 | tf_op jit(solution)/shard_map/ppermute | solution.py:297
  47.9 0.7 copy-start.1
  50.7 22.4 %copy-start = (bf16[4,128,3200]{2,1,0:T(8,128)(2,1)}, bf16[4,128,3200]{2,1,0:T(8,128)(2,1)S(1)}, u32[]{:S(2)}) copy-start(bf16[4,128,3200]{2,1,0:T(8,128)(2,1)S(1)} %all-to-all-done) | copy-start | bytes 9830404
  50.7 22.3 %all-to-all-start.1 = ((bf16[16,32,1024]{2,1,0:T(8,128)(2,1)}), bf16[16,32,1024]{2,1,0:T(8,128)(2,1)}, u32[]{:S(2)}, u32[]{:S(2)}) async-start(bf16[16,32,1024]{2,1,0:T(8,128)(2,1)} %get-tuple-element.12), calls=%async_computation.1 | async-start | bytes 2097152 | tf_op jit(solution)/shard_map/all_to_all | solution.py:301
  56.5 10.4 %collective-permute-start.1 = (bf16[128,640]{1,0:T(8,128)(2,1)}, bf16[128,640]{1,0:T(8,128)(2,1)S(1)}, u32[]{:S(2)}, u32[]{:S(2)}) collective-permute-start(bf16[128,640]{1,0:T(8,128)(2,1)} %get-tuple-element.11.refs_1_), channel_id=1, source_target_pairs={{0,2},{2,4},{4,6},{6,0},{1,3},{3,5},{5,7},{7,1},{8,10},{10,12},{12... | collective-permute-start | bytes 491528 | tf_op jit(solution)/shard_map/ppermute | solution.py:297
  59.9 10.8 %collective-permute-start.2 = (bf16[128,640]{1,0:T(8,128)(2,1)}, bf16[128,640]{1,0:T(8,128)(2,1)}, u32[]{:S(2)}, u32[]{:S(2)}) collective-permute-start(bf16[128,640]{1,0:T(8,128)(2,1)} %get-tuple-element.11.refs_1_), channel_id=1, source_target_pairs={{0,4},{2,6},{4,0},{6,2},{1,5},{3,7},{5,1},{7,3},{8,12},{10,14},{12... | collective-permute-start | bytes 491528 | tf_op jit(solution)/shard_map/ppermute | solution.py:297
  62.7 10.4 %collective-permute-start.3 = (bf16[128,640]{1,0:T(8,128)(2,1)}, bf16[128,640]{1,0:T(8,128)(2,1)}, u32[]{:S(2)}, u32[]{:S(2)}) collective-permute-start(bf16[128,640]{1,0:T(8,128)(2,1)} %get-tuple-element.11.refs_1_), channel_id=1, source_target_pairs={{0,6},{2,0},{4,2},{6,4},{1,7},{3,1},{5,3},{7,5},{8,14},{10,8},{12,... | collective-permute-start | bytes 491528 | tf_op jit(solution)/shard_map/ppermute | solution.py:297
  66.9 6.1 %copy-start.2 = (bf16[128,640]{1,0:T(8,128)(2,1)}, bf16[128,640]{1,0:T(8,128)(2,1)S(1)}, u32[]{:S(2)}) copy-start(bf16[128,640]{1,0:T(8,128)(2,1)S(1)} %collective-permute-done.1.refs_2_) | copy-start | bytes 491524
  98.8 5.8 %collective-permute-start.5 = (bf16[4,2,64,1024]{3,2,1,0:T(8,128)(2,1)}, bf16[4,2,64,1024]{3,2,1,0:T(8,128)(2,1)S(1)}, u32[]{:S(2)}, u32[]{:S(2)}) collective-permute-start(bf16[4,2,64,1024]{3,2,1,0:T(8,128)(2,1)} %get-tuple-element.15), channel_id=1, source_target_pairs={{0,8},{8,0},{1,9},{9,1},{2,10},{10,2},{3,11},{11,3},{4,12},{12,4},... | collective-permute-start | bytes 3145736 | tf_op jit(solution)/shard_map/ppermute | solution.py:297
  100.7 28.9 %all-to-all-start.2 = ((bf16[4,256,512]{2,1,0:T(8,128)(2,1)}), bf16[4,256,512]{2,1,0:T(8,128)(2,1)S(1)}, u32[]{:S(2)}, u32[]{:S(2)}) async-start(bf16[4,256,512]{2,1,0:T(8,128)(2,1)} %bitcast.44), calls=%async_computation.2 | async-start | bytes 2097152 | tf_op jit(solution)/shard_map/all_to_all | solution.py:301
  106.1 16.1 %collective-permute-start.8 = (bf16[2,64,1024]{2,1,0:T(8,128)(2,1)S(1)}, bf16[2,64,1024]{2,1,0:T(8,128)(2,1)S(1)}, u32[]{:S(2)}, u32[]{:S(2)}) collective-permute-start(bf16[2,64,1024]{2,1,0:T(8,128)(2,1)S(1)} %get-tuple-element.17), channel_id=1, source_target_pairs={{0,384},{128,0},{256,128},{384,256},{1,385},{129,1},{257,129},{385... | collective-permute-start | bytes 786440 | tf_op jit(solution)/shard_map/ppermute | solution.py:297
  110.7 12.6 %collective-permute-start.7 = (bf16[2,64,1024]{2,1,0:T(8,128)(2,1)S(1)}, bf16[2,64,1024]{2,1,0:T(8,128)(2,1)S(1)}, u32[]{:S(2)}, u32[]{:S(2)}) collective-permute-start(bf16[2,64,1024]{2,1,0:T(8,128)(2,1)S(1)} %get-tuple-element.18), channel_id=1, source_target_pairs={{0,256},{128,384},{256,0},{384,128},{1,257},{129,385},{257,1},{385... | collective-permute-start | bytes 786440 | tf_op jit(solution)/shard_map/ppermute | solution.py:297
  113.4 14.3 %collective-permute-start.6 = (bf16[2,64,1024]{2,1,0:T(8,128)(2,1)S(1)}, bf16[2,64,1024]{2,1,0:T(8,128)(2,1)S(1)}, u32[]{:S(2)}, u32[]{:S(2)}) collective-permute-start(bf16[2,64,1024]{2,1,0:T(8,128)(2,1)S(1)} %get-tuple-element.16), channel_id=1, source_target_pairs={{0,128},{128,256},{256,384},{384,0},{1,129},{129,257},{257,385},{3... | collective-permute-start | bytes 786440 | tf_op jit(solution)/shard_map/ppermute | solution.py:297
  129.6 34.8 %all-to-all-start.3 = ((bf16[8,2,8,1024]{3,2,1,0:T(8,128)(2,1)}), bf16[8,2,8,1024]{3,2,1,0:T(8,128)(2,1)S(1)}, u32[]{:S(2)}, u32[]{:S(2)}) async-start(bf16[8,2,8,1024]{3,2,1,0:T(8,128)(2,1)} %copy_bitcast_fusion), calls=%async_computation.3 | async-start | bytes 524288 | tf_op jit(solution)/shard_map/all_to_all | solution.py:301
  139.4 34.6 %collective-permute-start.4 = (bf16[128,512]{1,0:T(8,128)(2,1)S(1)}, bf16[128,512]{1,0:T(8,128)(2,1)S(1)}, u32[]{:S(2)}, u32[]{:S(2)}) collective-permute-start(bf16[128,512]{1,0:T(8,128)(2,1)S(1)} %fusion.8), channel_id=1, source_target_pairs={{0,1},{1,0},{2,3},{3,2},{4,5},{5,4},{6,7},{7,6},{8,9},{9,8},{10,11... | collective-permute-start | bytes 393224 | tf_op jit(solution)/shard_map/ppermute | solution.py:297
  164.5 14.5 %collective-permute-start.9 = (f32[8,1024]{1,0:T(8,128)S(1)}, f32[8,1024]{1,0:T(8,128)S(1)}, u32[]{:S(2)}, u32[]{:S(2)}) collective-permute-start(f32[8,1024]{1,0:T(8,128)S(1)} %dynamic-slice_bitcast_fusion), channel_id=1, source_target_pairs={{0,1},{1,0},{2,3},{3,2},{4,5},{5,4},{6,7},{7,6},{8,9},{9,8},{10,11... | collective-permute-start | bytes 98312 | tf_op jit(solution)/shard_map/ppermute | solution.py:297

commit v6 on v5

--- a/solution.py
+++ b/solution.py
@@ -29,43 +29,48 @@
     grad_cols = [[[None, None], [None, None]] for _ in range(2)]
 
     def products(h, part):
-        n_keys = half * (part + 1)
         rows = slice(part * rows_each, (part + 1) * rows_each)
-        keys = jnp.concatenate([kv[:n_keys, h * KVW : h * KVW + NOPE], rope[:n_keys]], axis=1)
-        values = kv[:n_keys, h * KVW + NOPE : (h + 1) * KVW]
         query = q2[rows, h * QW : (h + 1) * QW]
         grad = g2[rows, h * VDIM : (h + 1) * VDIM]
-        scores = lax.dot_general(keys, query, NT, preferred_element_type=F32)
-        prob_grad = lax.dot_general(values, grad, NT, preferred_element_type=F32)
-        return scores, prob_grad, query[:, :NOPE], grad
-
-    def softmax(part, scores, prob_grad):
-        if part == 0:
-            scores = scores + bias
-        else:
-            scores = jnp.concatenate([scores[:half], scores[half:] + bias], axis=0)
-        row_max = jnp.max(scores, axis=0, keepdims=True)
-        expo = jnp.exp2((scores - row_max) * (SCALE * math.log2(math.e)))
-        probs = expo * (1.0 / jnp.sum(expo, axis=0, keepdims=True))
-        row_dot = jnp.sum(probs * prob_grad, axis=0, keepdims=True)
-        return probs.astype(BF16), (probs * (prob_grad - row_dot)).astype(BF16)
-
-    def accumulate(h, part, probs, score_grad, query_nope, grad):
+        pairs = []
         for block in range(part + 1):
             cut = slice(block * half, (block + 1) * half)
+            keys = jnp.concatenate([kv[cut, h * KVW : h * KVW + NOPE], rope[cut]], axis=1)
+            values = kv[cut, h * KVW + NOPE : (h + 1) * KVW]
+            scores = lax.dot_general(keys, query, NT, preferred_element_type=F32)
+            if block == part:
+                scores = scores + bias
+            prob_grad = lax.dot_general(values, grad, NT, preferred_element_type=F32)
+            pairs.append((scores, prob_grad))
+        return pairs, query[:, :NOPE], grad
+
+    def over_keys(reduce, combine, blocks):
+        return functools.reduce(combine, [reduce(b, axis=0, keepdims=True) for b in blocks])
+
+    def softmax(pairs):
+        row_max = over_keys(jnp.max, jnp.maximum, [scores for scores, _ in pairs])
+        expo = [
+            jnp.exp2((scores - row_max) * (SCALE * math.log2(math.e))) for scores, _ in pairs
+        ]
+        inverse = 1.0 / over_keys(jnp.sum, jnp.add, expo)
+        probs = [e * inverse for e in expo]
+        row_dot = over_keys(jnp.sum, jnp.add, [p * g for p, (_, g) in zip(probs, pairs)])
+        return [(p.astype(BF16), (p * (g - row_dot)).astype(BF16)) for p, (_, g) in zip(probs, pairs)]
+
+    def accumulate(h, blocks, query_nope, grad):
+        for block, (probs, score_grad) in enumerate(blocks):
             for which, (left, right) in enumerate(((score_grad, query_nope), (probs, grad))):
-                product = jnp.dot(left[cut], right, preferred_element_type=F32)
+                product = jnp.dot(left, right, preferred_element_type=F32)
                 before = grad_cols[h][block][which]
                 grad_cols[h][block][which] = product if before is None else before + product
 
     units = [(h, part) for h in range(2) for part in (1, 0)]
     ready = products(*units[0])
     for n, (h, part) in enumerate(units):
-        scores, prob_grad, query_nope, grad = ready
+        pairs, query_nope, grad = ready
         if n + 1 < len(units):
             ready = products(*units[n + 1])
-        probs, score_grad = softmax(part, scores, prob_grad)
-        accumulate(h, part, probs, score_grad, query_nope, grad)
+        accumulate(h, softmax(pairs), query_nope, grad)
     weight_parts = []
     latent_sum = None
     for h in range(2):

time: 181 us -> 179 us (0.989)
  transfers between devices with their start and end apart: 14 -> 14, of which waited for: 8 -> 8; matrix products, arithmetic and copies ran while one was open for 3% -> 3% of each run, Pallas kernels for 2% -> 3%
where the time goes in v6:
time: 179 us; the launch traced here: 178 us
  starting transfers between devices  79.3 us (44%)
  waiting for transfers between devices  58.9 us (33%)
  Pallas kernels  32.8 us (18%)
  other arithmetic  4.82 us (3%)
    ppermute x10, starting transfers between devices, rotate(): return lax.ppermute(array, axis, [(i, (i + shift) % n) for i in range(n)])  55 us
    ppermute x10, waiting for transfers between devices, rotate(): return lax.ppermute(array, axis, [(i, (i + shift) % n) for i in range(n)])  42.1 us
    all_to_all x4, starting transfers between devices, exchange(): return lax.all_to_all(pieces, axes, split_axis=0, concat_axis=0, tiled=True)  24.2 us
    pallas_call x1, Pallas kernels, attention(): pl.pallas_call(functools.partial(attention_kernel, n_core, n_x, n_zl, n_y...  24.1 us
    all_to_all x4, waiting for transfers between devices, exchange(): return lax.all_to_all(pieces, axes, split_axis=0, concat_axis=0, tiled=True)  16.7 us
    pallas_call x1, Pallas kernels, split_heads(): pl.pallas_call(split_kernel, grid=(n_y,), in_specs=[pl.BlockSpec((tokens,...  4.26 us
  transfers between devices with their start and end apart: 14, of which 8 were waited for; matrix products, arithmetic and copies ran while one was open for 3% of the time, Pallas kernels for 3%

profile of v6, /device:TPU:40, one launch (start us, length us, event | category | flops | bytes accessed | tf_op | source)
XLA Modules:
  0.0 177.9 jit_solution(5499993302720939828)
XLA Ops:
  0.6 4.3 %shard_map.70 = bf16[4,128,3200]{2,1,0:T(8,128)(2,1)} custom-call(bf16[128,6144]{1,0:T(8,128)(2,1)} %queries_ref.1, bf16[128,4096]{1,0:T(8,128)(2,1)} %grads_ref.1, bf16[128,512]{1,0:T(8,128)(2,1)} %latent_ref.3, bf16[64,128]{1,0:T(8,128)(2,1)} %bitcast.45), custom_call_target="tpu_custom_call" | custom-call | bytes 6553600 | tf_op jit(solution)/shard_map/pallas_call | solution.py:222
  4.9 4.9 %all-to-all-start = ((bf16[4,128,3200]{2,1,0:T(8,128)(2,1)}), bf16[4,128,3200]{2,1,0:T(8,128)(2,1)S(1)}, u32[]{:S(2)}, u32[]{:S(2)}) async-start(bf16[4,128,3200]{2,1,0:T(8,128)(2,1)} %shard_map.70), calls=%async_computation | async-start | bytes 6553600 | tf_op jit(solution)/shard_map/all_to_all | solution.py:306
  9.8 0.7 stack.23.place_ref
  10.5 2.4 %shard_map.68 = bf16[128,896]{1,0:T(8,128)(2,1)} custom-call(s32[5]{0:T(128)} %stack.23.place_ref, bf16[128,512]{1,0:T(8,128)(2,1)} %latent_ref.3, bf16[64,128]{1,0:T(8,128)(2,1)} %bitcast.46, bf16[512,1024]{1,0:T(8,128)(2,1)} %refs_7_.1), custom_call_target="tpu_custom_call" | custom-call | bytes 458752 | tf_op jit(solution)/shard_map/pallas_call | solution.py:253
  12.9 14.8 %collective-permute-start = (bf16[128,896]{1,0:T(8,128)(2,1)}, bf16[128,896]{1,0:T(8,128)(2,1)S(1)}, u32[]{:S(2)}, u32[]{:S(2)}) collective-permute-start(bf16[128,896]{1,0:T(8,128)(2,1)} %shard_map.68), channel_id=1, source_target_pairs={{0,1},{1,0},{2,3},{3,2},{4,5},{5,4},{6,7},{7,6},{8,9},{9,8},{10,11... | collective-permute-start | bytes 688136 | tf_op jit(solution)/shard_map/ppermute | solution.py:302
  27.7 20.3 %collective-permute-done.other_ref = bf16[128,896]{1,0:T(8,128)(2,1)S(1)} collective-permute-done((bf16[128,896]{1,0:T(8,128)(2,1)}, bf16[128,896]{1,0:T(8,128)(2,1)S(1)}, u32[]{:S(2)}, u32[]{:S(2)}) %collective-permute-start) | collective-permute-done | bytes 229408 | tf_op jit(solution)/shard_map/ppermute | solution.py:302
  47.9 0.0 copy-start.1
  47.9 0.7 copy-done.1
  48.6 2.1 %shard_map.69 = (bf16[128,640]{1,0:T(8,128)(2,1)}, bf16[16,32,1024]{2,1,0:T(8,128)(2,1)}) custom-call(bf16[128,896]{1,0:T(8,128)(2,1)} %copy-done.1), custom_call_target="tpu_custom_call" | custom-call | bytes 1572864 | tf_op jit(solution)/shard_map/pallas_call | solution.py:288
  50.7 0.0 all-to-all-done
  50.7 0.0 copy-start
  50.7 5.8 %all-to-all-start.1 = ((bf16[16,32,1024]{2,1,0:T(8,128)(2,1)}), bf16[16,32,1024]{2,1,0:T(8,128)(2,1)}, u32[]{:S(2)}, u32[]{:S(2)}) async-start(bf16[16,32,1024]{2,1,0:T(8,128)(2,1)} %get-tuple-element.12), calls=%async_computation.1 | async-start | bytes 2097152 | tf_op jit(solution)/shard_map/all_to_all | solution.py:306
  56.5 3.4 %collective-permute-start.1 = (bf16[128,640]{1,0:T(8,128)(2,1)}, bf16[128,640]{1,0:T(8,128)(2,1)S(1)}, u32[]{:S(2)}, u32[]{:S(2)}) collective-permute-start(bf16[128,640]{1,0:T(8,128)(2,1)} %get-tuple-element.11.refs_1_), channel_id=1, source_target_pairs={{0,2},{2,4},{4,6},{6,0},{1,3},{3,5},{5,7},{7,1},{8,10},{10,12},{12... | collective-permute-start | bytes 491528 | tf_op jit(solution)/shard_map/ppermute | solution.py:302
  59.9 2.8 %collective-permute-start.2 = (bf16[128,640]{1,0:T(8,128)(2,1)}, bf16[128,640]{1,0:T(8,128)(2,1)}, u32[]{:S(2)}, u32[]{:S(2)}) collective-permute-start(bf16[128,640]{1,0:T(8,128)(2,1)} %get-tuple-element.11.refs_1_), channel_id=1, source_target_pairs={{0,4},{2,6},{4,0},{6,2},{1,5},{3,7},{5,1},{7,3},{8,12},{10,14},{12... | collective-permute-start | bytes 491528 | tf_op jit(solution)/shard_map/ppermute | solution.py:302
  62.7 4.3 %collective-permute-start.3 = (bf16[128,640]{1,0:T(8,128)(2,1)}, bf16[128,640]{1,0:T(8,128)(2,1)}, u32[]{:S(2)}, u32[]{:S(2)}) collective-permute-start(bf16[128,640]{1,0:T(8,128)(2,1)} %get-tuple-element.11.refs_1_), channel_id=1, source_target_pairs={{0,6},{2,0},{4,2},{6,4},{1,7},{3,1},{5,3},{7,5},{8,14},{10,8},{12,... | collective-permute-start | bytes 491528 | tf_op jit(solution)/shard_map/ppermute | solution.py:302
  66.9 0.0 collective-permute-done.1.refs_2_
  66.9 0.0 copy-start.2
  66.9 3.7 %collective-permute-done.2.refs_3_ = bf16[128,640]{1,0:T(8,128)(2,1)} collective-permute-done((bf16[128,640]{1,0:T(8,128)(2,1)}, bf16[128,640]{1,0:T(8,128)(2,1)}, u32[]{:S(2)}, u32[]{:S(2)}) %collective-permute-start.2) | collective-permute-done | bytes 163872 | tf_op jit(solution)/shard_map/ppermute | solution.py:302
  70.6 2.4 %collective-permute-done.3.refs_4_ = bf16[128,640]{1,0:T(8,128)(2,1)} collective-permute-done((bf16[128,640]{1,0:T(8,128)(2,1)}, bf16[128,640]{1,0:T(8,128)(2,1)}, u32[]{:S(2)}, u32[]{:S(2)}) %collective-permute-start.3) | collective-permute-done | bytes 163872 | tf_op jit(solution)/shard_map/ppermute | solution.py:302
  73.1 0.0 all-to-all-done.1
  73.1 0.0 copy-done
  73.1 0.0 copy-done.2
  73.1 24.1 %shard_map.71 = (bf16[4,2,64,1024]{3,2,1,0:T(8,128)(2,1)}, bf16[4,2,64,1024]{3,2,1,0:T(8,128)(2,1)}, bf16[1024,512]{1,0:T(8,128)(2,1)}) custom-call(s32[5]{0:T(128)} %stack.23.place_ref, bf16[512,3200]{1,0:T(8,128)(2,1)} %bitcast.39, bf16[128,640]{1,0:T(8,128)(2,1)} %get-tuple-element.11.refs_1_, bf16[128,640]{1,0:T(8,128)(2,1)} %copy-done.2, ...), custom_call_target="tpu_custom_call" | custom-call | flops 12884901888 | bytes 16777216 | tf_op jit(solution)/shard_map/pallas_call | solution.py:174
  97.1 1.9 %collective-permute-start.5 = (bf16[4,2,64,1024]{3,2,1,0:T(8,128)(2,1)}, bf16[4,2,64,1024]{3,2,1,0:T(8,128)(2,1)S(1)}, u32[]{:S(2)}, u32[]{:S(2)}) collective-permute-start(bf16[4,2,64,1024]{3,2,1,0:T(8,128)(2,1)} %get-tuple-element.15), channel_id=1, source_target_pairs={{0,8},{8,0},{1,9},{9,1},{2,10},{10,2},{3,11},{11,3},{4,12},{12,4},... | collective-permute-start | bytes 3145736 | tf_op jit(solution)/shard_map/ppermute | solution.py:302
  99.1 3.9 %all-to-all-start.2 = ((bf16[4,256,512]{2,1,0:T(8,128)(2,1)}), bf16[4,256,512]{2,1,0:T(8,128)(2,1)S(1)}, u32[]{:S(2)}, u32[]{:S(2)}) async-start(bf16[4,256,512]{2,1,0:T(8,128)(2,1)} %bitcast.44), calls=%async_computation.2 | async-start | bytes 2097152 | tf_op jit(solution)/shard_map/all_to_all | solution.py:306
  103.0 0.0 collective-permute-done.5
  103.0 1.4 fusion.4
  104.4 4.6 %collective-permute-start.8 = (bf16[2,64,1024]{2,1,0:T(8,128)(2,1)S(1)}, bf16[2,64,1024]{2,1,0:T(8,128)(2,1)S(1)}, u32[]{:S(2)}, u32[]{:S(2)}) collective-permute-start(bf16[2,64,1024]{2,1,0:T(8,128)(2,1)S(1)} %get-tuple-element.17), channel_id=1, source_target_pairs={{0,384},{128,0},{256,128},{384,256},{1,385},{129,1},{257,129},{385... | collective-permute-start | bytes 786440 | tf_op jit(solution)/shard_map/ppermute | solution.py:302
  109.0 2.8 %collective-permute-start.7 = (bf16[2,64,1024]{2,1,0:T(8,128)(2,1)S(1)}, bf16[2,64,1024]{2,1,0:T(8,128)(2,1)S(1)}, u32[]{:S(2)}, u32[]{:S(2)}) collective-permute-start(bf16[2,64,1024]{2,1,0:T(8,128)(2,1)S(1)} %get-tuple-element.18), channel_id=1, source_target_pairs={{0,256},{128,384},{256,0},{384,128},{1,257},{129,385},{257,1},{385... | collective-permute-start | bytes 786440 | tf_op jit(solution)/shard_map/ppermute | solution.py:302
  111.7 2.8 %collective-permute-start.6 = (bf16[2,64,1024]{2,1,0:T(8,128)(2,1)S(1)}, bf16[2,64,1024]{2,1,0:T(8,128)(2,1)S(1)}, u32[]{:S(2)}, u32[]{:S(2)}) collective-permute-start(bf16[2,64,1024]{2,1,0:T(8,128)(2,1)S(1)} %get-tuple-element.16), channel_id=1, source_target_pairs={{0,128},{128,256},{256,384},{384,0},{1,129},{129,257},{257,385},{3... | collective-permute-start | bytes 786440 | tf_op jit(solution)/shard_map/ppermute | solution.py:302
  114.5 5.9 %collective-permute-done.8 = bf16[2,64,1024]{2,1,0:T(8,128)(2,1)S(1)} collective-permute-done((bf16[2,64,1024]{2,1,0:T(8,128)(2,1)S(1)}, bf16[2,64,1024]{2,1,0:T(8,128)(2,1)S(1)}, u32[]{:S(2)}, u32[]{:S(2)}) %collective-permute-start.8) | collective-permute-done | bytes 262176 | tf_op jit(solution)/shard_map/ppermute | solution.py:302
  120.5 1.2 collective-permute-done.7
  121.6 4.4 %collective-permute-done.6 = bf16[2,64,1024]{2,1,0:T(8,128)(2,1)S(1)} collective-permute-done((bf16[2,64,1024]{2,1,0:T(8,128)(2,1)S(1)}, bf16[2,64,1024]{2,1,0:T(8,128)(2,1)S(1)}, u32[]{:S(2)}, u32[]{:S(2)}) %collective-permute-start.6) | collective-permute-done | bytes 262176 | tf_op jit(solution)/shard_map/ppermute | solution.py:302
  126.0 1.9 %copy_bitcast_fusion = bf16[8,2,8,1024]{3,2,1,0:T(8,128)(2,1)} fusion(bf16[2,64,1024]{2,1,0:T(8,128)(2,1)S(1)} %collective-permute-done.8, bf16[2,64,1024]{2,1,0:T(8,128)(2,1)S(1)} %collective-permute-done.7, bf16[2,64,1024]{2,1,0:T(8,128)(2,1)S(1)} %collective-permute-done.6, bf16[4,2,64,1024]{3,2,1,0:T(8,128)(2,1)S(1)} %collective-permute-done.5, ...), kind=kLoop, calls=%fused_computation.16 | loop fusion | flops 1572864 | bytes 1572864 | tf_op jit(solution)/shard_map/transpose | solution.py:343
  127.9 0.0 all-to-all-done.2
  127.9 9.7 %all-to-all-start.3 = ((bf16[8,2,8,1024]{3,2,1,0:T(8,128)(2,1)}), bf16[8,2,8,1024]{3,2,1,0:T(8,128)(2,1)S(1)}, u32[]{:S(2)}, u32[]{:S(2)}) async-start(bf16[8,2,8,1024]{3,2,1,0:T(8,128)(2,1)} %copy_bitcast_fusion), calls=%async_computation.3 | async-start | bytes 524288 | tf_op jit(solution)/shard_map/all_to_all | solution.py:306
  137.6 0.1 convert_reduce_fusion
  137.8 8.2 %collective-permute-start.4 = (bf16[128,512]{1,0:T(8,128)(2,1)S(1)}, bf16[128,512]{1,0:T(8,128)(2,1)S(1)}, u32[]{:S(2)}, u32[]{:S(2)}) collective-permute-start(bf16[128,512]{1,0:T(8,128)(2,1)S(1)} %fusion.8), channel_id=1, source_target_pairs={{0,1},{1,0},{2,3},{3,2},{4,5},{5,4},{6,7},{7,6},{8,9},{9,8},{10,11... | collective-permute-start | bytes 393224 | tf_op jit(solution)/shard_map/ppermute | solution.py:302
  146.0 16.7 %all-to-all-done.3 = bf16[8,2,8,1024]{3,2,1,0:T(8,128)(2,1)S(1)} async-done(((bf16[8,2,8,1024]{3,2,1,0:T(8,128)(2,1)}), bf16[8,2,8,1024]{3,2,1,0:T(8,128)(2,1)S(1)}, u32[]{:S(2)}, u32[]{:S(2)}) %all-to-all-start.3) | async-done | bytes 262176 | tf_op jit(solution)/shard_map/all_to_all | solution.py:306
  162.8 9.5 %collective-permute-start.9 = (f32[8,1024]{1,0:T(8,128)S(1)}, f32[8,1024]{1,0:T(8,128)S(1)}, u32[]{:S(2)}, u32[]{:S(2)}) collective-permute-start(f32[8,1024]{1,0:T(8,128)S(1)} %dynamic-slice_bitcast_fusion), channel_id=1, source_target_pairs={{0,1},{1,0},{2,3},{3,2},{4,5},{5,4},{6,7},{7,6},{8,9},{9,8},{10,11... | collective-permute-start | bytes 98312 | tf_op jit(solution)/shard_map/ppermute | solution.py:302
  172.3 0.0 collective-permute-done.4
  172.3 0.7 bitcast_add_fusion
  173.1 4.2 %collective-permute-done.9 = f32[8,1024]{1,0:T(8,128)S(1)} collective-permute-done((f32[8,1024]{1,0:T(8,128)S(1)}, f32[8,1024]{1,0:T(8,128)S(1)}, u32[]{:S(2)}, u32[]{:S(2)}) %collective-permute-start.9) | collective-permute-done | bytes 32800 | tf_op jit(solution)/shard_map/ppermute | solution.py:302
  177.3 0.6 fusion.9
  (3 shorter events, 0.1 us)
Async XLA Ops:
  4.9 45.8 %all-to-all-start = ((bf16[4,128,3200]{2,1,0:T(8,128)(2,1)}), bf16[4,128,3200]{2,1,0:T(8,128)(2,1)S(1)}, u32[]{:S(2)}, u32[]{:S(2)}) async-start(bf16[4,128,3200]{2,1,0:T(8,128)(2,1)} %shard_map.70), calls=%async_computation | async-start | bytes 6553600 | tf_op jit(solution)/shard_map/all_to_all | solution.py:306
  12.9 35.1 %collective-permute-start = (bf16[128,896]{1,0:T(8,128)(2,1)}, bf16[128,896]{1,0:T(8,128)(2,1)S(1)}, u32[]{:S(2)}, u32[]{:S(2)}) collective-permute-start(bf16[128,896]{1,0:T(8,128)(2,1)} %shard_map.68), channel_id=1, source_target_pairs={{0,1},{1,0},{2,3},{3,2},{4,5},{5,4},{6,7},{7,6},{8,9},{9,8},{10,11... | collective-permute-start | bytes 688136 | tf_op jit(solution)/shard_map/ppermute | solution.py:302
  47.9 0.7 copy-start.1
  50.7 22.4 %copy-start = (bf16[4,128,3200]{2,1,0:T(8,128)(2,1)}, bf16[4,128,3200]{2,1,0:T(8,128)(2,1)S(1)}, u32[]{:S(2)}) copy-start(bf16[4,128,3200]{2,1,0:T(8,128)(2,1)S(1)} %all-to-all-done) | copy-start | bytes 9830404
  50.7 22.3 %all-to-all-start.1 = ((bf16[16,32,1024]{2,1,0:T(8,128)(2,1)}), bf16[16,32,1024]{2,1,0:T(8,128)(2,1)}, u32[]{:S(2)}, u32[]{:S(2)}) async-start(bf16[16,32,1024]{2,1,0:T(8,128)(2,1)} %get-tuple-element.12), calls=%async_computation.1 | async-start | bytes 2097152 | tf_op jit(solution)/shard_map/all_to_all | solution.py:306
  56.5 10.4 %collective-permute-start.1 = (bf16[128,640]{1,0:T(8,128)(2,1)}, bf16[128,640]{1,0:T(8,128)(2,1)S(1)}, u32[]{:S(2)}, u32[]{:S(2)}) collective-permute-start(bf16[128,640]{1,0:T(8,128)(2,1)} %get-tuple-element.11.refs_1_), channel_id=1, source_target_pairs={{0,2},{2,4},{4,6},{6,0},{1,3},{3,5},{5,7},{7,1},{8,10},{10,12},{12... | collective-permute-start | bytes 491528 | tf_op jit(solution)/shard_map/ppermute | solution.py:302
  59.9 10.8 %collective-permute-start.2 = (bf16[128,640]{1,0:T(8,128)(2,1)}, bf16[128,640]{1,0:T(8,128)(2,1)}, u32[]{:S(2)}, u32[]{:S(2)}) collective-permute-start(bf16[128,640]{1,0:T(8,128)(2,1)} %get-tuple-element.11.refs_1_), channel_id=1, source_target_pairs={{0,4},{2,6},{4,0},{6,2},{1,5},{3,7},{5,1},{7,3},{8,12},{10,14},{12... | collective-permute-start | bytes 491528 | tf_op jit(solution)/shard_map/ppermute | solution.py:302
  62.7 10.4 %collective-permute-start.3 = (bf16[128,640]{1,0:T(8,128)(2,1)}, bf16[128,640]{1,0:T(8,128)(2,1)}, u32[]{:S(2)}, u32[]{:S(2)}) collective-permute-start(bf16[128,640]{1,0:T(8,128)(2,1)} %get-tuple-element.11.refs_1_), channel_id=1, source_target_pairs={{0,6},{2,0},{4,2},{6,4},{1,7},{3,1},{5,3},{7,5},{8,14},{10,8},{12,... | collective-permute-start | bytes 491528 | tf_op jit(solution)/shard_map/ppermute | solution.py:302
  66.9 6.1 %copy-start.2 = (bf16[128,640]{1,0:T(8,128)(2,1)}, bf16[128,640]{1,0:T(8,128)(2,1)S(1)}, u32[]{:S(2)}) copy-start(bf16[128,640]{1,0:T(8,128)(2,1)S(1)} %collective-permute-done.1.refs_2_) | copy-start | bytes 491524
  97.1 5.8 %collective-permute-start.5 = (bf16[4,2,64,1024]{3,2,1,0:T(8,128)(2,1)}, bf16[4,2,64,1024]{3,2,1,0:T(8,128)(2,1)S(1)}, u32[]{:S(2)}, u32[]{:S(2)}) collective-permute-start(bf16[4,2,64,1024]{3,2,1,0:T(8,128)(2,1)} %get-tuple-element.15), channel_id=1, source_target_pairs={{0,8},{8,0},{1,9},{9,1},{2,10},{10,2},{3,11},{11,3},{4,12},{12,4},... | collective-permute-start | bytes 3145736 | tf_op jit(solution)/shard_map/ppermute | solution.py:302
  99.1 28.9 %all-to-all-start.2 = ((bf16[4,256,512]{2,1,0:T(8,128)(2,1)}), bf16[4,256,512]{2,1,0:T(8,128)(2,1)S(1)}, u32[]{:S(2)}, u32[]{:S(2)}) async-start(bf16[4,256,512]{2,1,0:T(8,128)(2,1)} %bitcast.44), calls=%async_computation.2 | async-start | bytes 2097152 | tf_op jit(solution)/shard_map/all_to_all | solution.py:306
  104.4 16.1 %collective-permute-start.8 = (bf16[2,64,1024]{2,1,0:T(8,128)(2,1)S(1)}, bf16[2,64,1024]{2,1,0:T(8,128)(2,1)S(1)}, u32[]{:S(2)}, u32[]{:S(2)}) collective-permute-start(bf16[2,64,1024]{2,1,0:T(8,128)(2,1)S(1)} %get-tuple-element.17), channel_id=1, source_target_pairs={{0,384},{128,0},{256,128},{384,256},{1,385},{129,1},{257,129},{385... | collective-permute-start | bytes 786440 | tf_op jit(solution)/shard_map/ppermute | solution.py:302
  109.0 12.6 %collective-permute-start.7 = (bf16[2,64,1024]{2,1,0:T(8,128)(2,1)S(1)}, bf16[2,64,1024]{2,1,0:T(8,128)(2,1)S(1)}, u32[]{:S(2)}, u32[]{:S(2)}) collective-permute-start(bf16[2,64,1024]{2,1,0:T(8,128)(2,1)S(1)} %get-tuple-element.18), channel_id=1, source_target_pairs={{0,256},{128,384},{256,0},{384,128},{1,257},{129,385},{257,1},{385... | collective-permute-start | bytes 786440 | tf_op jit(solution)/shard_map/ppermute | solution.py:302
  111.7 14.3 %collective-permute-start.6 = (bf16[2,64,1024]{2,1,0:T(8,128)(2,1)S(1)}, bf16[2,64,1024]{2,1,0:T(8,128)(2,1)S(1)}, u32[]{:S(2)}, u32[]{:S(2)}) collective-permute-start(bf16[2,64,1024]{2,1,0:T(8,128)(2,1)S(1)} %get-tuple-element.16), channel_id=1, source_target_pairs={{0,128},{128,256},{256,384},{384,0},{1,129},{129,257},{257,385},{3... | collective-permute-start | bytes 786440 | tf_op jit(solution)/shard_map/ppermute | solution.py:302
  127.9 34.8 %all-to-all-start.3 = ((bf16[8,2,8,1024]{3,2,1,0:T(8,128)(2,1)}), bf16[8,2,8,1024]{3,2,1,0:T(8,128)(2,1)S(1)}, u32[]{:S(2)}, u32[]{:S(2)}) async-start(bf16[8,2,8,1024]{3,2,1,0:T(8,128)(2,1)} %copy_bitcast_fusion), calls=%async_computation.3 | async-start | bytes 524288 | tf_op jit(solution)/shard_map/all_to_all | solution.py:306
  137.8 34.6 %collective-permute-start.4 = (bf16[128,512]{1,0:T(8,128)(2,1)S(1)}, bf16[128,512]{1,0:T(8,128)(2,1)S(1)}, u32[]{:S(2)}, u32[]{:S(2)}) collective-permute-start(bf16[128,512]{1,0:T(8,128)(2,1)S(1)} %fusion.8), channel_id=1, source_target_pairs={{0,1},{1,0},{2,3},{3,2},{4,5},{5,4},{6,7},{7,6},{8,9},{9,8},{10,11... | collective-permute-start | bytes 393224 | tf_op jit(solution)/shard_map/ppermute | solution.py:302
  162.8 14.5 %collective-permute-start.9 = (f32[8,1024]{1,0:T(8,128)S(1)}, f32[8,1024]{1,0:T(8,128)S(1)}, u32[]{:S(2)}, u32[]{:S(2)}) collective-permute-start(f32[8,1024]{1,0:T(8,128)S(1)} %dynamic-slice_bitcast_fusion), channel_id=1, source_target_pairs={{0,1},{1,0},{2,3},{3,2},{4,5},{5,4},{6,7},{7,6},{8,9},{9,8},{10,11... | collective-permute-start | bytes 98312 | tf_op jit(solution)/shard_map/ppermute | solution.py:302
